TPU v7x, 32 devices: a whole 2x2x4 slice. The times are simulated.
32 devices in a mesh: tm: 4 (over z), lon: 8 (over y, x, core).
Axes of the slice: x: 2, y: 2, z: 4, core: 2. Of those that a mesh axis runs over, the one named last changes fastest.
Arguments:
- rhs_state: float32 [4, 3, 1024, 2048], P('tm', None, None, 'lon'), may hold values from -30 to 30
- innovations: float32 [4, 8192], P('tm', 'lon'), may hold values from -6 to 6
- trajectory: bfloat16 [4, 2, 3, 1024, 2048], P('tm', None, None, None, 'lon'), may hold values from -1 to 1.5, as said below
- model_var: float32 [4, 3, 1024, 2048], P('tm', None, None, 'lon'), may hold values from 0.2 to 2
- obs_var: float32 [4, 8192], P('tm', 'lon'), may hold values from 0.2 to 2
- obs_index: int32 [4, 8192], P('tm', 'lon'), may hold values from 0 to 786431, as said below
- control_rhs: float32 [4, 3, 1024, 2048], P('tm', None, None, 'lon'), may hold values from -30 to 30
Outputs:
- multiplier_out: float32 [4, 3, 1024, 2048], P('tm', None, None, 'lon')
- obs_dual_out: float32 [4, 8192], P('tm', 'lon')
- increment_out: float32 [4, 3, 1024, 2048], P('tm', None, None, 'lon')
Inputs may be any that keep to these rules, and one draw needn't show every extreme that they name: obs_index[k, j] = (field 1024 + row) * 256 + column with field 0 to 2, row 0 to 1023 and column 0 to 255 within the band j // 1024; an index may repeat. Field 0 of trajectory is the depth, fields 1 and 2 the winds.
All inputs are finite; a program needn't handle non-finite values.
Results may differ from a plain program's by a relative error of at most 0.0003.
Values sent between devices are 32-bit elements; how exact they have to be, the bound alone decides.
No kernel may reach another device: no remote copies, remote signals or barrier semaphores. Data moves between devices by JAX's collectives and lax.ppermute only.
A program may use at most 192 MiB of HBM per device.

v0:
```python
import functools

import jax
import jax.numpy as jnp
from jax import lax
from jax.experimental import pallas as pl
from jax.experimental.pallas import tpu as pltpu
from jax.sharding import PartitionSpec as P

courant = 0.25
coriolis = 0.2
slope = 0.5 * courant

LANE = 128
GROUP = 16
MARGIN = 8
HALO = 4
TRAJ, INC, VAR, LAST, PLANES = 0, 6, 9, 12, 16
F32 = jnp.float32
PARAMS = pltpu.CompilerParams(vmem_limit_bytes=56 * 1024 * 1024)


def iota(shape, dim):
    return lax.broadcasted_iota(jnp.int32, shape, dim)


def spread_shift(plane):
    return (LANE - (8 * plane + HALO)) % LANE


def pack_shift(plane):
    return (8 * plane + HALO) % LANE


def edges_of(planes, rows):
    lane = iota((rows, LANE), 1)
    packed = jnp.zeros((rows, LANE), F32)
    for number, plane in enumerate(planes):
        both = jnp.where(lane < LANE // 2, plane[:, :LANE], plane[:, LANE:])
        packed = jnp.where(lane // 8 == number, pltpu.roll(both, pack_shift(number), 1), packed)
    return packed


def split_edges(turned, to_right, to_left, count):
    top = iota((8, turned.shape[1]), 0) < HALO
    for pair in range(count // 2):
        even = turned[16 * pair : 16 * pair + 8]
        odd = turned[16 * pair + 8 : 16 * pair + 16]
        to_right[8 * pair : 8 * pair + 8, :] = jnp.where(top, even, pltpu.roll(odd, HALO, 0))
        to_left[8 * pair : 8 * pair + 8, :] = jnp.where(top, pltpu.roll(even, HALO, 0), odd)


def joined_edges(from_left, from_right, count):
    top = iota((8, from_left.shape[1]), 0) < HALO
    pieces = []
    for pair in range(count // 2):
        left = from_left[8 * pair : 8 * pair + 8]
        right = from_right[8 * pair : 8 * pair + 8]
        pieces.append(jnp.where(top, left, pltpu.roll(right, HALO, 0)))
        pieces.append(jnp.where(top, pltpu.roll(left, HALO, 0), right))
    return jnp.concatenate(pieces, axis=0)


def padded_turn(message):
    rest = LANE - message.shape[0]
    if rest:
        message = jnp.concatenate([message, jnp.zeros((rest, message.shape[1]), F32)], axis=0)
    return message.T


def edges_kernel(first, last, variance, traj, to_right, to_left, increment):
    rows = first.shape[1]
    planes = [traj[p].astype(F32) for p in range(6)]
    for f in range(3):
        value = first[f] - variance[f] * last[f]
        increment[f] = value
        planes.append(value)
    planes += [variance[f] for f in range(3)]
    planes += [last[f] for f in range(3)]
    split_edges(edges_of(planes, rows).T, to_right, to_left, PLANES)


def edges_call(first, last, variance, traj):
    rows = first.shape[1]
    block = pl.BlockSpec((3, LANE, 2 * LANE), lambda i: (0, i, 0))
    sent = pl.BlockSpec((PLANES * HALO, LANE), lambda i: (0, i))
    return pl.pallas_call(
        edges_kernel,
        grid=(rows // LANE,),
        in_specs=[block, block, block, pl.BlockSpec((6, LANE, 2 * LANE), lambda i: (0, i, 0))],
        out_specs=[sent, sent, block],
        out_shape=[jax.ShapeDtypeStruct((PLANES * HALO, rows), F32)] * 2
        + [jax.ShapeDtypeStruct(first.shape, F32)],
        compiler_params=PARAMS,
        cost_estimate=pl.CostEstimate(flops=10**6, bytes_accessed=16 * 2**20, transcendentals=0),
        name="edges",
    )(first, last, variance, traj)


def spread_edges_kernel(spread, to_right, to_left):
    planes = [spread[f] for f in range(3)]
    split_edges(edges_of(planes, spread.shape[1]).T, to_right, to_left, 4)


def spread_edges_call(spread):
    rows = spread.shape[1]
    sent = pl.BlockSpec((16, LANE), lambda i: (0, i))
    return pl.pallas_call(
        spread_edges_kernel,
        grid=(rows // LANE,),
        in_specs=[pl.BlockSpec((3, LANE, 2 * LANE), lambda i: (0, i, 0))],
        out_specs=[sent, sent],
        out_shape=[jax.ShapeDtypeStruct((16, rows), F32)] * 2,
        compiler_params=PARAMS,
        cost_estimate=pl.CostEstimate(flops=10**6, bytes_accessed=3 * 2**20, transcendentals=0),
        name="spread_edges",
    )(spread)


def x_differences(tiles, first_lane, last_lane):
    ahead = [pltpu.roll(t, LANE - 1, 1) for t in tiles]
    behind = [pltpu.roll(t, 1, 1) for t in tiles]
    return [
        jnp.where(last_lane, ahead[(t + 1) % 3], ahead[t])
        - jnp.where(first_lane, behind[(t - 1) % 3], behind[t])
        for t in range(3)
    ]


def rotation_at(start, total):
    position = (iota((GROUP, LANE), 0) + start).astype(F32)
    return coriolis * ((2.0 * position + 1.0) / total - 1.0)


def lane_ends():
    lane = iota((GROUP, LANE), 1)
    return lane == 0, lane == LANE - 1


def traj_tiles(traj, packed_ref, step, start):
    packed = packed_ref[pl.ds(start, GROUP), :]
    out = []
    for field in range(3):
        plane = 3 * step + field
        out.append(
            [traj[plane, pl.ds(start, GROUP), t * LANE : (t + 1) * LANE].astype(F32) for t in range(2)]
            + [pltpu.roll(packed, spread_shift(TRAJ + plane), 1)]
        )
    return out


def load_rows(ref, start, offset):
    return [[ref[f, t, pl.ds(start + (MARGIN + offset), GROUP), :] for t in range(3)] for f in range(3)]


def store_rows(ref, start, value):
    for f in range(3):
        for t in range(3):
            ref[f, t, pl.ds(start + MARGIN, GROUP), :] = value[f][t]


def clear_margins(ref):
    rows = ref.shape[2]
    zero = jnp.zeros((MARGIN, LANE), F32)
    for f in range(3):
        for t in range(3):
            ref[f, t, 0:MARGIN, :] = zero
            ref[f, t, rows - MARGIN : rows, :] = zero


def tangent_rows(source, traj, packed_ref, step, start, total):
    here, above, below = (load_rows(source, start, k) for k in (0, 1, -1))
    trajectory = traj_tiles(traj, packed_ref, step, start)
    turn = rotation_at(start, total)
    ends = lane_ends()
    dx = [x_differences(here[f], *ends) for f in range(3)]
    new = [[], [], []]
    for t in range(3):
        b, e, n = (trajectory[f][t] for f in range(3))
        h, u, v = (here[f][t] for f in range(3))
        xh, xu, xv = (dx[f][t] for f in range(3))
        yh, yu, yv = (above[f][t] - below[f][t] for f in range(3))
        new[0].append(h - slope * (b * (xu + yv) + e * xh + n * yh))
        new[1].append(u - slope * (xh + e * xu + n * yu) + turn * v)
        new[2].append(v - slope * (yh + e * xv + n * yv) - turn * u)
    return new


def north_rows(field, trajectory):
    out = [[], [], []]
    for t in range(3):
        b, _, n = (trajectory[f][t] for f in range(3))
        p, q, w = (field[f][t] for f in range(3))
        out[0].append(n * p + w)
        out[1].append(n * q)
        out[2].append(b * p + n * w)
    return out


def adjoint_rows(source, flux, traj, packed_ref, step, start, total):
    here = load_rows(source, start, 0)
    above, below = (load_rows(flux, start, k) for k in (1, -1))
    trajectory = traj_tiles(traj, packed_ref, step, start)
    turn = rotation_at(start, total)
    ends = lane_ends()
    east = [[], [], []]
    for t in range(3):
        b, e, _ = (trajectory[f][t] for f in range(3))
        p, q, w = (here[f][t] for f in range(3))
        east[0].append(e * p + q)
        east[1].append(b * p + e * q)
        east[2].append(e * w)
    dx = [x_differences(east[f], *ends) for f in range(3)]
    new = [[], [], []]
    for t in range(3):
        p, q, w = (here[f][t] for f in range(3))
        change = [slope * (dx[f][t] + (above[f][t] - below[f][t])) for f in range(3)]
        new[0].append(p + change[0])
        new[1].append(q + change[1] - turn * w)
        new[2].append(w + change[2] + turn * q)
    return new


def over_rows(total, body):
    def step(i, carry):
        body(pl.multiple_of(i * GROUP, GROUP))
        return carry

    lax.fori_loop(0, total // GROUP, step, 0)


def turn_in(message, packed_ref):
    for j in range(message.shape[1] // LANE):
        packed_ref[j * LANE : (j + 1) * LANE, :] = padded_turn(message[:, j * LANE : (j + 1) * LANE])


def turn_out(packed_ref, message):
    for j in range(message.shape[1] // LANE):
        turned = packed_ref[j * LANE : (j + 1) * LANE, :].T
        message[:, j * LANE : (j + 1) * LANE] = turned[: message.shape[0]]


def pack_three(halo_tiles):
    lane = iota((GROUP, LANE), 1) // 8
    packed = jnp.zeros((GROUP, LANE), F32)
    for f in range(3):
        packed = jnp.where(lane == f, pltpu.roll(halo_tiles[f], pack_shift(f), 1), packed)
    return packed


def wide_scratch(rows):
    return pltpu.VMEM((3, 3, rows + 2 * MARGIN, LANE), F32)


def tile_of(ref, f, start, t):
    return ref[f, pl.ds(start, GROUP), t * LANE : (t + 1) * LANE]


def set_tile(ref, f, start, t, value):
    ref[f, pl.ds(start, GROUP), t * LANE : (t + 1) * LANE] = value


def run_tangent(get, traj, packed_ref, wide_a, wide_b, total, put):
    clear_margins(wide_a)
    clear_margins(wide_b)
    over_rows(total, lambda s: store_rows(wide_a, s, get(s)))
    over_rows(
        total, lambda s: store_rows(wide_b, s, tangent_rows(wide_a, traj, packed_ref, 0, s, total))
    )
    over_rows(total, lambda s: put(s, tangent_rows(wide_b, traj, packed_ref, 1, s, total)))


def run_adjoint(get, traj, packed_ref, wide_a, wide_b, flux_a, flux_b, total, put):
    clear_margins(flux_a)
    clear_margins(flux_b)

    def begin(s):
        field = get(s)
        store_rows(wide_a, s, field)
        store_rows(flux_a, s, north_rows(field, traj_tiles(traj, packed_ref, 1, s)))

    def middle(s):
        field = adjoint_rows(wide_a, flux_a, traj, packed_ref, 1, s, total)
        store_rows(wide_b, s, field)
        store_rows(flux_b, s, north_rows(field, traj_tiles(traj, packed_ref, 0, s)))

    over_rows(total, begin)
    over_rows(total, middle)
    over_rows(total, lambda s: put(s, adjoint_rows(wide_b, flux_b, traj, packed_ref, 0, s, total)))


def tangent_first_kernel(
    increment, traj, from_left, from_right, ahead, ahead_edges, packed, last_edges, wide_a, wide_b, own
):
    total = increment.shape[1]
    for j in range(total // LANE):
        cut = slice(j * LANE, (j + 1) * LANE)
        joined = joined_edges(from_left[:, cut], from_right[:, cut], PLANES)
        last_edges[:, cut] = joined[8 * LAST : 8 * LAST + 24]
        packed[cut, :] = joined.T

    def get(s):
        lanes = packed[pl.ds(s, GROUP), :]
        return [
            [tile_of(increment, f, s, 0), tile_of(increment, f, s, 1), pltpu.roll(lanes, spread_shift(INC + f), 1)]
            for f in range(3)
        ]

    def put(s, new):
        for f in range(3):
            for t in range(2):
                set_tile(ahead, f, s, t, -new[f][t])
        own[pl.ds(s, GROUP), :] = pack_three([-new[f][2] for f in range(3)])

    run_tangent(get, traj, packed, wide_a, wide_b, total, put)
    turn_out(own, ahead_edges)


def whole(count):
    return [pl.BlockSpec(memory_space=pltpu.VMEM)] * count


def cost(mib, steps=2):
    return pl.CostEstimate(flops=steps * 40 * 2**20, bytes_accessed=mib * 2**20, transcendentals=0)


def tangent_first(increment, traj, from_left, from_right):
    rows = increment.shape[1]
    return pl.pallas_call(
        tangent_first_kernel,
        in_specs=whole(4),
        out_specs=whole(4),
        out_shape=[
            jax.ShapeDtypeStruct(increment.shape, F32),
            jax.ShapeDtypeStruct((24, rows), F32),
            jax.ShapeDtypeStruct((rows, LANE), F32),
            jax.ShapeDtypeStruct((24, rows), F32),
        ],
        scratch_shapes=[wide_scratch(rows)] * 2 + [pltpu.VMEM((rows, LANE), F32)],
        compiler_params=PARAMS,
        cost_estimate=cost(10),
        name="tangent_first",
    )(increment, traj, from_left, from_right)


def adjoint_first_kernel(
    later, later_edges, traj, packed, spread, z_left, z_right, pulled, pulled_edges,
    wide_a, wide_b, flux_a, flux_b, own, z_own,
):
    total = later.shape[1]
    turn_in(later_edges, own)
    for j in range(total // LANE):
        cut = slice(j * LANE, (j + 1) * LANE)
        z_own[cut, :] = padded_turn(joined_edges(z_left[:, cut], z_right[:, cut], 4))

    def get(s):
        lanes = own[pl.ds(s, GROUP), :]
        return [
            [tile_of(later, f, s, 0), tile_of(later, f, s, 1), pltpu.roll(lanes, spread_shift(f), 1)]
            for f in range(3)
        ]

    def put(s, new):
        lanes = z_own[pl.ds(s, GROUP), :]
        halo = []
        for f in range(3):
            for t in range(2):
                set_tile(pulled, f, s, t, tile_of(spread, f, s, t) - new[f][t])
            halo.append(pltpu.roll(lanes, spread_shift(f), 1) - new[f][2])
        own[pl.ds(s, GROUP), :] = pack_three(halo)

    run_adjoint(get, traj, packed, wide_a, wide_b, flux_a, flux_b, total, put)
    turn_out(own, pulled_edges)


def adjoint_first(later, later_edges, traj, packed, spread, z_left, z_right):
    rows = later.shape[1]
    return pl.pallas_call(
        adjoint_first_kernel,
        in_specs=whole(7),
        out_specs=whole(2),
        out_shape=[jax.ShapeDtypeStruct(later.shape, F32), jax.ShapeDtypeStruct((24, rows), F32)],
        scratch_shapes=[wide_scratch(rows)] * 4 + [pltpu.VMEM((rows, LANE), F32)] * 2,
        compiler_params=PARAMS,
        cost_estimate=cost(13),
        name="adjoint_first",
    )(later, later_edges, traj, packed, spread, z_left, z_right)


def tangent_second_kernel(
    earlier, earlier_edges, pulled, pulled_edges, variance, traj, packed, increment, ahead, wide_a, wide_b, e_own, p_own
):
    total = earlier.shape[1]
    turn_in(earlier_edges, e_own)
    turn_in(pulled_edges, p_own)

    def get(s):
        e_lanes = e_own[pl.ds(s, GROUP), :]
        p_lanes = p_own[pl.ds(s, GROUP), :]
        v_lanes = packed[pl.ds(s, GROUP), :]
        out = []
        for f in range(3):
            tiles = [tile_of(earlier, f, s, t) - tile_of(variance, f, s, t) * tile_of(pulled, f, s, t) for t in range(2)]
            for t in range(2):
                set_tile(increment, f, s, t, tiles[t])
            shift = spread_shift(f)
            tiles.append(
                pltpu.roll(e_lanes, shift, 1)
                - pltpu.roll(v_lanes, spread_shift(VAR + f), 1) * pltpu.roll(p_lanes, shift, 1)
            )
            out.append(tiles)
        return out

    def put(s, new):
        for f in range(3):
            for t in range(2):
                set_tile(ahead, f, s, t, -new[f][t])

    run_tangent(get, traj, packed, wide_a, wide_b, total, put)


def tangent_second(earlier, earlier_edges, pulled, pulled_edges, variance, traj, packed):
    rows = earlier.shape[1]
    return pl.pallas_call(
        tangent_second_kernel,
        in_specs=whole(7),
        out_specs=whole(2),
        out_shape=[jax.ShapeDtypeStruct(earlier.shape, F32)] * 2,
        scratch_shapes=[wide_scratch(rows)] * 2 + [pltpu.VMEM((rows, LANE), F32)] * 2,
        compiler_params=PARAMS,
        cost_estimate=cost(18),
        name="tangent_second",
    )(earlier, earlier_edges, pulled, pulled_edges, variance, traj, packed)


def adjoint_second_kernel(
    later, later_edges, traj, packed, spread, last, pulled, sums, wide_a, wide_b, flux_a, flux_b, own
):
    total = later.shape[1]
    turn_in(later_edges, own)
    sums[...] = jnp.zeros_like(sums)

    def get(s):
        lanes = own[pl.ds(s, GROUP), :]
        return [
            [tile_of(later, f, s, 0), tile_of(later, f, s, 1), pltpu.roll(lanes, spread_shift(f), 1)]
            for f in range(3)
        ]

    def put(s, new):
        parts = [jnp.zeros((GROUP, LANE), F32)] * 3
        for f in range(3):
            for t in range(2):
                value = tile_of(spread, f, s, t) - new[f][t]
                for k, other in enumerate((tile_of(last, f, s, t), tile_of(pulled, f, s, t), value)):
                    parts[k] = parts[k] + other * value
        for k in range(3):
            sums[k] = sums[k] + parts[k]

    run_adjoint(get, traj, packed, wide_a, wide_b, flux_a, flux_b, total, put)


def adjoint_second(later, later_edges, traj, packed, spread, last, pulled):
    rows = later.shape[1]
    return pl.pallas_call(
        adjoint_second_kernel,
        in_specs=whole(7),
        out_specs=pl.BlockSpec(memory_space=pltpu.VMEM),
        out_shape=jax.ShapeDtypeStruct((3, GROUP, LANE), F32),
        scratch_shapes=[wide_scratch(rows)] * 4 + [pltpu.VMEM((rows, LANE), F32)],
        compiler_params=PARAMS,
        cost_estimate=cost(16),
        name="adjoint_second",
    )(later, later_edges, traj, packed, spread, last, pulled)


def products_kernel(pairs, *refs):
    arrays, sums = refs[:-1], refs[-1]

    @pl.when(pl.program_id(0) == 0)
    def _():
        sums[...] = jnp.zeros_like(sums)

    for k, (i, j) in enumerate(pairs):
        product = arrays[i][...] * arrays[j][...]
        sums[k] = sums[k] + jnp.sum(product.reshape(-1, 8, product.shape[-1]), axis=0)


def products(pairs, arrays):
    rows = arrays[0].shape[1]
    block = pl.BlockSpec((3, LANE, 2 * LANE), lambda i: (0, i, 0))
    return pl.pallas_call(
        functools.partial(products_kernel, pairs),
        grid=(rows // LANE,),
        in_specs=[block] * len(arrays),
        out_specs=pl.BlockSpec((len(pairs), 8, 2 * LANE), lambda i: (0, 0, 0)),
        out_shape=jax.ShapeDtypeStruct((len(pairs), 8, 2 * LANE), F32),
        compiler_params=PARAMS,
        cost_estimate=cost(3 * len(arrays), 1),
        name="products",
    )(*arrays)


def mesh_sums(row):
    count = lax.axis_size("tm") * lax.axis_size("lon")
    sent = jnp.broadcast_to(row, (count, 8, LANE))
    received = lax.all_to_all(sent, ("tm", "lon"), 0, 0)
    return jnp.sum(received[:, 0, :], axis=0)


def weights(s00, s01, s02, s11, s12, s22):
    alpha = s01 / s00
    t11 = s11 - alpha * s01
    along = (s12 - alpha * s02) / t11
    beta = jnp.sqrt(s00)
    gamma = 1.0 / jnp.sqrt(t11)
    h00 = 1.0 + alpha
    h10_square = t11 / s00
    h10 = jnp.sqrt(h10_square)
    h01 = (s02 - alpha * s01) * gamma / beta
    h11 = 1.0 - alpha + along
    h21_square = (s22 - s02 * (s02 / s00) - along * (s12 - alpha * s02)) / t11
    g00 = h00 * h00 + h10_square
    g01 = h00 * h01 + h10 * h11
    g11 = h01 * h01 + h11 * h11 + h21_square
    q0 = beta * h00
    q1 = beta * h01
    det = g00 * g11 - g01 * g01
    y0 = (g11 * q0 - g01 * q1) / det
    y1 = (g00 * q1 - g01 * q0) / det
    c1 = y1 * gamma
    return (y0 / beta - c1 * alpha, c1)


def moved(block, axis, distance, wrap):
    size = lax.axis_size(axis)
    if wrap:
        route = [(i, (i + distance) % size) for i in range(size)]
    else:
        route = [(i, i + distance) for i in range(size) if 0 <= i + distance < size]
    return lax.ppermute(block, axis, route)


def shards(rhs_state, innovations, trajectory, model_var, obs_var, obs_index, control_rhs):
    rows, columns = rhs_state.shape[2:]
    first, last, variance = rhs_state[0], control_rhs[0], model_var[0]
    traj = trajectory.reshape(-1, rows, columns)
    middle, obs_part, where = innovations[0], obs_var[0], obs_index[0]

    def observed(field):
        return field.reshape(-1)[where]

    def spread(values):
        flat = jnp.zeros((3 * rows * columns,), F32).at[where].add(values / obs_part)
        return flat.reshape(3, rows, columns)

    later = moved(last, "tm", -1, False)
    to_right, to_left, inc0 = edges_call(first, last, variance, traj)
    from_left = moved(to_right, "lon", 1, True)
    from_right = moved(to_left, "lon", -1, True)
    ahead, ahead_edges, packed, last_edges = tangent_first(inc0, traj, from_left, from_right)
    a1 = moved(ahead, "tm", 1, False)
    a1_edges = moved(ahead_edges, "tm", 1, False)
    later_edges = moved(last_edges, "tm", -1, False)
    z0 = spread(middle)
    z_right, z_left = spread_edges_call(z0)
    z_left, z_right = moved(z_right, "lon", 1, True), moved(z_left, "lon", -1, True)
    m1 = observed(inc0)
    d1, d1_edges = adjoint_first(later, later_edges, traj, packed, z0, z_left, z_right)

    d1_later = moved(d1, "tm", -1, False)
    d1_later_edges = moved(d1_edges, "tm", -1, False)
    inc1, ahead2 = tangent_second(a1, a1_edges, d1, d1_edges, variance, traj, packed)
    a2 = moved(ahead2, "tm", 1, False)
    z1 = spread(m1)
    m2 = observed(inc1)
    early = products(((0, 0), (1, 1), (0, 2), (1, 3), (2, 2), (3, 3)), (first, last, a1, d1))
    d_sums = adjoint_second(d1_later, d1_later_edges, traj, packed, z1, last, d1)
    a_sums = products(((0, 2), (1, 2), (2, 2)), (first, a1, a2))

    early = jnp.sum(early, axis=(1, 2))
    d_sums = jnp.sum(d_sums, axis=(1, 2))
    a_sums = jnp.sum(a_sums, axis=(1, 2))
    scalars = jnp.stack(
        [
            early[0] + early[1] + jnp.sum(middle * middle),
            early[2] + early[3] + jnp.sum(middle * m1),
            d_sums[0] + a_sums[0] + jnp.sum(middle * m2),
            early[4] + early[5] + jnp.sum(m1 * m1),
            d_sums[1] + a_sums[1] + jnp.sum(m1 * m2),
            d_sums[2] + a_sums[2] + jnp.sum(m2 * m2),
        ]
    )
    total = mesh_sums(jnp.pad(scalars, (0, LANE - 6)))
    c0, c1 = weights(*[total[k] for k in range(6)])
    return (
        (c0 * last + c1 * d1)[None],
        ((c0 * middle + c1 * m1) / obs_part)[None],
        (c0 * inc0 + c1 * inc1)[None],
    )


def solution(mesh):
    in_specs = (
        P("tm", None, None, "lon"),
        P("tm", "lon"),
        P("tm", None, None, None, "lon"),
        P("tm", None, None, "lon"),
        P("tm", "lon"),
        P("tm", "lon"),
        P("tm", None, None, "lon"),
    )
    out_specs = (P("tm", None, None, "lon"), P("tm", "lon"), P("tm", None, None, "lon"))
    return jax.shard_map(shards, mesh=mesh, in_specs=in_specs, out_specs=out_specs, check_vma=False)
```

profile of v0, /device:TPU:0, one launch (start us, length us, event | category | flops | bytes accessed | tf_op | source)
XLA Modules:
  0.0 287.8 jit_solution(15556591001242910886)
XLA Ops:
  0.6 9.4 %edges.1 = (f32[64,1024]{1,0:T(8,128)}, f32[64,1024]{1,0:T(8,128)}, f32[3,1024,256]{2,1,0:T(8,128)}) custom-call(f32[3,1024,256]{2,1,0:T(8,128)} %bitcast.48, f32[3,1024,256]{2,1,0:T(8,128)} %bitcast.43, f32[3,1024,256]{2,1,0:T(8,128)} %bitcast.54, bf16[6,1024,256]{2,1,0:T(8,128)(2,1)} %bitcast.38), custom_call_target="tpu_custom_call" | custom-call | flops 1000000 | bytes 16777216 | tf_op jit(solution)/shard_map/edges/pallas_call | solution.py:87
  10.5 2.9 %collective-permute-start.1 = (f32[64,1024]{1,0:T(8,128)}, f32[64,1024]{1,0:T(8,128)S(1)}, u32[]{:S(2)}, u32[]{:S(2)}) collective-permute-start(f32[64,1024]{1,0:T(8,128)} %get-tuple-element.18), channel_id=1, source_target_pairs={{0,7},{1,0},{2,1},{3,2},{4,3},{5,4},{6,5},{7,6},{8,15},{9,8},{10,9... | collective-permute-start | bytes 786440 | tf_op jit(solution)/shard_map/ppermute | solution.py:541
  14.8 3.1 %collective-permute-done.from_left = f32[64,1024]{1,0:T(8,128)S(1)} collective-permute-done((f32[64,1024]{1,0:T(8,128)}, f32[64,1024]{1,0:T(8,128)S(1)}, u32[]{:S(2)}, u32[]{:S(2)}) %collective-permute-start) | collective-permute-done | bytes 262176 | tf_op jit(solution)/shard_map/ppermute | solution.py:541
  20.1 29.1 %tangent_first.1 = (f32[3,1024,256]{2,1,0:T(8,128)}, f32[24,1024]{1,0:T(8,128)}, f32[1024,128]{1,0:T(8,128)}, f32[24,1024]{1,0:T(8,128)}) custom-call(f32[3,1024,256]{2,1,0:T(8,128)} %get-tuple-element.16.increment, bf16[6,1024,256]{2,1,0:T(8,128)(2,1)} %bitcast.39, f32[64,1024]{1,0:T(8,128)} %copy-done.5, f32[64,1024]{1,0:T(8,128)} %copy-done.6), custom_call_target="tpu_custom_call" | custom-call | flops 83886080 | bytes 10485760 | tf_op jit(solution)/shard_map/tangent_first/pallas_call | solution.py:329
  49.2 5.2 %collective-permute-start.2 = (f32[3,1024,256]{2,1,0:T(8,128)}, f32[3,1024,256]{2,1,0:T(8,128)}, u32[]{:S(2)}, u32[]{:S(2)}) collective-permute-start(f32[3,1024,256]{2,1,0:T(8,128)} %get-tuple-element.19), channel_id=1, source_target_pairs={{0,8},{8,16},{16,24},{1,9},{9,17},{17,25},{2,10},{10,18},{18,26},{... | collective-permute-start | bytes 9437192 | tf_op jit(solution)/shard_map/ppermute | solution.py:541
  54.4 3.3 %copy.11 = f32[384,2,8,128]{3,1,2,0:T(2,128)} copy(f32[384,2,8,128]{3,2,1,0:T(8,128)S(1)} %bitcast.47) | data formatting | bytes 6291456
  57.7 12.5 %gather_fusion = f32[1024]{0:T(1024)S(1)} fusion(f32[786432]{0:T(1024)} %bitcast.51, s32[1024]{0:T(1024)S(1)} %broadcast_clamp_fusion), kind=kCustom, calls=%fused_computation | custom fusion | bytes 12288 | tf_op jit(solution)/shard_map/gather | solution.py:551
  70.3 7.7 %scatter_custom_fusion = f32[786432]{0:T(1024)} fusion(s32[1024]{0:T(1024)S(1)} %bitcast.61, f32[1024]{0:T(1024)S(1)} %get-tuple-element.36, f32[]{:T(128)} %constant.4.clone.1), kind=kCustom, calls=%fused_computation.8 | custom fusion | flops 1024 | bytes 3145732 | tf_op jit(solution)/shard_map/scatter-add | solution.py:554
  78.0 4.8 %reshape.65.spread = f32[3,1024,256]{2,1,0:T(8,128)} reshape(f32[786432]{0:T(1024)} %scatter_custom_fusion) | data formatting | bytes 6291456 | tf_op jit(solution)/shard_map/reshape | solution.py:555
  82.8 6.0 %spread_edges.1 = (f32[16,1024]{1,0:T(8,128)}, f32[16,1024]{1,0:T(8,128)}) custom-call(f32[3,1024,256]{2,1,0:T(8,128)} %reshape.65.spread), custom_call_target="tpu_custom_call" | custom-call | flops 1000000 | bytes 3145728 | tf_op jit(solution)/shard_map/spread_edges/pallas_call | solution.py:108
  91.9 4.6 %collective-permute-start.9 = (f32[24,1024]{1,0:T(8,128)S(1)}, f32[24,1024]{1,0:T(8,128)S(1)}, u32[]{:S(2)}, u32[]{:S(2)}) collective-permute-start(f32[24,1024]{1,0:T(8,128)S(1)} %copy-done.16), channel_id=1, source_target_pairs={{0,8},{8,16},{16,24},{1,9},{9,17},{17,25},{2,10},{10,18},{18,26},{... | collective-permute-start | bytes 294920 | tf_op jit(solution)/shard_map/ppermute | solution.py:541
  96.8 2.2 collective-permute-done.6.z_right
  99.7 36.0 %adjoint_first.1 = (f32[3,1024,256]{2,1,0:T(8,128)}, f32[24,1024]{1,0:T(8,128)}) custom-call(f32[3,1024,256]{2,1,0:T(8,128)} %collective-permute-done.3.later, f32[24,1024]{1,0:T(8,128)} %copy-done.10, bf16[6,1024,256]{2,1,0:T(8,128)(2,1)} %bitcast.40, f32[1024,128]{1,0:T(8,128)} %get-tuple-element.21.packed, f32[3,1024,256]{2,1,0:T(8,128)} %reshape.65.spread, ...), custom_call_target="tpu_custom_call" | custom-call | flops 83886080 | bytes 13631488 | tf_op jit(solution)/shard_map/adjoint_first/pallas_call | solution.py:378
  137.7 29.1 %tangent_second.1 = (f32[3,1024,256]{2,1,0:T(8,128)}, f32[3,1024,256]{2,1,0:T(8,128)}) custom-call(f32[3,1024,256]{2,1,0:T(8,128)} %collective-permute-done.2.refs_2_.earlier.refs_1_, f32[24,1024]{1,0:T(8,128)} %copy-done.9, f32[3,1024,256]{2,1,0:T(8,128)} %get-tuple-element.24.refs_3_.pulled, f32[24,1024]{1,0:T(8,128)} %get-tuple-element.25.pulled_edges, ...), custom_call_target="tpu_custom_call" | custom-call | flops 83886080 | bytes 18874368 | tf_op jit(solution)/shard_map/tangent_second/pallas_call | solution.py:424
  166.8 6.2 %collective-permute-start.10 = (f32[3,1024,256]{2,1,0:T(8,128)}, f32[3,1024,256]{2,1,0:T(8,128)}, u32[]{:S(2)}, u32[]{:S(2)}) collective-permute-start(f32[3,1024,256]{2,1,0:T(8,128)} %get-tuple-element.27), channel_id=1, source_target_pairs={{0,8},{8,16},{16,24},{1,9},{9,17},{17,25},{2,10},{10,18},{18,26},{... | collective-permute-start | bytes 9437192 | tf_op jit(solution)/shard_map/ppermute | solution.py:541
  173.0 6.7 %scatter_custom_fusion.1 = f32[786432]{0:T(1024)S(1)} fusion(s32[1024]{0:T(1024)S(1)} %bitcast.62, f32[1024]{0:T(1024)S(1)} %get-tuple-element.35, f32[]{:T(128)} %constant.4.clone.1), kind=kCustom, calls=%fused_computation.6 | custom fusion | flops 1024 | bytes 3145732 | tf_op jit(solution)/shard_map/scatter-add | solution.py:554
  179.7 2.6 reshape.67.spread
  183.7 7.7 %products.2 = f32[6,8,256]{2,1,0:T(8,128)} custom-call(f32[3,1024,256]{2,1,0:T(8,128)} %bitcast.49, f32[3,1024,256]{2,1,0:T(8,128)} %bitcast.44, f32[3,1024,256]{2,1,0:T(8,128)} %collective-permute-done.2.refs_2_.earlier.refs_1_, f32[3,1024,256]{2,1,0:T(8,128)} %get-tuple-element.24.refs_3_.pulled), custom_call_target="tpu_custom_call" | custom-call | flops 41943040 | bytes 12582912 | tf_op jit(solution)/shard_map/products/pallas_call | solution.py:492
  192.3 3.5 %copy.12 = f32[384,2,8,128]{3,1,2,0:T(2,128)S(1)} copy(f32[384,2,8,128]{3,2,1,0:T(8,128)} %bitcast.53) | data formatting | bytes 6291456
  195.8 6.2 %gather_fusion.1 = f32[1024]{0:T(1024)S(1)} fusion(f32[786432]{0:T(1024)S(1)} %bitcast.52, s32[1024]{0:T(1024)S(1)} %broadcast_clamp_fusion), kind=kCustom, calls=%fused_computation.1 | custom fusion | bytes 12288 | tf_op jit(solution)/shard_map/gather | solution.py:551
  211.5 32.6 %adjoint_second.1 = f32[3,16,128]{2,1,0:T(8,128)} custom-call(f32[3,1024,256]{2,1,0:T(8,128)} %collective-permute-done.7.later, f32[24,1024]{1,0:T(8,128)} %copy-done.8, bf16[6,1024,256]{2,1,0:T(8,128)(2,1)} %bitcast.42, f32[1024,128]{1,0:T(8,128)} %get-tuple-element.21.packed, f32[3,1024,256]{2,1,0:T(8,128)} %reshape.67.spread, f32[3,1024,256]{2,1,0:T(8,128)} %bitcast.45, ...), custom_call_target="tpu_custom_call" | custom-call | flops 83886080 | bytes 16777216 | tf_op jit(solution)/shard_map/adjoint_second/pallas_call | solution.py:465
  244.9 6.9 %products.3 = f32[3,8,256]{2,1,0:T(8,128)} custom-call(f32[3,1024,256]{2,1,0:T(8,128)} %bitcast.50, f32[3,1024,256]{2,1,0:T(8,128)} %collective-permute-done.2.refs_2_.earlier.refs_1_, f32[3,1024,256]{2,1,0:T(8,128)} %collective-permute-done.10.refs_2_), custom_call_target="tpu_custom_call" | custom-call | flops 41943040 | bytes 9437184 | tf_op jit(solution)/shard_map/products/pallas_call | solution.py:492
  259.1 11.9 %all_to_all.5 = f32[32,8,128]{2,1,0:T(8,128)S(1)} all-to-all(f32[32,8,128]{2,1,0:T(8,128)S(1)} %broadcast_in_dim.6), channel_id=1, replica_groups=mesh['tm'=4,'lon'=8] {'tm','lon'}, dimensions={0} | all-to-all | bytes 262144 | tf_op jit(solution)/shard_map/all_to_all | solution.py:507
  280.6 4.1 %add_bitcast_fusion.1 = f32[1,3,1024,256]{3,2,1,0:T(8,128)} fusion(f32[3,1024,256]{2,1,0:T(8,128)} %get-tuple-element.24.refs_3_.pulled, f32[]{:T(128)S(6)} %mul.147, f32[]{:T(128)S(6)} %sub.40, f32[1,3,1024,256]{3,2,1,0:T(8,128)S(1)} %copy-done.1), kind=kLoop, calls=%fused_computation.5 | loop fusion | flops 2359296 | bytes 9437192 | tf_op jit(solution)/shard_map/broadcast_in_dim | solution.py:597
  (70 shorter events, 22.5 us)
Async XLA Ops:
  0.6 12.8 %copy-start = (f32[1,3,1024,256]{3,2,1,0:T(8,128)S(1)}, f32[1,3,1024,256]{3,2,1,0:T(8,128)}, u32[]{:S(2)}) copy-start(f32[1,3,1024,256]{3,2,1,0:T(8,128)} %param.13) | copy-start | bytes 9437188
  10.1 7.7 %collective-permute-start = (f32[64,1024]{1,0:T(8,128)}, f32[64,1024]{1,0:T(8,128)S(1)}, u32[]{:S(2)}, u32[]{:S(2)}) collective-permute-start(f32[64,1024]{1,0:T(8,128)} %get-tuple-element.17), channel_id=1, source_target_pairs={{0,1},{1,2},{2,3},{3,4},{4,5},{5,6},{6,7},{7,0},{8,9},{9,10},{10,1... | collective-permute-start | bytes 786440 | tf_op jit(solution)/shard_map/ppermute | solution.py:541
  10.5 8.9 %collective-permute-start.1 = (f32[64,1024]{1,0:T(8,128)}, f32[64,1024]{1,0:T(8,128)S(1)}, u32[]{:S(2)}, u32[]{:S(2)}) collective-permute-start(f32[64,1024]{1,0:T(8,128)} %get-tuple-element.18), channel_id=1, source_target_pairs={{0,7},{1,0},{2,1},{3,2},{4,3},{5,4},{6,5},{7,6},{8,15},{9,8},{10,9... | collective-permute-start | bytes 786440 | tf_op jit(solution)/shard_map/ppermute | solution.py:541
  13.5 85.6 %collective-permute-start.3 = (f32[3,1024,256]{2,1,0:T(8,128)S(1)}, f32[3,1024,256]{2,1,0:T(8,128)}, u32[]{:S(2)}, u32[]{:S(2)}) collective-permute-start(f32[3,1024,256]{2,1,0:T(8,128)S(1)} %bitcast.46), channel_id=1, source_target_pairs={{8,0},{16,8},{24,16},{9,1},{17,9},{25,17},{10,2},{18,10},{26,18},{... | collective-permute-start | bytes 9437192 | tf_op jit(solution)/shard_map/ppermute | solution.py:541
  17.8 1.6 copy-start.5
  20.1 34.3 %copy-start.2 = (f32[3,1024,256]{2,1,0:T(8,128)S(1)}, f32[3,1024,256]{2,1,0:T(8,128)}, u32[]{:S(2)}) copy-start(f32[3,1024,256]{2,1,0:T(8,128)} %get-tuple-element.16.increment) | copy-start | bytes 9437188
  49.2 87.8 %collective-permute-start.2 = (f32[3,1024,256]{2,1,0:T(8,128)}, f32[3,1024,256]{2,1,0:T(8,128)}, u32[]{:S(2)}, u32[]{:S(2)}) collective-permute-start(f32[3,1024,256]{2,1,0:T(8,128)} %get-tuple-element.19), channel_id=1, source_target_pairs={{0,8},{8,16},{16,24},{1,9},{9,17},{17,25},{2,10},{10,18},{18,26},{... | collective-permute-start | bytes 9437192 | tf_op jit(solution)/shard_map/ppermute | solution.py:541
  54.4 3.3 %copy-start.15 = (s32[1,1024]{1,0:T(1,128)S(1)}, s32[1,1024]{1,0:T(1,128)}, u32[]{:S(2)}) copy-start(s32[1,1024]{1,0:T(1,128)} %param.12) | copy-start | bytes 12292
  57.7 12.5 %copy-start.13 = (f32[1,1024]{1,0:T(1,128)S(1)}, f32[1,1024]{1,0:T(1,128)}, u32[]{:S(2)}) copy-start(f32[1,1024]{1,0:T(1,128)} %param.8) | copy-start | bytes 12292
  57.7 12.5 %copy-start.14 = (f32[1,1024]{1,0:T(1,128)S(1)}, f32[1,1024]{1,0:T(1,128)}, u32[]{:S(2)}) copy-start(f32[1,1024]{1,0:T(1,128)} %param.11) | copy-start | bytes 12292
  82.8 7.8 %copy-start.17 = (f32[24,1024]{1,0:T(8,128)S(1)}, f32[24,1024]{1,0:T(8,128)}, u32[]{:S(2)}) copy-start(f32[24,1024]{1,0:T(8,128)} %get-tuple-element.20) | copy-start | bytes 294916
  82.8 9.1 %copy-start.16 = (f32[24,1024]{1,0:T(8,128)S(1)}, f32[24,1024]{1,0:T(8,128)}, u32[]{:S(2)}) copy-start(f32[24,1024]{1,0:T(8,128)} %get-tuple-element.26) | copy-start | bytes 294916
  88.8 7.6 %collective-permute-start.5 = (f32[16,1024]{1,0:T(8,128)}, f32[16,1024]{1,0:T(8,128)S(1)}, u32[]{:S(2)}, u32[]{:S(2)}) collective-permute-start(f32[16,1024]{1,0:T(8,128)} %get-tuple-element.22), channel_id=1, source_target_pairs={{0,1},{1,2},{2,3},{3,4},{4,5},{5,6},{6,7},{7,0},{8,9},{9,10},{10,1... | collective-permute-start | bytes 196616 | tf_op jit(solution)/shard_map/ppermute | solution.py:541
  90.6 8.5 %collective-permute-start.4 = (f32[24,1024]{1,0:T(8,128)S(1)}, f32[24,1024]{1,0:T(8,128)S(1)}, u32[]{:S(2)}, u32[]{:S(2)}) collective-permute-start(f32[24,1024]{1,0:T(8,128)S(1)} %copy-done.17), channel_id=1, source_target_pairs={{8,0},{16,8},{24,16},{9,1},{17,9},{25,17},{10,2},{18,10},{26,18},{... | collective-permute-start | bytes 294920 | tf_op jit(solution)/shard_map/ppermute | solution.py:541
  91.9 45.2 %collective-permute-start.9 = (f32[24,1024]{1,0:T(8,128)S(1)}, f32[24,1024]{1,0:T(8,128)S(1)}, u32[]{:S(2)}, u32[]{:S(2)}) collective-permute-start(f32[24,1024]{1,0:T(8,128)S(1)} %copy-done.16), channel_id=1, source_target_pairs={{0,8},{8,16},{16,24},{1,9},{9,17},{17,25},{2,10},{10,18},{18,26},{... | collective-permute-start | bytes 294920 | tf_op jit(solution)/shard_map/ppermute | solution.py:541
  96.5 2.6 copy-start.11
  96.5 2.6 collective-permute-start.6
  135.8 75.1 %collective-permute-start.7 = (f32[3,1024,256]{2,1,0:T(8,128)}, f32[3,1024,256]{2,1,0:T(8,128)}, u32[]{:S(2)}, u32[]{:S(2)}) collective-permute-start(f32[3,1024,256]{2,1,0:T(8,128)} %get-tuple-element.24.refs_3_.pulled), channel_id=1, source_target_pairs={{8,0},{16,8},{24,16},{9,1},{17,9},{25,17},{10,2},{18,10},{26,18},{... | collective-permute-start | bytes 9437192 | tf_op jit(solution)/shard_map/ppermute | solution.py:541
  166.8 78.1 %collective-permute-start.10 = (f32[3,1024,256]{2,1,0:T(8,128)}, f32[3,1024,256]{2,1,0:T(8,128)}, u32[]{:S(2)}, u32[]{:S(2)}) collective-permute-start(f32[3,1024,256]{2,1,0:T(8,128)} %get-tuple-element.27), channel_id=1, source_target_pairs={{0,8},{8,16},{16,24},{1,9},{9,17},{17,25},{2,10},{10,18},{18,26},{... | collective-permute-start | bytes 9437192 | tf_op jit(solution)/shard_map/ppermute | solution.py:541
  179.7 2.6 copy-start.7
  182.3 28.6 %collective-permute-start.8 = (f32[24,1024]{1,0:T(8,128)S(1)}, f32[24,1024]{1,0:T(8,128)S(1)}, u32[]{:S(2)}, u32[]{:S(2)}) collective-permute-start(f32[24,1024]{1,0:T(8,128)S(1)} %copy-done.7), channel_id=1, source_target_pairs={{8,0},{16,8},{24,16},{9,1},{17,9},{25,17},{10,2},{18,10},{26,18},{... | collective-permute-start | bytes 294920 | tf_op jit(solution)/shard_map/ppermute | solution.py:541
  244.9 35.7 %copy-start.1 = (f32[1,3,1024,256]{3,2,1,0:T(8,128)S(1)}, f32[1,3,1024,256]{3,2,1,0:T(8,128)}, u32[]{:S(2)}) copy-start(f32[1,3,1024,256]{3,2,1,0:T(8,128)} %param.13) | copy-start | bytes 9437188
  280.6 4.2 %copy-start.3 = (f32[3,1024,256]{2,1,0:T(8,128)S(1)}, f32[3,1024,256]{2,1,0:T(8,128)}, u32[]{:S(2)}) copy-start(f32[3,1024,256]{2,1,0:T(8,128)} %get-tuple-element.16.increment) | copy-start | bytes 9437188
  280.6 4.5 %copy-start.4 = (f32[3,1024,256]{2,1,0:T(8,128)S(1)}, f32[3,1024,256]{2,1,0:T(8,128)}, u32[]{:S(2)}) copy-start(f32[3,1024,256]{2,1,0:T(8,128)} %get-tuple-element.28) | copy-start | bytes 9437188
  (5 other events, 3.3 us)
where the time goes:
time: 289 us; the launch traced here: 288 us
  Pallas kernels  157 us (54%)
  local copies, waits for them, and re-layouts  38 us (13%)
  starting transfers between devices  26.7 us (9%)
  other arithmetic  24.5 us (8%)
  between operations  21 us (7%)
  blocking collectives  11.9 us (4%)
  waiting for transfers between devices  8.8 us (3%)
    pallas_call x1, Pallas kernels, adjoint_first(): pl.pallas_call(adjoint_first_kernel, in_specs=whole(7), out_specs=whole(2...  36 us
    pallas_call x1, Pallas kernels, adjoint_second(): pl.pallas_call(adjoint_second_kernel, in_specs=whole(7), out_specs=pl.Blo...  32.6 us
    pallas_call x1, Pallas kernels, tangent_first(): pl.pallas_call(tangent_first_kernel, in_specs=whole(4), out_specs=whole(4...  29.1 us
    pallas_call x1, Pallas kernels, tangent_second(): pl.pallas_call(tangent_second_kernel, in_specs=whole(7), out_specs=whole(...  29.1 us
    ppermute x11, starting transfers between devices, moved(): return lax.ppermute(block, axis, route)  26.7 us
    gather x2, local copies, waits for them, and re-layouts, observed(): return field.reshape(-1)[where]  18.7 us
    pallas_call x2, Pallas kernels, products(): pl.pallas_call(functools.partial(products_kernel, pairs), grid=(rows // L...  14.6 us
    scatter-add x2, other arithmetic, spread(): jnp.zeros((3 * rows * columns,), F32).at[where].add(values / obs_part)  14.4 us
  transfers between devices with their start and end apart: 11, of which 4 were waited for; matrix products, arithmetic and copies ran while one was open for 18% of the time, Pallas kernels for 49%

commit v1 on v0

--- a/solution.py
+++ b/solution.py
@@ -12,6 +12,7 @@
 slope = 0.5 * courant
 
 LANE = 128
+BLOCK = 256
 GROUP = 16
 MARGIN = 8
 HALO = 4
@@ -82,17 +83,17 @@
 
 def edges_call(first, last, variance, traj):
     rows = first.shape[1]
-    block = pl.BlockSpec((3, LANE, 2 * LANE), lambda i: (0, i, 0))
-    sent = pl.BlockSpec((PLANES * HALO, LANE), lambda i: (0, i))
+    block = pl.BlockSpec((3, BLOCK, 2 * LANE), lambda i: (0, i, 0))
+    sent = pl.BlockSpec((PLANES * HALO, BLOCK), lambda i: (0, i))
     return pl.pallas_call(
         edges_kernel,
-        grid=(rows // LANE,),
-        in_specs=[block, block, block, pl.BlockSpec((6, LANE, 2 * LANE), lambda i: (0, i, 0))],
+        grid=(rows // BLOCK,),
+        in_specs=[block, block, block, pl.BlockSpec((6, BLOCK, 2 * LANE), lambda i: (0, i, 0))],
         out_specs=[sent, sent, block],
         out_shape=[jax.ShapeDtypeStruct((PLANES * HALO, rows), F32)] * 2
         + [jax.ShapeDtypeStruct(first.shape, F32)],
         compiler_params=PARAMS,
-        cost_estimate=pl.CostEstimate(flops=10**6, bytes_accessed=16 * 2**20, transcendentals=0),
+        cost_estimate=cost(16),
         name="edges",
     )(first, last, variance, traj)
 
@@ -104,15 +105,15 @@
 
 def spread_edges_call(spread):
     rows = spread.shape[1]
-    sent = pl.BlockSpec((16, LANE), lambda i: (0, i))
+    sent = pl.BlockSpec((16, BLOCK), lambda i: (0, i))
     return pl.pallas_call(
         spread_edges_kernel,
-        grid=(rows // LANE,),
-        in_specs=[pl.BlockSpec((3, LANE, 2 * LANE), lambda i: (0, i, 0))],
+        grid=(rows // BLOCK,),
+        in_specs=[pl.BlockSpec((3, BLOCK, 2 * LANE), lambda i: (0, i, 0))],
         out_specs=[sent, sent],
         out_shape=[jax.ShapeDtypeStruct((16, rows), F32)] * 2,
         compiler_params=PARAMS,
-        cost_estimate=pl.CostEstimate(flops=10**6, bytes_accessed=3 * 2**20, transcendentals=0),
+        cost_estimate=cost(3),
         name="spread_edges",
     )(spread)
 
@@ -226,7 +227,7 @@
         body(pl.multiple_of(i * GROUP, GROUP))
         return carry
 
-    lax.fori_loop(0, total // GROUP, step, 0)
+    lax.fori_loop(0, total // GROUP, step, 0, unroll=4)
 
 
 def turn_in(message, packed_ref):
@@ -321,7 +322,7 @@
 
 
 def cost(mib, steps=2):
-    return pl.CostEstimate(flops=steps * 40 * 2**20, bytes_accessed=mib * 2**20, transcendentals=0)
+    return pl.CostEstimate(flops=steps * 2**10, bytes_accessed=mib * 2**10, transcendentals=0)
 
 
 def tangent_first(increment, traj, from_left, from_right):
@@ -481,31 +482,84 @@
     def _():
         sums[...] = jnp.zeros_like(sums)
 
-    for k, (i, j) in enumerate(pairs):
-        product = arrays[i][...] * arrays[j][...]
-        sums[k] = sums[k] + jnp.sum(product.reshape(-1, 8, product.shape[-1]), axis=0)
+    add_products(pairs, arrays, sums)
+
+
+def add_products(pairs, arrays, sums):
+    def step(i, carry):
+        start = pl.multiple_of(i * GROUP, GROUP)
+        parts = [jnp.zeros((GROUP, 2 * LANE), F32)] * len(pairs)
+        for f in range(3):
+            tiles = [a[f, pl.ds(start, GROUP), :] for a in arrays]
+            for k, (one, two) in enumerate(pairs):
+                parts[k] = parts[k] + tiles[one] * tiles[two]
+        return tuple(c + p for c, p in zip(carry, parts))
+
+    begin = tuple(sums[k] for k in range(len(pairs)))
+    for k, value in enumerate(lax.fori_loop(0, arrays[0].shape[1] // GROUP, step, begin)):
+        sums[k] = value
 
 
 def products(pairs, arrays):
     rows = arrays[0].shape[1]
-    block = pl.BlockSpec((3, LANE, 2 * LANE), lambda i: (0, i, 0))
+    block = pl.BlockSpec((3, BLOCK, 2 * LANE), lambda i: (0, i, 0))
+    shape = (len(pairs), GROUP, 2 * LANE)
     return pl.pallas_call(
         functools.partial(products_kernel, pairs),
-        grid=(rows // LANE,),
+        grid=(rows // BLOCK,),
         in_specs=[block] * len(arrays),
-        out_specs=pl.BlockSpec((len(pairs), 8, 2 * LANE), lambda i: (0, 0, 0)),
-        out_shape=jax.ShapeDtypeStruct((len(pairs), 8, 2 * LANE), F32),
+        out_specs=pl.BlockSpec(shape, lambda i: (0, 0, 0)),
+        out_shape=jax.ShapeDtypeStruct(shape, F32),
         compiler_params=PARAMS,
         cost_estimate=cost(3 * len(arrays), 1),
         name="products",
     )(*arrays)
 
 
-def mesh_sums(row):
-    count = lax.axis_size("tm") * lax.axis_size("lon")
-    sent = jnp.broadcast_to(row, (count, 8, LANE))
-    received = lax.all_to_all(sent, ("tm", "lon"), 0, 0)
-    return jnp.sum(received[:, 0, :], axis=0)
+def one_sum(value):
+    return jnp.sum(jnp.sum(value, axis=1, keepdims=True), axis=0, keepdims=True)
+
+
+def last_products_kernel(first, a1, a2, early, d_sums, middle, m1, m2, sent, sums):
+    @pl.when(pl.program_id(0) == 0)
+    def _():
+        sums[...] = jnp.zeros_like(sums)
+
+    add_products(((0, 2), (1, 2), (2, 2)), (first, a1, a2), sums)
+
+    @pl.when(pl.program_id(0) == pl.num_programs(0) - 1)
+    def _():
+        o0, o1, o2 = middle[...], m1[...], m2[...]
+        values = (
+            one_sum(early[0] + early[1]) + one_sum(o0 * o0),
+            one_sum(early[2] + early[3]) + one_sum(o0 * o1),
+            one_sum(sums[0]) + one_sum(d_sums[0]) + one_sum(o0 * o2),
+            one_sum(early[4] + early[5]) + one_sum(o1 * o1),
+            one_sum(sums[1]) + one_sum(d_sums[1]) + one_sum(o1 * o2),
+            one_sum(sums[2]) + one_sum(d_sums[2]) + one_sum(o2 * o2),
+        )
+        lane = iota((8, LANE), 1)
+        row = jnp.zeros((8, LANE), F32)
+        for k, value in enumerate(values):
+            row = jnp.where(lane == k, value, row)
+        for k in range(sent.shape[0]):
+            sent[k] = row
+
+
+def last_products(count, first, a1, a2, early, d_sums, middle, m1, m2):
+    rows = first.shape[1]
+    block = pl.BlockSpec((3, BLOCK, 2 * LANE), lambda i: (0, i, 0))
+    return pl.pallas_call(
+        last_products_kernel,
+        grid=(rows // BLOCK,),
+        in_specs=[block] * 3 + whole(5),
+        out_specs=pl.BlockSpec((count, 8, LANE), lambda i: (0, 0, 0)),
+        out_shape=jax.ShapeDtypeStruct((count, 8, LANE), F32),
+        scratch_shapes=[pltpu.VMEM((3, GROUP, 2 * LANE), F32)],
+        compiler_params=PARAMS,
+        cost_estimate=cost(9, 1),
+        name="last_products",
+    )(first, a1, a2, early, d_sums, middle, m1, m2)
 
 
 def weights(s00, s01, s02, s11, s12, s22):
@@ -532,6 +586,50 @@
     return (y0 / beta - c1 * alpha, c1)
 
 
+def result_kernel(received, last, d1, inc0, inc1, middle, m1, obs_part, multiplier, increment, dual, coefs):
+    @pl.when(pl.program_id(0) == 0)
+    def _():
+        total = jnp.sum(received[...], axis=0)
+        lane = iota((8, LANE), 1)
+        scalars = [
+            jnp.broadcast_to(jnp.sum(jnp.where(lane == k, total, 0.0), axis=1, keepdims=True), (8, LANE))
+            for k in range(6)
+        ]
+        c0, c1 = weights(*scalars)
+        coefs[0] = c0
+        coefs[1] = c1
+        dual[...] = (c0[0:1] * middle[...] + c1[0:1] * m1[...]) / obs_part[...]
+
+    def step(i, carry):
+        start = pl.multiple_of(i * 8, 8)
+        c0, c1 = coefs[0], coefs[1]
+        for f in range(3):
+            for t in range(2):
+                at = (f, pl.ds(start, 8), slice(t * LANE, (t + 1) * LANE))
+                multiplier[at] = c0 * last[at] + c1 * d1[at]
+                increment[at] = c0 * inc0[at] + c1 * inc1[at]
+        return carry
+
+    lax.fori_loop(0, last.shape[1] // 8, step, 0, unroll=4)
+
+
+def result(received, last, d1, inc0, inc1, middle, m1, obs_part):
+    rows = last.shape[1]
+    block = pl.BlockSpec((3, BLOCK, 2 * LANE), lambda i: (0, i, 0))
+    obs = pl.BlockSpec(middle.shape, lambda i: (0, 0))
+    return pl.pallas_call(
+        result_kernel,
+        grid=(rows // BLOCK,),
+        in_specs=whole(1) + [block] * 4 + whole(3),
+        out_specs=[block, block, obs],
+        out_shape=[jax.ShapeDtypeStruct(last.shape, F32)] * 2 + [jax.ShapeDtypeStruct(middle.shape, F32)],
+        scratch_shapes=[pltpu.VMEM((2, 8, LANE), F32)],
+        compiler_params=PARAMS,
+        cost_estimate=cost(18, 1),
+        name="result",
+    )(received, last, d1, inc0, inc1, middle, m1, obs_part)
+
+
 def moved(block, axis, distance, wrap):
     size = lax.axis_size(axis)
     if wrap:
@@ -576,28 +674,12 @@
     m2 = observed(inc1)
     early = products(((0, 0), (1, 1), (0, 2), (1, 3), (2, 2), (3, 3)), (first, last, a1, d1))
     d_sums = adjoint_second(d1_later, d1_later_edges, traj, packed, z1, last, d1)
-    a_sums = products(((0, 2), (1, 2), (2, 2)), (first, a1, a2))
-
-    early = jnp.sum(early, axis=(1, 2))
-    d_sums = jnp.sum(d_sums, axis=(1, 2))
-    a_sums = jnp.sum(a_sums, axis=(1, 2))
-    scalars = jnp.stack(
-        [
-            early[0] + early[1] + jnp.sum(middle * middle),
-            early[2] + early[3] + jnp.sum(middle * m1),
-            d_sums[0] + a_sums[0] + jnp.sum(middle * m2),
-            early[4] + early[5] + jnp.sum(m1 * m1),
-            d_sums[1] + a_sums[1] + jnp.sum(m1 * m2),
-            d_sums[2] + a_sums[2] + jnp.sum(m2 * m2),
-        ]
-    )
-    total = mesh_sums(jnp.pad(scalars, (0, LANE - 6)))
-    c0, c1 = weights(*[total[k] for k in range(6)])
-    return (
-        (c0 * last + c1 * d1)[None],
-        ((c0 * middle + c1 * m1) / obs_part)[None],
-        (c0 * inc0 + c1 * inc1)[None],
-    )
+    count = lax.axis_size("tm") * lax.axis_size("lon")
+    middle, m1, m2, obs_part = (o.reshape(-1, LANE) for o in (middle, m1, m2, obs_part))
+    sent = last_products(count, first, a1, a2, early, d_sums, middle, m1, m2)
+    received = lax.all_to_all(sent, ("tm", "lon"), 0, 0)
+    multiplier, increment, dual = result(received, last, d1, inc0, inc1, middle, m1, obs_part)
+    return (multiplier[None], dual.reshape(1, -1), increment[None])
 
 
 def solution(mesh):

time: 289 us -> 231 us (0.80)
  Pallas kernels: 157 us -> 110 us
  between operations: 21 us -> 0.94 us
  waiting for transfers between devices: 8.8 us -> 26.2 us
  other arithmetic: 24.5 us -> 14.6 us
    ppermute x11, waiting for transfers between devices: 8.8 us -> 26.2 us  [moved(): return lax.ppermute(block, axis, route)]
    pallas_call x1, Pallas kernels: 36 us -> 21.3 us  [adjoint_first(): pl.pallas_call(adjoint_first_kernel, in_specs=whole(7), out_specs=whole(2...]
    pallas_call x1, Pallas kernels: 32.6 us -> 20.4 us  [adjoint_second(): pl.pallas_call(adjoint_second_kernel, in_specs=whole(7), out_specs=pl.Blo...]
    pallas_call x1, Pallas kernels: 29.1 us -> 18 us  [tangent_first(): pl.pallas_call(tangent_first_kernel, in_specs=whole(4), out_specs=whole(4...]
    pallas_call x1, Pallas kernels: 29.1 us -> 18.4 us  [tangent_second(): pl.pallas_call(tangent_second_kernel, in_specs=whole(7), out_specs=whole(...]
    broadcast_in_dim x2 -> x0, other arithmetic: 6.2 us -> none  [the longest x1 4.13 us: shards(): (c0 * last + c1 * d1)[None]]
    gather x2, local copies, waits for them, and re-layouts: 18.7 us -> 24 us  [observed(): return field.reshape(-1)[where]]
    reduce_sum x5 -> x0, other arithmetic: 3.3 us -> none  [the longest x1 0.92 us: shards(): early = jnp.sum(early, axis=(1, 2))]
  transfers between devices with their start and end apart: 11 -> 11, of which waited for: 4 -> 6; matrix products, arithmetic and copies ran while one was open for 18% -> 22% of each run, Pallas kernels for 49% -> 39%
where the time goes in v1:
time: 231 us; the launch traced here: 230 us
  Pallas kernels  110 us (48%)
  local copies, waits for them, and re-layouts  38.9 us (17%)
  starting transfers between devices  26.4 us (11%)
  waiting for transfers between devices  26.2 us (11%)
  other arithmetic  14.6 us (6%)
  blocking collectives  13.1 us (6%)
    ppermute x11, starting transfers between devices, moved(): return lax.ppermute(block, axis, route)  26.4 us
    ppermute x11, waiting for transfers between devices, moved(): return lax.ppermute(block, axis, route)  26.2 us
    gather x2, local copies, waits for them, and re-layouts, observed(): return field.reshape(-1)[where]  24 us
    pallas_call x1, Pallas kernels, adjoint_first(): pl.pallas_call(adjoint_first_kernel, in_specs=whole(7), out_specs=whole(2...  21.3 us
    pallas_call x1, Pallas kernels, adjoint_second(): pl.pallas_call(adjoint_second_kernel, in_specs=whole(7), out_specs=pl.Blo...  20.4 us
    pallas_call x1, Pallas kernels, tangent_second(): pl.pallas_call(tangent_second_kernel, in_specs=whole(7), out_specs=whole(...  18.4 us
    pallas_call x1, Pallas kernels, tangent_first(): pl.pallas_call(tangent_first_kernel, in_specs=whole(4), out_specs=whole(4...  18 us
    scatter-add x2, other arithmetic, spread(): jnp.zeros((3 * rows * columns,), F32).at[where].add(values / obs_part)  14.6 us
  transfers between devices with their start and end apart: 11, of which 6 were waited for; matrix products, arithmetic and copies ran while one was open for 22% of the time, Pallas kernels for 39%

profile of v1, /device:TPU:0, one launch (start us, length us, event | category | flops | bytes accessed | tf_op | source)
XLA Modules:
  0.0 229.9 jit_solution(4256484239323723865)
XLA Ops:
  0.6 7.8 %edges.1 = (f32[64,1024]{1,0:T(8,128)}, f32[64,1024]{1,0:T(8,128)}, f32[3,1024,256]{2,1,0:T(8,128)}) custom-call(f32[3,1024,256]{2,1,0:T(8,128)} %bitcast.30, f32[3,1024,256]{2,1,0:T(8,128)} %bitcast.25, f32[3,1024,256]{2,1,0:T(8,128)} %bitcast.37, bf16[6,1024,256]{2,1,0:T(8,128)(2,1)} %bitcast.20), custom_call_target="tpu_custom_call" | custom-call | flops 2048 | bytes 16384 | tf_op jit(solution)/shard_map/edges/pallas_call | solution.py:88
  8.9 2.9 %collective-permute-start.1 = (f32[64,1024]{1,0:T(8,128)}, f32[64,1024]{1,0:T(8,128)S(1)}, u32[]{:S(2)}, u32[]{:S(2)}) collective-permute-start(f32[64,1024]{1,0:T(8,128)} %get-tuple-element.21), channel_id=1, source_target_pairs={{0,7},{1,0},{2,1},{3,2},{4,3},{5,4},{6,5},{7,6},{8,15},{9,8},{10,9... | collective-permute-start | bytes 786440 | tf_op jit(solution)/shard_map/ppermute | solution.py:639
  13.1 3.1 %collective-permute-done.from_left = f32[64,1024]{1,0:T(8,128)S(1)} collective-permute-done((f32[64,1024]{1,0:T(8,128)}, f32[64,1024]{1,0:T(8,128)S(1)}, u32[]{:S(2)}, u32[]{:S(2)}) %collective-permute-start) | collective-permute-done | bytes 262176 | tf_op jit(solution)/shard_map/ppermute | solution.py:639
  18.5 18.0 %tangent_first.1 = (f32[3,1024,256]{2,1,0:T(8,128)}, f32[24,1024]{1,0:T(8,128)}, f32[1024,128]{1,0:T(8,128)}, f32[24,1024]{1,0:T(8,128)}) custom-call(f32[3,1024,256]{2,1,0:T(8,128)} %get-tuple-element.19.increment.inc0, bf16[6,1024,256]{2,1,0:T(8,128)(2,1)} %bitcast.21, f32[64,1024]{1,0:T(8,128)} %copy-done.3, f32[64,1024]{1,0:T(8,128)} %copy-done.4), custom_call_target="tpu_custom_call" | custom-call | flops 2048 | bytes 10240 | tf_op jit(solution)/shard_map/tangent_first/pallas_call | solution.py:330
  36.5 5.2 %collective-permute-start.2 = (f32[3,1024,256]{2,1,0:T(8,128)}, f32[3,1024,256]{2,1,0:T(8,128)}, u32[]{:S(2)}, u32[]{:S(2)}) collective-permute-start(f32[3,1024,256]{2,1,0:T(8,128)} %get-tuple-element.22), channel_id=1, source_target_pairs={{0,8},{8,16},{16,24},{1,9},{9,17},{17,25},{2,10},{10,18},{18,26},{... | collective-permute-start | bytes 9437192 | tf_op jit(solution)/shard_map/ppermute | solution.py:639
  41.6 3.3 %copy.10 = f32[384,2,8,128]{3,1,2,0:T(2,128)} copy(f32[384,2,8,128]{3,2,1,0:T(8,128)S(1)} %bitcast.33) | data formatting | bytes 6291456
  44.9 13.4 %gather_fusion = f32[1024]{0:T(1024)S(1)} fusion(f32[786432]{0:T(1024)} %bitcast.34, s32[1024]{0:T(1024)S(1)} %broadcast_clamp_fusion), kind=kCustom, calls=%fused_computation | custom fusion | bytes 12288 | tf_op jit(solution)/shard_map/gather | solution.py:649
  58.4 7.7 %scatter_custom_fusion = f32[786432]{0:T(1024)} fusion(s32[1024]{0:T(1024)S(1)} %bitcast.47, f32[1024]{0:T(1024)S(1)} %get-tuple-element.36, f32[]{:T(128)} %constant.0.clone.1), kind=kCustom, calls=%fused_computation.6 | custom fusion | flops 1024 | bytes 3145732 | tf_op jit(solution)/shard_map/scatter-add | solution.py:652
  66.2 4.8 %reshape.59.spread = f32[3,1024,256]{2,1,0:T(8,128)} reshape(f32[786432]{0:T(1024)} %scatter_custom_fusion) | data formatting | bytes 6291456 | tf_op jit(solution)/shard_map/reshape | solution.py:653
  71.0 4.1 %spread_edges.1 = (f32[16,1024]{1,0:T(8,128)}, f32[16,1024]{1,0:T(8,128)}) custom-call(f32[3,1024,256]{2,1,0:T(8,128)} %reshape.59.spread), custom_call_target="tpu_custom_call" | custom-call | flops 2048 | bytes 3072 | tf_op jit(solution)/shard_map/spread_edges/pallas_call | solution.py:109
  78.2 4.6 %collective-permute-start.3 = (f32[24,1024]{1,0:T(8,128)S(1)}, f32[24,1024]{1,0:T(8,128)S(1)}, u32[]{:S(2)}, u32[]{:S(2)}) collective-permute-start(f32[24,1024]{1,0:T(8,128)S(1)} %copy-done.15), channel_id=1, source_target_pairs={{0,8},{8,16},{16,24},{1,9},{9,17},{17,25},{2,10},{10,18},{18,26},{... | collective-permute-start | bytes 294920 | tf_op jit(solution)/shard_map/ppermute | solution.py:639
  83.1 2.2 collective-permute-done.7.z_right
  86.1 21.3 %adjoint_first.1 = (f32[3,1024,256]{2,1,0:T(8,128)}, f32[24,1024]{1,0:T(8,128)}) custom-call(f32[3,1024,256]{2,1,0:T(8,128)} %collective-permute-done.4.later, f32[24,1024]{1,0:T(8,128)} %copy-done.7, bf16[6,1024,256]{2,1,0:T(8,128)(2,1)} %bitcast.22, f32[1024,128]{1,0:T(8,128)} %get-tuple-element.25.packed, f32[3,1024,256]{2,1,0:T(8,128)} %reshape.59.spread, ...), custom_call_target="tpu_custom_call" | custom-call | flops 2048 | bytes 13312 | tf_op jit(solution)/shard_map/adjoint_first/pallas_call | solution.py:379
  110.3 18.4 %tangent_second.1 = (f32[3,1024,256]{2,1,0:T(8,128)}, f32[3,1024,256]{2,1,0:T(8,128)}) custom-call(f32[3,1024,256]{2,1,0:T(8,128)} %collective-permute-done.2.earlier.refs_2_.a1, f32[24,1024]{1,0:T(8,128)} %copy-done.5, f32[3,1024,256]{2,1,0:T(8,128)} %get-tuple-element.28.pulled.refs_3_.d1, f32[24,1024]{1,0:T(8,128)} %get-tuple-element.29.pulled_edges, ...), custom_call_target="tpu_custom_call" | custom-call | flops 2048 | bytes 18432 | tf_op jit(solution)/shard_map/tangent_second/pallas_call | solution.py:425
  128.7 6.0 %collective-permute-start.8 = (f32[3,1024,256]{2,1,0:T(8,128)}, f32[3,1024,256]{2,1,0:T(8,128)}, u32[]{:S(2)}, u32[]{:S(2)}) collective-permute-start(f32[3,1024,256]{2,1,0:T(8,128)} %get-tuple-element.30), channel_id=1, source_target_pairs={{0,8},{8,16},{16,24},{1,9},{9,17},{17,25},{2,10},{10,18},{18,26},{... | collective-permute-start | bytes 9437192 | tf_op jit(solution)/shard_map/ppermute | solution.py:639
  136.0 6.9 %scatter_custom_fusion.1 = f32[786432]{0:T(1024)S(1)} fusion(s32[1024]{0:T(1024)S(1)} %bitcast.48, f32[1024]{0:T(1024)S(1)} %get-tuple-element.35, f32[]{:T(128)} %constant.0.clone.1), kind=kCustom, calls=%fused_computation.4 | custom fusion | flops 1024 | bytes 3145732 | tf_op jit(solution)/shard_map/scatter-add | solution.py:652
  142.9 2.5 %reshape.61.spread = f32[3,1024,256]{2,1,0:T(8,128)} reshape(f32[786432]{0:T(1024)S(1)} %scatter_custom_fusion.1) | data formatting | bytes 6291456 | tf_op jit(solution)/shard_map/reshape | solution.py:653
  145.5 6.6 %products.1.early = f32[6,16,256]{2,1,0:T(8,128)} custom-call(f32[3,1024,256]{2,1,0:T(8,128)} %bitcast.31, f32[3,1024,256]{2,1,0:T(8,128)} %bitcast.26, f32[3,1024,256]{2,1,0:T(8,128)} %collective-permute-done.2.earlier.refs_2_.a1, f32[3,1024,256]{2,1,0:T(8,128)} %get-tuple-element.28.pulled.refs_3_.d1), custom_call_target="tpu_custom_call" | custom-call | flops 1024 | bytes 12288 | tf_op jit(solution)/shard_map/products/pallas_call | solution.py:507
  153.6 10.5 %gather_fusion.1 = f32[1024]{0:T(1024)} fusion(f32[786432]{0:T(1024)S(1)} %bitcast.35, s32[1024]{0:T(1024)S(1)} %broadcast_clamp_fusion), kind=kCustom, calls=%fused_computation.1 | custom fusion | bytes 12288 | tf_op jit(solution)/shard_map/gather | solution.py:649
  164.2 18.1 %collective-permute-done.10.later_edges = f32[24,1024]{1,0:T(8,128)S(1)} collective-permute-done((f32[24,1024]{1,0:T(8,128)S(1)}, f32[24,1024]{1,0:T(8,128)S(1)}, u32[]{:S(2)}, u32[]{:S(2)}) %collective-permute-start.10) | collective-permute-done | bytes 98336 | tf_op jit(solution)/shard_map/ppermute | solution.py:639
  182.9 20.4 %adjoint_second.1.d_sums = f32[3,16,128]{2,1,0:T(8,128)} custom-call(f32[3,1024,256]{2,1,0:T(8,128)} %collective-permute-done.9.later, f32[24,1024]{1,0:T(8,128)} %copy-done.8, bf16[6,1024,256]{2,1,0:T(8,128)(2,1)} %bitcast.24, f32[1024,128]{1,0:T(8,128)} %get-tuple-element.25.packed, f32[3,1024,256]{2,1,0:T(8,128)} %reshape.61.spread, ...), custom_call_target="tpu_custom_call" | custom-call | flops 2048 | bytes 16384 | tf_op jit(solution)/shard_map/adjoint_second/pallas_call | solution.py:466
  203.3 5.5 %last_products.1 = f32[32,8,128]{2,1,0:T(8,128)} custom-call(f32[3,1024,256]{2,1,0:T(8,128)} %bitcast.32, f32[3,1024,256]{2,1,0:T(8,128)} %collective-permute-done.2.earlier.refs_2_.a1, f32[3,1024,256]{2,1,0:T(8,128)} %collective-permute-done.8.a2, f32[6,16,256]{2,1,0:T(8,128)} %products.1.early, f32[3,16,128]{2,1,0:T(8,128)} %adjoint_second.1.d_sums, ...), custom_call_target="tpu_custom_call" | custom-call | flops 1024 | bytes 9216 | tf_op jit(solution)/shard_map/last_products/pallas_call | solution.py:552
  208.9 13.1 %all_to_all.5.received = f32[32,8,128]{2,1,0:T(8,128)} all-to-all(f32[32,8,128]{2,1,0:T(8,128)} %last_products.1), channel_id=1, replica_groups=mesh['tm'=4,'lon'=8] {'tm','lon'}, dimensions={0} | all-to-all | bytes 262144 | tf_op jit(solution)/shard_map/all_to_all | solution.py:680
  222.0 7.8 %result.1 = (f32[3,1024,256]{2,1,0:T(8,128)}, f32[3,1024,256]{2,1,0:T(8,128)}, f32[8,128]{1,0:T(8,128)}) custom-call(f32[32,8,128]{2,1,0:T(8,128)} %all_to_all.5.received, f32[3,1024,256]{2,1,0:T(8,128)} %bitcast.28, f32[3,1024,256]{2,1,0:T(8,128)} %get-tuple-element.28.pulled.refs_3_.d1, f32[3,1024,256]{2,1,0:T(8,128)} %get-tuple-element.19.increment.inc0, ...), custom_call_target="tpu_custom_call" | custom-call | flops 1024 | bytes 18432 | tf_op jit(solution)/shard_map/result/pallas_call | solution.py:620
  (53 shorter events, 14.7 us)
Async XLA Ops:
  0.6 11.2 %copy-start = (f32[1,3,1024,256]{3,2,1,0:T(8,128)S(1)}, f32[1,3,1024,256]{3,2,1,0:T(8,128)}, u32[]{:S(2)}) copy-start(f32[1,3,1024,256]{3,2,1,0:T(8,128)} %param.13) | copy-start | bytes 9437188
  8.4 7.7 %collective-permute-start = (f32[64,1024]{1,0:T(8,128)}, f32[64,1024]{1,0:T(8,128)S(1)}, u32[]{:S(2)}, u32[]{:S(2)}) collective-permute-start(f32[64,1024]{1,0:T(8,128)} %get-tuple-element.20), channel_id=1, source_target_pairs={{0,1},{1,2},{2,3},{3,4},{4,5},{5,6},{6,7},{7,0},{8,9},{9,10},{10,1... | collective-permute-start | bytes 786440 | tf_op jit(solution)/shard_map/ppermute | solution.py:639
  8.9 8.9 %collective-permute-start.1 = (f32[64,1024]{1,0:T(8,128)}, f32[64,1024]{1,0:T(8,128)S(1)}, u32[]{:S(2)}, u32[]{:S(2)}) collective-permute-start(f32[64,1024]{1,0:T(8,128)} %get-tuple-element.21), channel_id=1, source_target_pairs={{0,7},{1,0},{2,1},{3,2},{4,3},{5,4},{6,5},{7,6},{8,15},{9,8},{10,9... | collective-permute-start | bytes 786440 | tf_op jit(solution)/shard_map/ppermute | solution.py:639
  11.8 73.7 %collective-permute-start.4 = (f32[3,1024,256]{2,1,0:T(8,128)S(1)}, f32[3,1024,256]{2,1,0:T(8,128)}, u32[]{:S(2)}, u32[]{:S(2)}) collective-permute-start(f32[3,1024,256]{2,1,0:T(8,128)S(1)} %bitcast.29), channel_id=1, source_target_pairs={{8,0},{16,8},{24,16},{9,1},{17,9},{25,17},{10,2},{18,10},{26,18},{... | collective-permute-start | bytes 9437192 | tf_op jit(solution)/shard_map/ppermute | solution.py:639
  16.2 1.6 copy-start.3
  17.8 0.7 copy-start.4
  18.5 23.1 %copy-start.1 = (f32[3,1024,256]{2,1,0:T(8,128)S(1)}, f32[3,1024,256]{2,1,0:T(8,128)}, u32[]{:S(2)}) copy-start(f32[3,1024,256]{2,1,0:T(8,128)} %get-tuple-element.19.increment.inc0) | copy-start | bytes 9437188
  36.5 73.2 %collective-permute-start.2 = (f32[3,1024,256]{2,1,0:T(8,128)}, f32[3,1024,256]{2,1,0:T(8,128)}, u32[]{:S(2)}, u32[]{:S(2)}) collective-permute-start(f32[3,1024,256]{2,1,0:T(8,128)} %get-tuple-element.22), channel_id=1, source_target_pairs={{0,8},{8,16},{16,24},{1,9},{9,17},{17,25},{2,10},{10,18},{18,26},{... | collective-permute-start | bytes 9437192 | tf_op jit(solution)/shard_map/ppermute | solution.py:639
  41.6 3.3 %copy-start.14 = (s32[1,1024]{1,0:T(1,128)S(1)}, s32[1,1024]{1,0:T(1,128)}, u32[]{:S(2)}) copy-start(s32[1,1024]{1,0:T(1,128)} %param.12) | copy-start | bytes 12292
  44.9 13.5 %copy-start.12 = (f32[1,1024]{1,0:T(1,128)S(1)}, f32[1,1024]{1,0:T(1,128)}, u32[]{:S(2)}) copy-start(f32[1,1024]{1,0:T(1,128)} %param.8) | copy-start | bytes 12292
  44.9 13.5 %copy-start.13 = (f32[1,1024]{1,0:T(1,128)S(1)}, f32[1,1024]{1,0:T(1,128)}, u32[]{:S(2)}) copy-start(f32[1,1024]{1,0:T(1,128)} %param.11) | copy-start | bytes 12292
  58.4 12.6 %copy-start.9 = (f32[1024]{0:T(1024)}, f32[1024]{0:T(1024)S(1)}, u32[]{:S(2)}) copy-start(f32[1024]{0:T(1024)S(1)} %gather_fusion) | copy-start | bytes 12292
  71.0 5.9 %copy-start.16 = (f32[24,1024]{1,0:T(8,128)S(1)}, f32[24,1024]{1,0:T(8,128)}, u32[]{:S(2)}) copy-start(f32[24,1024]{1,0:T(8,128)} %get-tuple-element.24) | copy-start | bytes 294916
  71.0 7.1 %copy-start.15 = (f32[24,1024]{1,0:T(8,128)S(1)}, f32[24,1024]{1,0:T(8,128)}, u32[]{:S(2)}) copy-start(f32[24,1024]{1,0:T(8,128)} %get-tuple-element.23) | copy-start | bytes 294916
  75.1 7.6 %collective-permute-start.6 = (f32[16,1024]{1,0:T(8,128)}, f32[16,1024]{1,0:T(8,128)S(1)}, u32[]{:S(2)}, u32[]{:S(2)}) collective-permute-start(f32[16,1024]{1,0:T(8,128)} %get-tuple-element.26), channel_id=1, source_target_pairs={{0,1},{1,2},{2,3},{3,4},{4,5},{5,6},{6,7},{7,0},{8,9},{9,10},{10,1... | collective-permute-start | bytes 196616 | tf_op jit(solution)/shard_map/ppermute | solution.py:639
  76.9 8.6 %collective-permute-start.5 = (f32[24,1024]{1,0:T(8,128)S(1)}, f32[24,1024]{1,0:T(8,128)S(1)}, u32[]{:S(2)}, u32[]{:S(2)}) collective-permute-start(f32[24,1024]{1,0:T(8,128)S(1)} %copy-done.16), channel_id=1, source_target_pairs={{8,0},{16,8},{24,16},{9,1},{17,9},{25,17},{10,2},{18,10},{26,18},{... | collective-permute-start | bytes 294920 | tf_op jit(solution)/shard_map/ppermute | solution.py:639
  78.2 31.5 %collective-permute-start.3 = (f32[24,1024]{1,0:T(8,128)S(1)}, f32[24,1024]{1,0:T(8,128)S(1)}, u32[]{:S(2)}, u32[]{:S(2)}) collective-permute-start(f32[24,1024]{1,0:T(8,128)S(1)} %copy-done.15), channel_id=1, source_target_pairs={{0,8},{8,16},{16,24},{1,9},{9,17},{17,25},{2,10},{10,18},{18,26},{... | collective-permute-start | bytes 294920 | tf_op jit(solution)/shard_map/ppermute | solution.py:639
  82.7 2.8 %copy-start.10 = (f32[16,1024]{1,0:T(8,128)}, f32[16,1024]{1,0:T(8,128)S(1)}, u32[]{:S(2)}) copy-start(f32[16,1024]{1,0:T(8,128)S(1)} %collective-permute-done.6.z_left) | copy-start | bytes 196612
  82.7 2.6 %collective-permute-start.7 = (f32[16,1024]{1,0:T(8,128)}, f32[16,1024]{1,0:T(8,128)S(1)}, u32[]{:S(2)}, u32[]{:S(2)}) collective-permute-start(f32[16,1024]{1,0:T(8,128)} %get-tuple-element.27), channel_id=1, source_target_pairs={{0,7},{1,0},{2,1},{3,2},{4,3},{5,4},{6,5},{7,6},{8,15},{9,8},{10,9... | collective-permute-start | bytes 196616 | tf_op jit(solution)/shard_map/ppermute | solution.py:639
  107.4 74.9 %collective-permute-start.9 = (f32[3,1024,256]{2,1,0:T(8,128)}, f32[3,1024,256]{2,1,0:T(8,128)}, u32[]{:S(2)}, u32[]{:S(2)}) collective-permute-start(f32[3,1024,256]{2,1,0:T(8,128)} %get-tuple-element.28.pulled.refs_3_.d1), channel_id=1, source_target_pairs={{8,0},{16,8},{24,16},{9,1},{17,9},{25,17},{10,2},{18,10},{26,18},{... | collective-permute-start | bytes 9437192 | tf_op jit(solution)/shard_map/ppermute | solution.py:639
  110.3 24.5 %copy-start.6 = (f32[24,1024]{1,0:T(8,128)S(1)}, f32[24,1024]{1,0:T(8,128)}, u32[]{:S(2)}) copy-start(f32[24,1024]{1,0:T(8,128)} %get-tuple-element.29.pulled_edges) | copy-start | bytes 294916
  128.7 74.6 %collective-permute-start.8 = (f32[3,1024,256]{2,1,0:T(8,128)}, f32[3,1024,256]{2,1,0:T(8,128)}, u32[]{:S(2)}, u32[]{:S(2)}) collective-permute-start(f32[3,1024,256]{2,1,0:T(8,128)} %get-tuple-element.30), channel_id=1, source_target_pairs={{0,8},{8,16},{16,24},{1,9},{9,17},{17,25},{2,10},{10,18},{18,26},{... | collective-permute-start | bytes 9437192 | tf_op jit(solution)/shard_map/ppermute | solution.py:639
  134.7 47.6 %collective-permute-start.10 = (f32[24,1024]{1,0:T(8,128)S(1)}, f32[24,1024]{1,0:T(8,128)S(1)}, u32[]{:S(2)}, u32[]{:S(2)}) collective-permute-start(f32[24,1024]{1,0:T(8,128)S(1)} %copy-done.6), channel_id=1, source_target_pairs={{8,0},{16,8},{24,16},{9,1},{17,9},{25,17},{10,2},{18,10},{26,18},{... | collective-permute-start | bytes 294920 | tf_op jit(solution)/shard_map/ppermute | solution.py:639
  145.5 6.6 %copy-start.2 = (f32[3,1024,256]{2,1,0:T(8,128)S(1)}, f32[3,1024,256]{2,1,0:T(8,128)}, u32[]{:S(2)}) copy-start(f32[3,1024,256]{2,1,0:T(8,128)} %get-tuple-element.31.inc1) | copy-start | bytes 9437188
  (4 other events, 2.5 us)

commit v2 on v1

v2 whole, which is shorter than its diff:
```python
import jax
import jax.numpy as jnp
from jax import lax
from jax.experimental import pallas as pl
from jax.experimental.pallas import tpu as pltpu
from jax.sharding import PartitionSpec as P

courant = 0.25
coriolis = 0.2
slope = 0.5 * courant

LANE = 128
BLOCK = 256
GROUP = 16
MARGIN = 8
HALO = 4
TRAJ, INC, VAR, LAST, PLANES = 0, 6, 9, 12, 16
F32 = jnp.float32
PARAMS = pltpu.CompilerParams(vmem_limit_bytes=56 * 1024 * 1024)


def iota(shape, dim):
    return lax.broadcasted_iota(jnp.int32, shape, dim)


def spread_shift(plane):
    return (LANE - (8 * plane + HALO)) % LANE


def pack_shift(plane):
    return (8 * plane + HALO) % LANE


def edges_of(planes, rows):
    lane = iota((rows, LANE), 1)
    packed = jnp.zeros((rows, LANE), F32)
    for number, plane in enumerate(planes):
        both = jnp.where(lane < LANE // 2, plane[:, :LANE], plane[:, LANE:])
        packed = jnp.where((lane >= 8 * number) & (lane < 8 * number + 8), pltpu.roll(both, pack_shift(number), 1), packed)
    return packed


def split_edges(turned, to_right, to_left, count):
    top = iota((8, turned.shape[1]), 0) < HALO
    for pair in range(count // 2):
        even = turned[16 * pair : 16 * pair + 8]
        odd = turned[16 * pair + 8 : 16 * pair + 16]
        to_right[8 * pair : 8 * pair + 8, :] = jnp.where(top, even, pltpu.roll(odd, HALO, 0))
        to_left[8 * pair : 8 * pair + 8, :] = jnp.where(top, pltpu.roll(even, HALO, 0), odd)


def joined_edges(from_left, from_right, count):
    top = iota((8, from_left.shape[1]), 0) < HALO
    pieces = []
    for pair in range(count // 2):
        left = from_left[8 * pair : 8 * pair + 8]
        right = from_right[8 * pair : 8 * pair + 8]
        pieces.append(jnp.where(top, left, pltpu.roll(right, HALO, 0)))
        pieces.append(jnp.where(top, pltpu.roll(left, HALO, 0), right))
    return jnp.concatenate(pieces, axis=0)


def padded_turn(message):
    rest = LANE - message.shape[0]
    if rest:
        message = jnp.concatenate([message, jnp.zeros((rest, message.shape[1]), F32)], axis=0)
    return message.T


def edges_kernel(first, last, variance, traj, to_right, to_left, increment):
    rows = first.shape[1]
    planes = [traj[p].astype(F32) for p in range(6)]
    for f in range(3):
        value = first[f] - variance[f] * last[f]
        increment[f] = value
        planes.append(value)
    planes += [variance[f] for f in range(3)]
    planes += [last[f] for f in range(3)]
    split_edges(edges_of(planes, rows).T, to_right, to_left, PLANES)


def edges_call(first, last, variance, traj):
    rows = first.shape[1]
    block = pl.BlockSpec((3, BLOCK, 2 * LANE), lambda i: (0, i, 0))
    sent = pl.BlockSpec((PLANES * HALO, BLOCK), lambda i: (0, i))
    return pl.pallas_call(
        edges_kernel,
        grid=(rows // BLOCK,),
        in_specs=[block, block, block, pl.BlockSpec((6, BLOCK, 2 * LANE), lambda i: (0, i, 0))],
        out_specs=[sent, sent, block],
        out_shape=[jax.ShapeDtypeStruct((PLANES * HALO, rows), F32)] * 2
        + [jax.ShapeDtypeStruct(first.shape, F32)],
        compiler_params=PARAMS,
        cost_estimate=cost(16),
        name="edges",
    )(first, last, variance, traj)


def spread_edges_kernel(spread, to_right, to_left):
    planes = [spread[f] for f in range(3)]
    split_edges(edges_of(planes, spread.shape[1]).T, to_right, to_left, 4)


def spread_edges_call(spread):
    rows = spread.shape[1]
    sent = pl.BlockSpec((16, BLOCK), lambda i: (0, i))
    return pl.pallas_call(
        spread_edges_kernel,
        grid=(rows // BLOCK,),
        in_specs=[pl.BlockSpec((3, BLOCK, 2 * LANE), lambda i: (0, i, 0))],
        out_specs=[sent, sent],
        out_shape=[jax.ShapeDtypeStruct((16, rows), F32)] * 2,
        compiler_params=PARAMS,
        cost_estimate=cost(3),
        name="spread_edges",
    )(spread)


def x_differences(tiles, first_lane, last_lane):
    ahead = [pltpu.roll(t, LANE - 1, 1) for t in tiles]
    behind = [pltpu.roll(t, 1, 1) for t in tiles]
    return [
        jnp.where(last_lane, ahead[(t + 1) % 3], ahead[t])
        - jnp.where(first_lane, behind[(t - 1) % 3], behind[t])
        for t in range(3)
    ]


def rotation_at(start, total):
    position = (iota((GROUP, LANE), 0) + start).astype(F32)
    return coriolis * ((2.0 * position + 1.0) / total - 1.0)


def lane_ends():
    lane = iota((GROUP, LANE), 1)
    return lane == 0, lane == LANE - 1


def rows_at(start, offset=0):
    return pl.ds(pl.multiple_of(start + offset, GROUP), GROUP)


def traj_tiles(traj, traj_halo, step, start):
    out = []
    for plane in range(3 * step, 3 * step + 3):
        tiles = [traj[plane, rows_at(start), t * LANE : (t + 1) * LANE] for t in range(2)]
        out.append([t.astype(F32) for t in tiles + [traj_halo[plane, rows_at(start), :]]])
    return out


def load_rows(ref, start, offset):
    return [[ref[f, t, pl.ds(start + (MARGIN + offset), GROUP), :] for t in range(3)] for f in range(3)]


def store_rows(ref, start, value):
    for f in range(3):
        for t in range(3):
            ref[f, t, pl.ds(start + MARGIN, GROUP), :] = value[f][t]


def clear_margins(ref):
    rows = ref.shape[2]
    zero = jnp.zeros((MARGIN, LANE), F32)
    for f in range(3):
        for t in range(3):
            ref[f, t, 0:MARGIN, :] = zero
            ref[f, t, rows - MARGIN : rows, :] = zero


def tangent_rows(source, traj, traj_halo, step, start, total):
    here, above, below = (load_rows(source, start, k) for k in (0, 1, -1))
    trajectory = traj_tiles(traj, traj_halo, step, start)
    turn = rotation_at(start, total)
    ends = lane_ends()
    dx = [x_differences(here[f], *ends) for f in range(3)]
    new = [[], [], []]
    for t in range(3):
        b, e, n = (trajectory[f][t] for f in range(3))
        h, u, v = (here[f][t] for f in range(3))
        xh, xu, xv = (dx[f][t] for f in range(3))
        yh, yu, yv = (above[f][t] - below[f][t] for f in range(3))
        new[0].append(h - slope * (b * (xu + yv) + e * xh + n * yh))
        new[1].append(u - slope * (xh + e * xu + n * yu) + turn * v)
        new[2].append(v - slope * (yh + e * xv + n * yv) - turn * u)
    return new


def north_rows(field, trajectory):
    out = [[], [], []]
    for t in range(3):
        b, _, n = (trajectory[f][t] for f in range(3))
        p, q, w = (field[f][t] for f in range(3))
        out[0].append(n * p + w)
        out[1].append(n * q)
        out[2].append(b * p + n * w)
    return out


def adjoint_rows(source, flux, traj, traj_halo, step, start, total):
    here = load_rows(source, start, 0)
    above, below = (load_rows(flux, start, k) for k in (1, -1))
    trajectory = traj_tiles(traj, traj_halo, step, start)
    turn = rotation_at(start, total)
    ends = lane_ends()
    east = [[], [], []]
    for t in range(3):
        b, e, _ = (trajectory[f][t] for f in range(3))
        p, q, w = (here[f][t] for f in range(3))
        east[0].append(e * p + q)
        east[1].append(b * p + e * q)
        east[2].append(e * w)
    dx = [x_differences(east[f], *ends) for f in range(3)]
    new = [[], [], []]
    for t in range(3):
        p, q, w = (here[f][t] for f in range(3))
        change = [slope * (dx[f][t] + (above[f][t] - below[f][t])) for f in range(3)]
        new[0].append(p + change[0])
        new[1].append(q + change[1] - turn * w)
        new[2].append(w + change[2] + turn * q)
    return new


def over_rows(begin, end, body):
    count = (end - begin) // GROUP
    unroll = next(u for u in (8, 6, 5, 4, 3, 2, 1) if count % u == 0)

    def step(i, carry):
        body(pl.multiple_of(begin + i * GROUP, GROUP))
        return carry

    lax.fori_loop(0, count, step, 0, unroll=unroll)


def padded(rows):
    return -(-rows // (2 * LANE)) * 2 * LANE


def extra(rows):
    return 8 * padded(rows) // (2 * LANE)


def turn_in(message, packed_ref):
    for j in range(message.shape[1] // LANE):
        packed_ref[j * LANE : (j + 1) * LANE, :] = padded_turn(message[:, j * LANE : (j + 1) * LANE])


def unfold_in(folded, packed_ref):
    for j in range(packed_ref.shape[0] // LANE):
        at = (slice(j // 2 * 8, j // 2 * 8 + 8), slice(j % 2 * LANE, (j % 2 + 1) * LANE))
        message = jnp.concatenate([folded[(f,) + at] for f in range(3)], axis=0)
        packed_ref[j * LANE : (j + 1) * LANE, :] = padded_turn(message)


def turn_out(halo, payload, behind):
    low = iota((8, LANE), 0) < HALO
    for j in range(halo.shape[1] // LANE):
        for f in range(3):
            turned = halo[f, j * LANE : (j + 1) * LANE, :].T
            ends = jnp.where(low, turned[:8], turned[LANE - 8 :])
            row = behind + j // 2 * 8
            payload[f, row : row + 8, j % 2 * LANE : (j % 2 + 1) * LANE] = pltpu.roll(ends, HALO, 0)


def wide_scratch(rows):
    return pltpu.VMEM((3, 3, rows + 2 * MARGIN, LANE), F32)


def tile_of(ref, f, start, t, offset=0):
    return ref[f, rows_at(start, offset), t * LANE : (t + 1) * LANE]


def set_tile(ref, f, start, t, value, offset=0):
    ref[f, rows_at(start, offset), t * LANE : (t + 1) * LANE] = value


class Copies:
    def __init__(self, sems):
        self.sems, self.used = sems, 0

    def rows(self, parts, begin, end, target):
        started = []
        for ref, at, count in parts:
            low, high = max(begin, at), min(end, at + count)
            if low < high:
                source = ref.at[..., low - at : high - at, :]
                goal = target.at[..., low - begin : high - begin, :]
                copy = pltpu.make_async_copy(source, goal, self.sems.at[self.used])
                self.used += 1
                copy.start()
                started.append(copy)
        return started


def placed(refs, parts):
    return [(ref, at, count) for ref, (_, at, count) in zip(refs, parts)]


def wait(copies):
    for copy in copies:
        copy.wait()


def segments(total):
    return [(at, min(at + BLOCK, total)) for at in range(0, total, BLOCK)]


def fetch(copies, total, *pairs):
    return [
        [copy for source, target in pairs for copy in copies.rows([(source, 0, total)], low, high, target.at[..., low:high, :])]
        for low, high in segments(total)
    ]


def run_tangent(total, get, ready, traj, traj_halo, wide_a, wide_b, traj_ready, put, done):
    clear_margins(wide_a)
    clear_margins(wide_b)
    for (low, high), copies in zip(segments(total), ready):
        wait(copies)
        over_rows(low, high, lambda s: store_rows(wide_a, s, get(s)))
    for (low, high), copies in zip(segments(total), traj_ready):
        wait(copies)
        over_rows(low, high, lambda s: store_rows(wide_b, s, tangent_rows(wide_a, traj, traj_halo, 0, s, total)))
    for low, high in segments(total):
        over_rows(low, high, lambda s: put(s, tangent_rows(wide_b, traj, traj_halo, 1, s, total)))
        done(low, high)


def run_adjoint(total, get, ready, traj, traj_halo, wide_a, wide_b, flux_a, flux_b, put, begin_put, done):
    clear_margins(flux_a)
    clear_margins(flux_b)

    def begin(s):
        field = get(s)
        store_rows(wide_a, s, field)
        store_rows(flux_a, s, north_rows(field, traj_tiles(traj, traj_halo, 1, s)))

    def middle(s):
        field = adjoint_rows(wide_a, flux_a, traj, traj_halo, 1, s, total)
        store_rows(wide_b, s, field)
        store_rows(flux_b, s, north_rows(field, traj_tiles(traj, traj_halo, 0, s)))

    for (low, high), copies in zip(segments(total), ready):
        wait(copies)
        over_rows(low, high, begin)
    over_rows(0, total, middle)
    for (low, high), copies in zip(segments(total), begin_put):
        wait(copies)
        over_rows(low, high, lambda s: put(s, adjoint_rows(wide_b, flux_b, traj, traj_halo, 0, s, total)))
        done(low, high)


def halo_of(lanes, plane):
    return pltpu.roll(lanes, spread_shift(plane), 1)


ANY = pl.BlockSpec(memory_space=pl.ANY)


def whole(count):
    return [pl.BlockSpec(memory_space=pltpu.VMEM)] * count


def cost(mib, steps=2):
    return pl.CostEstimate(flops=2**10, bytes_accessed=mib * 2**20, transcendentals=0)


def f32(*shape):
    return jax.ShapeDtypeStruct(shape, F32)


def vmem(*shape, dtype=F32):
    return pltpu.VMEM(shape, dtype)


def call(name, kernel, ins, outs, scratch, mib, *args, first_any=False, outs_any=False):
    specs = [ANY if outs_any or (first_any and k == 0) else whole(1)[0] for k in range(len(outs))]
    return pl.pallas_call(
        kernel,
        in_specs=ins,
        out_specs=specs,
        out_shape=outs,
        scratch_shapes=scratch,
        compiler_params=PARAMS,
        cost_estimate=cost(mib),
        name=name,
    )(*args)


def tangent_first(increment, traj, from_left, from_right):
    _, total, columns = increment.shape

    def kernel(inc_in, traj_in, from_left, from_right, ahead, traj_halo, var_halo, last_edges, inc, traj, wide_a, wide_b, halo, out, sems):
        copies = Copies(sems)
        ready = fetch(copies, total, (inc_in, inc))
        traj_ready = fetch(copies, total, (traj_in, traj))
        for j in range(total // LANE):
            cut = slice(j * LANE, (j + 1) * LANE)
            joined = joined_edges(from_left[:, cut], from_right[:, cut], PLANES)
            last_edges[:, cut] = joined[8 * LAST : 8 * LAST + 24]
            packed = joined.T
            for plane in range(6):
                traj_halo[plane, cut, :] = halo_of(packed, TRAJ + plane).astype(traj_halo.dtype)
            for f in range(3):
                var_halo[f, cut, :] = halo_of(packed, VAR + f)
                halo[f, cut, :] = halo_of(packed, INC + f)

        def get(s):
            return [[tile_of(inc, f, s, t) for t in range(2)] + [halo[f, rows_at(s), :]] for f in range(3)]

        def put(s, new):
            for f in range(3):
                for t in range(2):
                    set_tile(out, f, s, t, -new[f][t])
                halo[f, rows_at(s), :] = -new[f][2]

        leaving = []

        def done(low, high):
            leaving.extend(copies.rows([(out, 0, total)], low, high, ahead.at[:, low:high, :]))

        run_tangent(total, get, ready, traj, traj_halo, wide_a, wide_b, traj_ready, put, done)
        turn_out(halo, out, total)
        end = total + extra(total)
        leaving.extend(copies.rows([(out, 0, end)], total, end, ahead.at[:, total:end, :]))
        wait(leaving)

    outs = [f32(3, total + extra(total), columns), jax.ShapeDtypeStruct((6, total, LANE), traj.dtype)]
    outs += [f32(3, total, LANE), f32(24, total)]
    scratch = [vmem(*increment.shape), vmem(*traj.shape, dtype=traj.dtype)] + [wide_scratch(total)] * 2
    scratch += [vmem(3, total, LANE), vmem(3, total + extra(total), columns)]
    scratch += [pltpu.SemaphoreType.DMA((3 * len(segments(total)) + 1,))]
    return call(
        "tangent_first", kernel, [ANY, ANY] + whole(2), outs, scratch, 10, increment, traj, from_left, from_right, first_any=True
    )


def adjoint_first(later, later_edges, traj, traj_halo, spread, z_left, z_right):
    _, total, columns = later.shape

    def kernel(later_in, traj_in, traj_halo_in, spread_in, later_edges, z_left, z_right, pulled, later, traj, traj_halo, spread,
               wide_a, wide_b, flux_a, flux_b, own, z_own, halo, out, sems):
        copies = Copies(sems)
        ready = fetch(copies, total, (later_in, later), (traj_in, traj), (traj_halo_in, traj_halo))
        begin_put = fetch(copies, total, (spread_in, spread))
        turn_in(later_edges, own)
        for j in range(total // LANE):
            cut = slice(j * LANE, (j + 1) * LANE)
            z_own[cut, :] = padded_turn(joined_edges(z_left[:, cut], z_right[:, cut], 4))

        def get(s):
            lanes = own[rows_at(s), :]
            return [[tile_of(later, f, s, t) for t in range(2)] + [halo_of(lanes, f)] for f in range(3)]

        def put(s, new):
            lanes = z_own[rows_at(s), :]
            for f in range(3):
                for t in range(2):
                    set_tile(out, f, s, t, tile_of(spread, f, s, t) - new[f][t])
                halo[f, rows_at(s), :] = halo_of(lanes, f) - new[f][2]

        leaving = []

        def done(low, high):
            leaving.extend(copies.rows([(out, 0, total)], low, high, pulled.at[:, low:high, :]))

        run_adjoint(total, get, ready, traj, traj_halo, wide_a, wide_b, flux_a, flux_b, put, begin_put, done)
        turn_out(halo, out, total)
        end = total + extra(total)
        leaving.extend(copies.rows([(out, 0, end)], total, end, pulled.at[:, total:end, :]))
        wait(leaving)

    outs = [f32(3, total + extra(total), columns)]
    scratch = [vmem(3, total, columns), vmem(6, total, columns, dtype=traj.dtype), vmem(6, total, LANE, dtype=traj.dtype)]
    scratch += [vmem(3, total, columns)] + [wide_scratch(total)] * 4 + [vmem(total, LANE)] * 2
    scratch += [vmem(3, total, LANE), vmem(3, total + extra(total), columns)]
    scratch += [pltpu.SemaphoreType.DMA((5 * len(segments(total)) + 1,))]
    return call(
        "adjoint_first", kernel, [ANY] * 4 + whole(3), outs, scratch, 10,
        later, traj, traj_halo, spread, later_edges, z_left, z_right, first_any=True,
    )[0]


def tangent_second(earlier, pulled, variance, traj, traj_halo, var_halo):
    _, total, columns = variance.shape
    end = total + extra(total)

    def kernel(earlier_in, pulled_in, variance_in, traj_in, traj_halo_in, var_halo_in, ahead, increment, earl, pulled, variance,
               traj, traj_halo, var_halo, wide_a, wide_b, e_own, p_own, e_fold, p_fold, inc, out, sems):
        copies = Copies(sems)
        edge_copies = copies.rows([(earlier_in, 0, end)], total, end, e_fold)
        edge_copies += copies.rows([(pulled_in, 0, end)], total, end, p_fold)
        ready = fetch(copies, total, (earlier_in, earl), (pulled_in, pulled), (variance_in, variance), (var_halo_in, var_halo))
        traj_ready = fetch(copies, total, (traj_in, traj), (traj_halo_in, traj_halo))
        wait(edge_copies)
        unfold_in(e_fold, e_own)
        unfold_in(p_fold, p_own)

        def get(s):
            e_lanes, p_lanes = e_own[rows_at(s), :], p_own[rows_at(s), :]
            tiles = []
            for f in range(3):
                own = [tile_of(earl, f, s, t) - tile_of(variance, f, s, t) * tile_of(pulled, f, s, t) for t in range(2)]
                for t in range(2):
                    set_tile(inc, f, s, t, own[t])
                tiles.append(own + [halo_of(e_lanes, f) - var_halo[f, rows_at(s), :] * halo_of(p_lanes, f)])
            return tiles

        def put(s, new):
            for f in range(3):
                for t in range(2):
                    set_tile(out, f, s, t, -new[f][t])

        leaving = []

        def done(low, high):
            leaving.extend(copies.rows([(out, 0, total)], low, high, ahead.at[:, low:high, :]))
            leaving.extend(copies.rows([(inc, 0, total)], low, high, increment.at[:, low:high, :]))

        run_tangent(total, get, ready, traj, traj_halo, wide_a, wide_b, traj_ready, put, done)
        wait(leaving)

    outs = [f32(3, total, columns)] * 2
    scratch = [vmem(3, total, columns)] * 3 + [vmem(6, total, columns, dtype=traj.dtype), vmem(6, total, LANE, dtype=traj.dtype)]
    scratch += [vmem(3, total, LANE)] + [wide_scratch(total)] * 2 + [vmem(total, LANE)] * 2
    scratch += [vmem(3, extra(total), columns)] * 2 + [vmem(3, total, columns)] * 2
    scratch += [pltpu.SemaphoreType.DMA((8 * len(segments(total)) + 2,))]
    return call(
        "tangent_second", kernel, [ANY] * 6, outs, scratch, 16,
        earlier, pulled, variance, traj, traj_halo, var_halo, outs_any=True,
    )


def adjoint_second(later, traj, traj_halo, spread, last, pulled):
    _, total, columns = last.shape
    end = total + extra(total)

    def kernel(later_in, traj_in, traj_halo_in, spread_in, last_in, pulled_in, sums, later, traj, traj_halo, spread, last, pulled,
               wide_a, wide_b, flux_a, flux_b, own, fold, sems):
        copies = Copies(sems)
        edge_copies = copies.rows([(later_in, 0, end)], total, end, fold)
        ready = fetch(copies, total, (later_in, later), (traj_in, traj), (traj_halo_in, traj_halo))
        begin_put = fetch(copies, total, (spread_in, spread), (last_in, last), (pulled_in, pulled))
        wait(edge_copies)
        unfold_in(fold, own)
        sums[...] = jnp.zeros_like(sums)

        def get(s):
            lanes = own[rows_at(s), :]
            return [[tile_of(later, f, s, t) for t in range(2)] + [halo_of(lanes, f)] for f in range(3)]

        def put(s, new):
            parts = [jnp.zeros((GROUP, LANE), F32)] * 3
            for f in range(3):
                for t in range(2):
                    value = tile_of(spread, f, s, t) - new[f][t]
                    for k, other in enumerate((tile_of(last, f, s, t), tile_of(pulled, f, s, t), value)):
                        parts[k] = parts[k] + other * value
            for k in range(3):
                sums[k] = sums[k] + parts[k]

        run_adjoint(total, get, ready, traj, traj_halo, wide_a, wide_b, flux_a, flux_b, put, begin_put, lambda low, high: None)

    scratch = [vmem(3, total, columns), vmem(6, total, columns, dtype=traj.dtype), vmem(6, total, LANE, dtype=traj.dtype)]
    scratch += [vmem(3, total, columns)] * 3 + [wide_scratch(total)] * 4 + [vmem(total, LANE), vmem(3, extra(total), columns)]
    scratch += [pltpu.SemaphoreType.DMA((6 * len(segments(total)) + 1,))]
    outs = [f32(3, GROUP, LANE)]
    return call("adjoint_second", kernel, [ANY] * 6, outs, scratch, 16, later, traj, traj_halo, spread, last, pulled)[0]


def observe(parts, total, where):
    count = where.shape[0]

    def kernel(*refs):
        parts_in, (where_smem, column, out, field, picked, sems) = refs[: len(parts)], refs[len(parts) :]
        copies = Copies(sems)
        started = []
        for f in range(3):
            source = [(ref.at[f], at, rows) for ref, at, rows in placed(parts_in, parts)]
            started += copies.rows(source, 0, total, field.at[f * total : (f + 1) * total])
        wait(started)

        def step(i, carry):
            row = lax.shift_right_logical(where_smem[i], 8)
            picked[pl.ds(i, 1), :] = field[pl.ds(row, 1), :]
            return carry

        lax.fori_loop(0, count, step, 0, unroll=16)
        lane = iota((LANE, LANE), 1).astype(F32)
        for j in range(count // LANE):
            cut = slice(j * LANE, (j + 1) * LANE)
            at = jnp.broadcast_to(column[j : j + 1, :], (LANE, LANE)).T
            kept = jnp.where(lane == at, picked[cut, :LANE], 0.0)
            kept = kept + jnp.where(lane + float(LANE) == at, picked[cut, LANE:], 0.0)
            out[j : j + 1, :] = jnp.sum(kept.T, axis=0, keepdims=True)

    columns = 2 * LANE
    column = (where % columns).astype(F32).reshape(-1, LANE)
    return pl.pallas_call(
        kernel,
        in_specs=[ANY] * len(parts) + [pl.BlockSpec(memory_space=pltpu.SMEM)] + whole(1),
        out_specs=whole(1)[0],
        out_shape=f32(count // LANE, LANE),
        scratch_shapes=[vmem(3 * total, columns), vmem(count, columns), pltpu.SemaphoreType.DMA((3 * len(parts),))],
        compiler_params=PARAMS,
        cost_estimate=cost(3),
        name="observe",
    )(*[part[0] for part in parts], where, column)


def scatter(where, values, total):
    count = where.shape[0]

    def kernel(where_smem, values_smem, field):
        field[...] = jnp.zeros_like(field)
        lane = iota((1, 2 * LANE), 1)

        def step(i, carry):
            index = where_smem[i]
            at = (pl.ds(lax.shift_right_logical(index, 8), 1), slice(None))
            field[at] = field[at] + jnp.where(lane == (index & (2 * LANE - 1)), values_smem[i], 0.0)
            return carry

        lax.fori_loop(0, count, step, 0, unroll=8)

    return pl.pallas_call(
        kernel,
        in_specs=[pl.BlockSpec(memory_space=pltpu.SMEM)] * 2,
        out_specs=whole(1)[0],
        out_shape=f32(3 * total, 2 * LANE),
        compiler_params=PARAMS,
        cost_estimate=cost(3),
        name="scatter",
    )(where, values).reshape(3, total, 2 * LANE)


def one_sum(value):
    return jnp.sum(jnp.sum(value, axis=1, keepdims=True), axis=0, keepdims=True)


def pieces(cuts):
    return [(at, min(at + BLOCK, high)) for low, high in cuts for at in range(low, high, BLOCK)]


def summed(values):
    total = values[0]
    for value in values[1:]:
        total = total + value
    return total


def row_products(pairs, arrays, low, high, finish=None):
    columns = arrays[0][0][0].shape[2]
    counts = [len(parts) for parts in arrays]
    cuts = pieces([(low, high)])
    if finish:
        devices, early, a_before, d_parts, obs = finish
        scalars = [early] + a_before + d_parts + list(obs)
        out = f32(devices, 8, LANE)
    else:
        scalars = []
        out = f32(len(pairs), GROUP, columns)

    def kernel(*refs):
        refs = list(refs)
        inputs = []
        for parts in arrays:
            inputs.append([(refs.pop(0), at, count) for _, at, count in parts])
        extras, refs = refs[: len(scalars)], refs[len(scalars) :]
        out_ref, held, sems = refs[0], refs[1:-1], refs[-1]
        copies = Copies(sems)
        started = []
        for begin, end in cuts:
            group = []
            for parts, scratch in zip(inputs, held):
                group += copies.rows(parts, begin, end, scratch.at[:, begin - low : end - low, :])
            started.append(group)
        sums = tuple(jnp.zeros((GROUP, columns), F32) for _ in pairs)
        for (begin, end), group in zip(cuts, started):
            wait(group)

            def step(i, carry, begin=begin):
                at = pl.ds(pl.multiple_of(begin - low + i * GROUP, GROUP), GROUP)
                parts = list(carry)
                for f in range(3):
                    tiles = [a[f, at, :] for a in held]
                    for k, (one, two) in enumerate(pairs):
                        parts[k] = parts[k] + tiles[one] * tiles[two]
                return tuple(parts)

            sums = lax.fori_loop(0, (end - begin) // GROUP, step, sums)
        if not finish:
            for k, value in enumerate(sums):
                out_ref[k] = value
            return
        early_ref, extras = extras[0], extras[1:]
        before, d_refs, (o0, o1, o2) = extras[: len(a_before)], extras[len(a_before) : -3], (e[...] for e in extras[-3:])
        tail = [
            summed([one_sum(summed([sums[k]] + [r[k] for r in before]))] + [one_sum(summed([r[k] for r in d_refs]))])
            for k in range(3)
        ]
        head = [one_sum(early_ref[2 * k] + early_ref[2 * k + 1]) for k in range(3)]
        values = (
            head[0] + one_sum(o0 * o0),
            head[1] + one_sum(o0 * o1),
            tail[0] + one_sum(o0 * o2),
            head[2] + one_sum(o1 * o1),
            tail[1] + one_sum(o1 * o2),
            tail[2] + one_sum(o2 * o2),
        )
        lane = iota((8, LANE), 1)
        row = jnp.zeros((8, LANE), F32)
        for k, value in enumerate(values):
            row = jnp.where(lane == k, value, row)
        for k in range(devices):
            out_ref[k] = row

    return pl.pallas_call(
        kernel,
        in_specs=[ANY] * sum(counts) + whole(len(scalars)),
        out_specs=whole(1)[0],
        out_shape=out,
        scratch_shapes=[vmem(3, high - low, columns) for _ in arrays]
        + [pltpu.SemaphoreType.DMA((len(cuts) * (sum(counts)),))],
        compiler_params=PARAMS,
        cost_estimate=cost(9, 1),
        name="last_products" if finish else "products",
    )(*[part[0] for parts in arrays for part in parts], *scalars)


def weights(s00, s01, s02, s11, s12, s22):
    alpha = s01 / s00
    t11 = s11 - alpha * s01
    along = (s12 - alpha * s02) / t11
    beta = jnp.sqrt(s00)
    gamma = 1.0 / jnp.sqrt(t11)
    h00 = 1.0 + alpha
    h10_square = t11 / s00
    h10 = jnp.sqrt(h10_square)
    h01 = (s02 - alpha * s01) * gamma / beta
    h11 = 1.0 - alpha + along
    h21_square = (s22 - s02 * (s02 / s00) - along * (s12 - alpha * s02)) / t11
    g00 = h00 * h00 + h10_square
    g01 = h00 * h01 + h10 * h11
    g11 = h01 * h01 + h11 * h11 + h21_square
    q0 = beta * h00
    q1 = beta * h01
    det = g00 * g11 - g01 * g01
    y0 = (g11 * q0 - g01 * q1) / det
    y1 = (g00 * q1 - g01 * q0) / det
    c1 = y1 * gamma
    return (y0 / beta - c1 * alpha, c1)


def result(received, arrays, cuts, middle, m1, obs_part):
    total, columns = cuts[-1][1], arrays[0][0][0].shape[2]
    counts = [len(parts) for parts in arrays]
    small = pieces(cuts)

    def kernel(*refs):
        refs = list(refs)
        inputs = []
        for parts in arrays:
            inputs.append([(refs.pop(0), at, count) for _, at, count in parts])
        received, middle, m1, obs_part, multiplier, increment, dual = refs[:7]
        held, (multi, incr, coefs, sems) = refs[7:11], refs[11:]
        copies = Copies(sems)
        started = []
        for begin, end in small:
            group = []
            for parts, scratch in zip(inputs, held):
                group += copies.rows(parts, begin, end, scratch.at[:, begin:end, :])
            started.append(group)
        sums = jnp.sum(received[...], axis=0)
        lane = iota((8, LANE), 1)
        scalars = [
            jnp.broadcast_to(jnp.sum(jnp.where(lane == k, sums, 0.0), axis=1, keepdims=True), (8, LANE))
            for k in range(6)
        ]
        c0, c1 = weights(*scalars)
        coefs[0] = c0
        coefs[1] = c1
        dual[...] = (c0[0:1] * middle[...] + c1[0:1] * m1[...]) / obs_part[...]
        last, d1, inc0, inc1 = held
        leaving = []
        for (begin, end), group in zip(small, started):
            wait(group)

            def step(i, carry, begin=begin):
                start = pl.ds(pl.multiple_of(begin + i * GROUP, GROUP), GROUP)
                c0, c1 = (jnp.concatenate([coefs[k]] * 2, axis=0) for k in range(2))
                for f in range(3):
                    for t in range(2):
                        at = (f, start, slice(t * LANE, (t + 1) * LANE))
                        multi[at] = c0 * last[at] + c1 * d1[at]
                        incr[at] = c0 * inc0[at] + c1 * inc1[at]
                return carry

            lax.fori_loop(0, (end - begin) // GROUP, step, 0)
            leaving += copies.rows([(multi.at[:, begin:end, :], begin, end - begin)], begin, end, multiplier.at[:, begin:end, :])
            leaving += copies.rows([(incr.at[:, begin:end, :], begin, end - begin)], begin, end, increment.at[:, begin:end, :])
        wait(leaving)

    shape = (3, total, columns)
    return pl.pallas_call(
        kernel,
        in_specs=[ANY] * sum(counts) + whole(4),
        out_specs=[ANY, ANY] + whole(1),
        out_shape=[f32(*shape)] * 2 + [f32(*middle.shape)],
        scratch_shapes=[vmem(*shape)] * 6
        + [vmem(2, 8, LANE), pltpu.SemaphoreType.DMA((len(small) * (sum(counts) + 2),))],
        compiler_params=PARAMS,
        cost_estimate=cost(18, 1),
        name="result",
    )(*[part[0] for parts in arrays for part in parts], received, middle, m1, obs_part)


def moved(block, axis, distance, wrap):
    size = lax.axis_size(axis)
    if wrap:
        route = [(i, (i + distance) % size) for i in range(size)]
    else:
        route = [(i, i + distance) for i in range(size) if 0 <= i + distance < size]
    return lax.ppermute(block, axis, route)


def after(value, other):
    return lax.optimization_barrier((value, other))


def part(array, at, count=None):
    return (array, at, array.shape[1] if count is None else count)


def shards(rhs_state, innovations, trajectory, model_var, obs_var, obs_index, control_rhs):
    total, columns = rhs_state.shape[2:]
    first, last, variance = rhs_state[0], control_rhs[0], model_var[0]
    traj = trajectory.reshape(-1, total, columns)
    where = obs_index[0]
    middle, obs_part = innovations[0].reshape(-1, LANE), obs_var[0].reshape(-1, LANE)

    later = moved(last, "tm", -1, False)
    to_right, to_left, inc0 = edges_call(first, last, variance, traj)
    from_left = moved(to_right, "lon", 1, True)
    from_right = moved(to_left, "lon", -1, True)
    ahead, traj_halo, var_halo, last_edges = tangent_first(inc0, traj, from_left, from_right)
    later_edges = moved(last_edges, "tm", -1, False)
    a1 = moved(ahead, "tm", 1, False)
    z0 = scatter(where, (middle / obs_part).reshape(-1), total)
    z_right, z_left = spread_edges_call(z0)
    z_left, z_right = moved(z_right, "lon", 1, True), moved(z_left, "lon", -1, True)
    m1 = observe([part(inc0, 0)], total, where)
    m1, later_edges = after(m1, later_edges)
    d1 = adjoint_first(later, later_edges, traj, traj_halo, z0, z_left, z_right)

    d1_later = moved(d1, "tm", -1, False)
    ahead2, inc1 = tangent_second(a1, d1, variance, traj, traj_halo, var_halo)
    a2 = moved(ahead2, "tm", 1, False)
    z1 = scatter(where, (m1 / obs_part).reshape(-1), total)
    m2 = observe([part(inc1, 0)], total, where)
    a1, d1 = part(a1, 0, total), part(d1, 0, total)
    early = row_products(
        ((0, 0), (1, 1), (0, 2), (1, 3), (2, 2), (3, 3)), ([part(first, 0)], [part(last, 0)], [a1], [d1]), 0, total
    )
    d_sums = [adjoint_second(d1_later, traj, traj_halo, z1, last, d1[0])]
    devices = lax.axis_size("tm") * lax.axis_size("lon")
    sent = row_products(
        ((0, 2), (1, 2), (2, 2)),
        ([part(first, 0)], [a1], [part(a2, 0)]),
        0,
        total,
        (devices, early, [], d_sums, (middle, m1, m2)),
    )
    received = lax.all_to_all(sent, ("tm", "lon"), 0, 0)
    multiplier, increment, dual = result(
        received,
        ([part(last, 0)], [d1], [part(inc0, 0)], [part(inc1, 0)]),
        [(0, total)],
        middle,
        m1,
        obs_part,
    )
    return (multiplier[None], dual.reshape(1, -1), increment[None])


def solution(mesh):
    in_specs = (
        P("tm", None, None, "lon"),
        P("tm", "lon"),
        P("tm", None, None, None, "lon"),
        P("tm", None, None, "lon"),
        P("tm", "lon"),
        P("tm", "lon"),
        P("tm", None, None, "lon"),
    )
    out_specs = (P("tm", None, None, "lon"), P("tm", "lon"), P("tm", None, None, "lon"))
    return jax.shard_map(shards, mesh=mesh, in_specs=in_specs, out_specs=out_specs, check_vma=False)
```

time: 231 us -> 224 us (0.970)
  waiting for transfers between devices: 26.2 us -> 72.6 us
  local copies, waits for them, and re-layouts: 38.9 us -> 4.79 us
  other arithmetic: 14.6 us -> 1.81 us
  starting transfers between devices: 26.4 us -> 18.2 us
    ppermute x11 -> x9, waiting for transfers between devices: 26.2 us -> 72.6 us  [moved(): return lax.ppermute(block, axis, route)]
    gather x2 -> x0, local copies, waits for them, and re-layouts: 24 us -> none  [observed(): return field.reshape(-1)[where]]
    scatter-add x2 -> x0, other arithmetic: 14.6 us -> none  [spread(): jnp.zeros((3 * rows * columns,), F32).at[where].add(values / obs_part)]
    ppermute x11 -> x9, starting transfers between devices: 26.4 us -> 18.2 us  [moved(): return lax.ppermute(block, axis, route)]
    reshape x2 -> x0, local copies, waits for them, and re-layouts: 7.39 us -> none  [spread(): return flat.reshape(3, rows, columns)]
    unnamed x36 -> x26, local copies, waits for them, and re-layouts: 7.54 us -> 4.79 us
    pallas_call x7 -> x11, Pallas kernels: 98 us -> 98.5 us  [the longest x4 49.3 us: call(): pl.pallas_call(kernel, in_specs=ins, out_specs=specs, out_shape=outs, scr...]
  transfers between devices with their start and end apart: 11 -> 9, of which waited for: 6 -> 6; matrix products, arithmetic and copies ran while one was open for 22% -> 1% of each run, Pallas kernels for 39% -> 39%
where the time goes in v2:
time: 224 us; the launch traced here: 223 us
  Pallas kernels  110 us (49%)
  waiting for transfers between devices  72.6 us (32%)
  starting transfers between devices  18.2 us (8%)
  blocking collectives  14.4 us (6%)
  local copies, waits for them, and re-layouts  4.79 us (2%)
    ppermute x9, waiting for transfers between devices, moved(): return lax.ppermute(block, axis, route)  72.6 us
    pallas_call x4, Pallas kernels, call(): pl.pallas_call(kernel, in_specs=ins, out_specs=specs, out_shape=outs, scr...  49.3 us
    ppermute x9, starting transfers between devices, moved(): return lax.ppermute(block, axis, route)  18.2 us
    pallas_call x2, Pallas kernels, observe(): pl.pallas_call(kernel, in_specs=[ANY] * len(parts) + [pl.BlockSpec(memory...  14.8 us
    all_to_all x1, blocking collectives, shards(): received = lax.all_to_all(sent, ('tm', 'lon'), 0, 0)  14.4 us
    pallas_call x2, Pallas kernels, scatter(): pl.pallas_call(kernel, in_specs=[pl.BlockSpec(memory_space=pltpu.SMEM)] *...  14.1 us
    pallas_call x2, Pallas kernels, row_products(): pl.pallas_call(kernel, in_specs=[ANY] * sum(counts) + whole(len(scalars))...  11.5 us
    pallas_call x1, Pallas kernels, result(): pl.pallas_call(kernel, in_specs=[ANY] * sum(counts) + whole(4), out_specs...  8.84 us
  transfers between devices with their start and end apart: 9, of which 6 were waited for; matrix products, arithmetic and copies ran while one was open for 1% of the time, Pallas kernels for 39%

profile of v2, /device:TPU:0, one launch (start us, length us, event | category | flops | bytes accessed | tf_op | source)
XLA Modules:
  0.0 223.1 jit_solution(12900969595273323723)
XLA Ops:
  0.6 7.8 %edges.1 = (f32[64,1024]{1,0:T(8,128)}, f32[64,1024]{1,0:T(8,128)}, f32[3,1024,256]{2,1,0:T(8,128)}) custom-call(f32[3,1024,256]{2,1,0:T(8,128)} %bitcast.28, f32[3,1024,256]{2,1,0:T(8,128)} %bitcast.21, f32[3,1024,256]{2,1,0:T(8,128)} %bitcast.32, bf16[6,1024,256]{2,1,0:T(8,128)(2,1)} %bitcast.16), custom_call_target="tpu_custom_call" | custom-call | flops 1024 | bytes 16777216 | tf_op jit(solution)/shard_map/edges/pallas_call | solution.py:86
  8.9 2.9 %collective-permute-start.2 = (f32[64,1024]{1,0:T(8,128)}, f32[64,1024]{1,0:T(8,128)S(1)}, u32[]{:S(2)}, u32[]{:S(2)}) collective-permute-start(f32[64,1024]{1,0:T(8,128)} %get-tuple-element.21), channel_id=1, source_target_pairs={{0,7},{1,0},{2,1},{3,2},{4,3},{5,4},{6,5},{7,6},{8,15},{9,8},{10,9... | collective-permute-start | bytes 786440 | tf_op jit(solution)/shard_map/ppermute | solution.py:823
  13.1 3.1 %collective-permute-done.1.from_left = f32[64,1024]{1,0:T(8,128)S(1)} collective-permute-done((f32[64,1024]{1,0:T(8,128)}, f32[64,1024]{1,0:T(8,128)S(1)}, u32[]{:S(2)}, u32[]{:S(2)}) %collective-permute-start.1) | collective-permute-done | bytes 262176 | tf_op jit(solution)/shard_map/ppermute | solution.py:823
  18.6 13.5 %tangent_first.1 = (f32[3,1056,256]{2,1,0:T(8,128)}, bf16[6,1024,128]{2,1,0:T(8,128)(2,1)}, f32[3,1024,128]{2,1,0:T(8,128)}, f32[24,1024]{1,0:T(8,128)}) custom-call(f32[3,1024,256]{2,1,0:T(8,128)} %get-tuple-element.19.inc_in.refs_0_.refs_2_, bf16[6,1024,256]{2,1,0:T(8,128)(2,1)} %bitcast.17, f32[64,1024]{1,0:T(8,128)} %copy-done.3, f32[64,1024]{1,0:T(8,128)} %copy-done.4), custom_call_target="tpu_custom_call" | custom-call | flops 1024 | bytes 10485760 | tf_op jit(solution)/shard_map/tangent_first/pallas_call | solution.py:377
  32.0 3.7 %collective-permute-start.6 = (f32[3,1056,256]{2,1,0:T(8,128)}, f32[3,1056,256]{2,1,0:T(8,128)S(1)}, u32[]{:S(2)}, u32[]{:S(2)}) collective-permute-start(f32[3,1056,256]{2,1,0:T(8,128)} %get-tuple-element.27), channel_id=1, source_target_pairs={{0,8},{8,16},{16,24},{1,9},{9,17},{17,25},{2,10},{10,18},{18,26},{... | collective-permute-start | bytes 9732104 | tf_op jit(solution)/shard_map/ppermute | solution.py:823
  36.4 7.1 %scatter.2 = f32[3072,256]{1,0:T(8,128)} custom-call(s32[1024]{0:T(1024)} %bitcast.34, f32[1024]{0:T(1024)} %bitcast.43), custom_call_target="tpu_custom_call" | custom-call | flops 1024 | bytes 3145728 | tf_op jit(solution)/shard_map/scatter/pallas_call | solution.py:625
  43.5 4.0 %spread_edges.1 = (f32[16,1024]{1,0:T(8,128)}, f32[16,1024]{1,0:T(8,128)}) custom-call(f32[3,1024,256]{2,1,0:T(8,128)} %bitcast.26), custom_call_target="tpu_custom_call" | custom-call | flops 1024 | bytes 3145728 | tf_op jit(solution)/shard_map/spread_edges/pallas_call | solution.py:107
  47.5 1.8 collective-permute-start.4
  52.0 7.4 %observe.2.refs_6_ = f32[8,128]{1,0:T(8,128)} custom-call(f32[3,1024,256]{2,1,0:T(8,128)} %get-tuple-element.19.inc_in.refs_0_.refs_2_, s32[1024]{0:T(1024)} %bitcast.35, f32[8,128]{1,0:T(8,128)} %fusion.1.refs_2_), custom_call_target="tpu_custom_call" | custom-call | flops 1024 | bytes 3145728 | tf_op jit(solution)/shard_map/observe/pallas_call | solution.py:598
  59.4 26.1 %collective-permute-done.3.later_edges = f32[24,1024]{1,0:T(8,128)S(1)} collective-permute-done((f32[24,1024]{1,0:T(8,128)S(1)}, f32[24,1024]{1,0:T(8,128)S(1)}, u32[]{:S(2)}, u32[]{:S(2)}) %collective-permute-start.3) | collective-permute-done | bytes 98336 | tf_op jit(solution)/shard_map/ppermute | solution.py:823
  86.2 12.5 %adjoint_first.1.pulled_in.refs_3_.refs_1_ = f32[3,1056,256]{2,1,0:T(8,128)} custom-call(f32[3,1024,256]{2,1,0:T(8,128)} %collective-permute-done.later_in, bf16[6,1024,256]{2,1,0:T(8,128)(2,1)} %bitcast.18, bf16[6,1024,128]{2,1,0:T(8,128)(2,1)} %get-tuple-element.22.traj_halo_in, f32[3,1024,256]{2,1,0:T(8,128)} %bitcast.27, f32[24,1024]{1,0:T(8,128)} %copy-done.6, ...), custom_call_target="tpu_custom_call" | custom-call | flops 1024 | bytes 10485760 | tf_op jit(solution)/shard_map/adjoint_first/pallas_call | solution.py:377
  100.2 5.1 %collective-permute-done.6.earlier_in.refs_2_.refs_1_ = f32[3,1056,256]{2,1,0:T(8,128)S(1)} collective-permute-done((f32[3,1056,256]{2,1,0:T(8,128)}, f32[3,1056,256]{2,1,0:T(8,128)S(1)}, u32[]{:S(2)}, u32[]{:S(2)}) %collective-permute-start.6) | collective-permute-done | bytes 3244064 | tf_op jit(solution)/shard_map/ppermute | solution.py:823
  105.3 1.7 copy-done.1
  107.0 12.4 %tangent_second.1 = (f32[3,1024,256]{2,1,0:T(8,128)}, f32[3,1024,256]{2,1,0:T(8,128)}) custom-call(f32[3,1056,256]{2,1,0:T(8,128)} %copy-done.1, f32[3,1056,256]{2,1,0:T(8,128)} %adjoint_first.1.pulled_in.refs_3_.refs_1_, f32[3,1024,256]{2,1,0:T(8,128)} %bitcast.33, bf16[6,1024,256]{2,1,0:T(8,128)(2,1)} %bitcast.19, ...), custom_call_target="tpu_custom_call" | custom-call | flops 1024 | bytes 16777216 | tf_op jit(solution)/shard_map/tangent_second/pallas_call | solution.py:377
  119.5 4.5 %collective-permute-start.7 = (f32[3,1024,256]{2,1,0:T(8,128)}, f32[3,1024,256]{2,1,0:T(8,128)S(1)}, u32[]{:S(2)}, u32[]{:S(2)}) collective-permute-start(f32[3,1024,256]{2,1,0:T(8,128)} %get-tuple-element.30), channel_id=1, source_target_pairs={{0,8},{8,16},{16,24},{1,9},{9,17},{17,25},{2,10},{10,18},{18,26},{... | collective-permute-start | bytes 9437192 | tf_op jit(solution)/shard_map/ppermute | solution.py:823
  124.6 7.0 %scatter.3 = f32[3072,256]{1,0:T(8,128)} custom-call(s32[1024]{0:T(1024)} %bitcast.36, f32[1024]{0:T(1024)} %divide_bitcast_fusion.values_smem), custom_call_target="tpu_custom_call" | custom-call | flops 1024 | bytes 3145728 | tf_op jit(solution)/shard_map/scatter/pallas_call | solution.py:625
  131.6 7.4 %observe.3.refs_7_ = f32[8,128]{1,0:T(8,128)} custom-call(f32[3,1024,256]{2,1,0:T(8,128)} %get-tuple-element.29.refs_0_.refs_3_, s32[1024]{0:T(1024)} %bitcast.37, f32[8,128]{1,0:T(8,128)} %fusion.1.refs_2_), custom_call_target="tpu_custom_call" | custom-call | flops 1024 | bytes 3145728 | tf_op jit(solution)/shard_map/observe/pallas_call | solution.py:598
  139.0 5.8 %products.1.refs_3_ = f32[6,16,256]{2,1,0:T(8,128)} custom-call(f32[3,1024,256]{2,1,0:T(8,128)} %bitcast.29, f32[3,1024,256]{2,1,0:T(8,128)} %bitcast.22, f32[3,1056,256]{2,1,0:T(8,128)} %copy-done.1, f32[3,1056,256]{2,1,0:T(8,128)} %adjoint_first.1.pulled_in.refs_3_.refs_1_), custom_call_target="tpu_custom_call" | custom-call | flops 1024 | bytes 9437184 | tf_op jit(solution)/shard_map/products/pallas_call | solution.py:717
  144.7 26.9 %collective-permute-done.8.later_in = f32[3,1056,256]{2,1,0:T(8,128)} collective-permute-done((f32[3,1056,256]{2,1,0:T(8,128)}, f32[3,1056,256]{2,1,0:T(8,128)}, u32[]{:S(2)}, u32[]{:S(2)}) %collective-permute-start.8) | collective-permute-done | bytes 3244064 | tf_op jit(solution)/shard_map/ppermute | solution.py:823
  171.6 10.9 %adjoint_second.1.refs_4_ = f32[3,16,128]{2,1,0:T(8,128)} custom-call(f32[3,1056,256]{2,1,0:T(8,128)} %collective-permute-done.8.later_in, bf16[6,1024,256]{2,1,0:T(8,128)(2,1)} %bitcast.20, bf16[6,1024,128]{2,1,0:T(8,128)(2,1)} %get-tuple-element.22.traj_halo_in, f32[3,1024,256]{2,1,0:T(8,128)} %bitcast.31, f32[3,1024,256]{2,1,0:T(8,128)} %bitcast.23, ...), custom_call_target="tpu_custom_call" | custom-call | flops 1024 | bytes 16777216 | tf_op jit(solution)/shard_map/adjoint_second/pallas_call | solution.py:377
  182.5 9.8 %collective-permute-done.7.refs_2_ = f32[3,1024,256]{2,1,0:T(8,128)S(1)} collective-permute-done((f32[3,1024,256]{2,1,0:T(8,128)}, f32[3,1024,256]{2,1,0:T(8,128)S(1)}, u32[]{:S(2)}, u32[]{:S(2)}) %collective-permute-start.7) | collective-permute-done | bytes 3145760 | tf_op jit(solution)/shard_map/ppermute | solution.py:823
  194.0 5.7 %last_products.1 = f32[32,8,128]{2,1,0:T(8,128)} custom-call(f32[3,1024,256]{2,1,0:T(8,128)} %bitcast.30, f32[3,1056,256]{2,1,0:T(8,128)} %copy-done.1, f32[3,1024,256]{2,1,0:T(8,128)} %copy-done.2, f32[6,16,256]{2,1,0:T(8,128)} %products.1.refs_3_, f32[3,16,128]{2,1,0:T(8,128)} %adjoint_second.1.refs_4_, f32[8,128]{1,0:T(8,128)} %bitcast.39, ...), custom_call_target="tpu_custom_call" | custom-call | flops 1024 | bytes 9437184 | tf_op jit(solution)/shard_map/last_products/pallas_call | solution.py:717
  199.7 14.4 %all_to_all.5.refs_4_ = f32[32,8,128]{2,1,0:T(8,128)} all-to-all(f32[32,8,128]{2,1,0:T(8,128)} %last_products.1), channel_id=1, replica_groups=mesh['tm'=4,'lon'=8] {'tm','lon'}, dimensions={0} | all-to-all | bytes 262144 | tf_op jit(solution)/shard_map/all_to_all | solution.py:873
  214.1 8.8 %result.1 = (f32[3,1024,256]{2,1,0:T(8,128)}, f32[3,1024,256]{2,1,0:T(8,128)}, f32[8,128]{1,0:T(8,128)}) custom-call(f32[3,1024,256]{2,1,0:T(8,128)} %bitcast.24, f32[3,1056,256]{2,1,0:T(8,128)} %adjoint_first.1.pulled_in.refs_3_.refs_1_, f32[3,1024,256]{2,1,0:T(8,128)} %get-tuple-element.19.inc_in.refs_0_.refs_2_, ...), custom_call_target="tpu_custom_call" | custom-call | flops 1024 | bytes 18874368 | tf_op jit(solution)/shard_map/result/pallas_call | solution.py:804
  (37 shorter events, 11.9 us)
Async XLA Ops:
  0.6 11.2 %copy-start = (f32[1,3,1024,256]{3,2,1,0:T(8,128)S(1)}, f32[1,3,1024,256]{3,2,1,0:T(8,128)}, u32[]{:S(2)}) copy-start(f32[1,3,1024,256]{3,2,1,0:T(8,128)} %param.13) | copy-start | bytes 9437188
  8.5 7.7 %collective-permute-start.1 = (f32[64,1024]{1,0:T(8,128)}, f32[64,1024]{1,0:T(8,128)S(1)}, u32[]{:S(2)}, u32[]{:S(2)}) collective-permute-start(f32[64,1024]{1,0:T(8,128)} %get-tuple-element.20), channel_id=1, source_target_pairs={{0,1},{1,2},{2,3},{3,4},{4,5},{5,6},{6,7},{7,0},{8,9},{9,10},{10,1... | collective-permute-start | bytes 786440 | tf_op jit(solution)/shard_map/ppermute | solution.py:823
  8.9 8.9 %collective-permute-start.2 = (f32[64,1024]{1,0:T(8,128)}, f32[64,1024]{1,0:T(8,128)S(1)}, u32[]{:S(2)}, u32[]{:S(2)}) collective-permute-start(f32[64,1024]{1,0:T(8,128)} %get-tuple-element.21), channel_id=1, source_target_pairs={{0,7},{1,0},{2,1},{3,2},{4,3},{5,4},{6,5},{7,6},{8,15},{9,8},{10,9... | collective-permute-start | bytes 786440 | tf_op jit(solution)/shard_map/ppermute | solution.py:823
  11.9 73.7 %collective-permute-start = (f32[3,1024,256]{2,1,0:T(8,128)S(1)}, f32[3,1024,256]{2,1,0:T(8,128)}, u32[]{:S(2)}, u32[]{:S(2)}) collective-permute-start(f32[3,1024,256]{2,1,0:T(8,128)S(1)} %bitcast.25), channel_id=1, source_target_pairs={{8,0},{16,8},{24,16},{9,1},{17,9},{25,17},{10,2},{18,10},{26,18},{... | collective-permute-start | bytes 9437192 | tf_op jit(solution)/shard_map/ppermute | solution.py:823
  16.2 1.6 copy-start.3
  17.8 0.7 copy-start.4
  18.6 17.2 %copy-start.10 = (f32[1,1024]{1,0:T(1,128)S(1)}, f32[1,1024]{1,0:T(1,128)}, u32[]{:S(2)}) copy-start(f32[1,1024]{1,0:T(1,128)} %param.8) | copy-start | bytes 12292
  18.6 17.2 %copy-start.11 = (f32[1,1024]{1,0:T(1,128)S(1)}, f32[1,1024]{1,0:T(1,128)}, u32[]{:S(2)}) copy-start(f32[1,1024]{1,0:T(1,128)} %param.11) | copy-start | bytes 12292
  32.0 73.3 %collective-permute-start.6 = (f32[3,1056,256]{2,1,0:T(8,128)}, f32[3,1056,256]{2,1,0:T(8,128)S(1)}, u32[]{:S(2)}, u32[]{:S(2)}) collective-permute-start(f32[3,1056,256]{2,1,0:T(8,128)} %get-tuple-element.27), channel_id=1, source_target_pairs={{0,8},{8,16},{16,24},{1,9},{9,17},{17,25},{2,10},{10,18},{18,26},{... | collective-permute-start | bytes 9732104 | tf_op jit(solution)/shard_map/ppermute | solution.py:823
  36.4 13.7 %copy-start.12 = (f32[24,1024]{1,0:T(8,128)S(1)}, f32[24,1024]{1,0:T(8,128)}, u32[]{:S(2)}) copy-start(f32[24,1024]{1,0:T(8,128)} %get-tuple-element.23) | copy-start | bytes 294916
  36.4 15.0 %copy-start.5 = (s32[1,1024]{1,0:T(1,128)S(1)}, s32[1,1024]{1,0:T(1,128)}, u32[]{:S(2)}) copy-start(s32[1,1024]{1,0:T(1,128)} %param.12) | copy-start | bytes 12292
  47.5 38.1 %collective-permute-start.4 = (f32[16,1024]{1,0:T(8,128)}, f32[16,1024]{1,0:T(8,128)S(1)}, u32[]{:S(2)}, u32[]{:S(2)}) collective-permute-start(f32[16,1024]{1,0:T(8,128)} %get-tuple-element.25), channel_id=1, source_target_pairs={{0,1},{1,2},{2,3},{3,4},{4,5},{5,6},{6,7},{7,0},{8,9},{9,10},{10,1... | collective-permute-start | bytes 196616 | tf_op jit(solution)/shard_map/ppermute | solution.py:823
  49.2 36.3 %collective-permute-start.5 = (f32[16,1024]{1,0:T(8,128)}, f32[16,1024]{1,0:T(8,128)S(1)}, u32[]{:S(2)}, u32[]{:S(2)}) collective-permute-start(f32[16,1024]{1,0:T(8,128)} %get-tuple-element.26), channel_id=1, source_target_pairs={{0,7},{1,0},{2,1},{3,2},{4,3},{5,4},{6,5},{7,6},{8,15},{9,8},{10,9... | collective-permute-start | bytes 196616 | tf_op jit(solution)/shard_map/ppermute | solution.py:823
  50.1 35.4 %collective-permute-start.3 = (f32[24,1024]{1,0:T(8,128)S(1)}, f32[24,1024]{1,0:T(8,128)S(1)}, u32[]{:S(2)}, u32[]{:S(2)}) collective-permute-start(f32[24,1024]{1,0:T(8,128)S(1)} %copy-done.12), channel_id=1, source_target_pairs={{8,0},{16,8},{24,16},{9,1},{17,9},{25,17},{10,2},{18,10},{26,18},{... | collective-permute-start | bytes 294920 | tf_op jit(solution)/shard_map/ppermute | solution.py:823
  85.5 0.6 copy-start.6
  85.5 0.7 copy-start.8
  85.5 0.7 copy-start.9
  98.7 72.9 %collective-permute-start.8 = (f32[3,1056,256]{2,1,0:T(8,128)}, f32[3,1056,256]{2,1,0:T(8,128)}, u32[]{:S(2)}, u32[]{:S(2)}) collective-permute-start(f32[3,1056,256]{2,1,0:T(8,128)} %adjoint_first.1.pulled_in.refs_3_.refs_1_), channel_id=1, source_target_pairs={{8,0},{16,8},{24,16},{9,1},{17,9},{25,17},{10,2},{18,10},{26,18},{... | collective-permute-start | bytes 9732104 | tf_op jit(solution)/shard_map/ppermute | solution.py:823
  105.3 1.7 copy-start.1
  107.0 16.9 %copy-start.7 = (f32[8,128]{1,0:T(8,128)S(1)}, f32[8,128]{1,0:T(8,128)}, u32[]{:S(2)}) copy-start(f32[8,128]{1,0:T(8,128)} %observe.2.refs_6_) | copy-start | bytes 12292
  119.5 72.8 %collective-permute-start.7 = (f32[3,1024,256]{2,1,0:T(8,128)}, f32[3,1024,256]{2,1,0:T(8,128)S(1)}, u32[]{:S(2)}, u32[]{:S(2)}) collective-permute-start(f32[3,1024,256]{2,1,0:T(8,128)} %get-tuple-element.30), channel_id=1, source_target_pairs={{0,8},{8,16},{16,24},{1,9},{9,17},{17,25},{2,10},{10,18},{18,26},{... | collective-permute-start | bytes 9437192 | tf_op jit(solution)/shard_map/ppermute | solution.py:823
  192.3 1.7 copy-start.2

commit v3 on v2

--- a/solution.py
+++ b/solution.py
@@ -15,6 +15,7 @@
 MARGIN = 8
 HALO = 4
 TRAJ, INC, VAR, LAST, PLANES = 0, 6, 9, 12, 16
+MAIN = PLANES * HALO
 F32 = jnp.float32
 PARAMS = pltpu.CompilerParams(vmem_limit_bytes=56 * 1024 * 1024)
 
@@ -67,62 +68,43 @@
     return message.T
 
 
-def edges_kernel(first, last, variance, traj, to_right, to_left, increment):
-    rows = first.shape[1]
+def edges_kernel(increment, last, variance, traj, spread, to_right, to_left):
+    rows = last.shape[1]
     planes = [traj[p].astype(F32) for p in range(6)]
-    for f in range(3):
-        value = first[f] - variance[f] * last[f]
-        increment[f] = value
-        planes.append(value)
+    planes += [increment[f] for f in range(3)]
     planes += [variance[f] for f in range(3)]
     planes += [last[f] for f in range(3)]
-    split_edges(edges_of(planes, rows).T, to_right, to_left, PLANES)
-
-
-def edges_call(first, last, variance, traj):
-    rows = first.shape[1]
+    split_edges(edges_of(planes, rows).T, to_right.at[:MAIN], to_left.at[:MAIN], PLANES)
+    spread_planes = [spread[f] for f in range(3)]
+    split_edges(edges_of(spread_planes, rows).T, to_right.at[MAIN:], to_left.at[MAIN:], 4)
+
+
+def edges_call(increment, last, variance, traj, spread):
+    rows = last.shape[1]
     block = pl.BlockSpec((3, BLOCK, 2 * LANE), lambda i: (0, i, 0))
-    sent = pl.BlockSpec((PLANES * HALO, BLOCK), lambda i: (0, i))
+    sent = pl.BlockSpec((MAIN + 4 * HALO, BLOCK), lambda i: (0, i))
     return pl.pallas_call(
         edges_kernel,
         grid=(rows // BLOCK,),
-        in_specs=[block, block, block, pl.BlockSpec((6, BLOCK, 2 * LANE), lambda i: (0, i, 0))],
-        out_specs=[sent, sent, block],
-        out_shape=[jax.ShapeDtypeStruct((PLANES * HALO, rows), F32)] * 2
-        + [jax.ShapeDtypeStruct(first.shape, F32)],
+        in_specs=[block, block, block, pl.BlockSpec((6, BLOCK, 2 * LANE), lambda i: (0, i, 0)), block],
+        out_specs=[sent, sent],
+        out_shape=[jax.ShapeDtypeStruct((MAIN + 4 * HALO, rows), F32)] * 2,
         compiler_params=PARAMS,
         cost_estimate=cost(16),
         name="edges",
-    )(first, last, variance, traj)
-
-
-def spread_edges_kernel(spread, to_right, to_left):
-    planes = [spread[f] for f in range(3)]
-    split_edges(edges_of(planes, spread.shape[1]).T, to_right, to_left, 4)
-
-
-def spread_edges_call(spread):
-    rows = spread.shape[1]
-    sent = pl.BlockSpec((16, BLOCK), lambda i: (0, i))
-    return pl.pallas_call(
-        spread_edges_kernel,
-        grid=(rows // BLOCK,),
-        in_specs=[pl.BlockSpec((3, BLOCK, 2 * LANE), lambda i: (0, i, 0))],
-        out_specs=[sent, sent],
-        out_shape=[jax.ShapeDtypeStruct((16, rows), F32)] * 2,
-        compiler_params=PARAMS,
-        cost_estimate=cost(3),
-        name="spread_edges",
-    )(spread)
-
-
-def x_differences(tiles, first_lane, last_lane):
+    )(increment, last, variance, traj, spread)
+
+
+def x_differences(tiles, first_lane, last_lane, joined):
+    count = len(tiles)
     ahead = [pltpu.roll(t, LANE - 1, 1) for t in tiles]
     behind = [pltpu.roll(t, 1, 1) for t in tiles]
+    if not joined:
+        return [a - b for a, b in zip(ahead, behind)]
     return [
-        jnp.where(last_lane, ahead[(t + 1) % 3], ahead[t])
-        - jnp.where(first_lane, behind[(t - 1) % 3], behind[t])
-        for t in range(3)
+        jnp.where(last_lane, ahead[(t + 1) % count], ahead[t])
+        - jnp.where(first_lane, behind[(t - 1) % count], behind[t])
+        for t in range(count)
     ]
 
 
@@ -143,18 +125,25 @@
 def traj_tiles(traj, traj_halo, step, start):
     out = []
     for plane in range(3 * step, 3 * step + 3):
-        tiles = [traj[plane, rows_at(start), t * LANE : (t + 1) * LANE] for t in range(2)]
-        out.append([t.astype(F32) for t in tiles + [traj_halo[plane, rows_at(start), :]]])
+        tiles = []
+        if traj is not None:
+            tiles += [traj[plane, rows_at(start), t * LANE : (t + 1) * LANE] for t in range(2)]
+        if traj_halo is not None:
+            at = [traj_halo.at[plane]] if len(traj_halo.shape) == 3 else [traj_halo.at[plane, t] for t in range(2)]
+            tiles += [ref[rows_at(start), :] for ref in at]
+        out.append([t.astype(F32) for t in tiles])
     return out
 
 
 def load_rows(ref, start, offset):
-    return [[ref[f, t, pl.ds(start + (MARGIN + offset), GROUP), :] for t in range(3)] for f in range(3)]
+    return [
+        [ref[f, t, pl.ds(start + (MARGIN + offset), GROUP), :] for t in range(ref.shape[1])] for f in range(3)
+    ]
 
 
 def store_rows(ref, start, value):
     for f in range(3):
-        for t in range(3):
+        for t in range(ref.shape[1]):
             ref[f, t, pl.ds(start + MARGIN, GROUP), :] = value[f][t]
 
 
@@ -162,19 +151,19 @@
     rows = ref.shape[2]
     zero = jnp.zeros((MARGIN, LANE), F32)
     for f in range(3):
-        for t in range(3):
+        for t in range(ref.shape[1]):
             ref[f, t, 0:MARGIN, :] = zero
             ref[f, t, rows - MARGIN : rows, :] = zero
 
 
-def tangent_rows(source, traj, traj_halo, step, start, total):
+def tangent_rows(source, traj, traj_halo, step, start, total, joined=True):
     here, above, below = (load_rows(source, start, k) for k in (0, 1, -1))
     trajectory = traj_tiles(traj, traj_halo, step, start)
     turn = rotation_at(start, total)
     ends = lane_ends()
-    dx = [x_differences(here[f], *ends) for f in range(3)]
+    dx = [x_differences(here[f], *ends, joined) for f in range(3)]
     new = [[], [], []]
-    for t in range(3):
+    for t in range(source.shape[1]):
         b, e, n = (trajectory[f][t] for f in range(3))
         h, u, v = (here[f][t] for f in range(3))
         xh, xu, xv = (dx[f][t] for f in range(3))
@@ -209,7 +198,7 @@
         east[0].append(e * p + q)
         east[1].append(b * p + e * q)
         east[2].append(e * w)
-    dx = [x_differences(east[f], *ends) for f in range(3)]
+    dx = [x_differences(east[f], *ends, True) for f in range(3)]
     new = [[], [], []]
     for t in range(3):
         p, q, w = (here[f][t] for f in range(3))
@@ -247,22 +236,22 @@
 def unfold_in(folded, packed_ref):
     for j in range(packed_ref.shape[0] // LANE):
         at = (slice(j // 2 * 8, j // 2 * 8 + 8), slice(j % 2 * LANE, (j % 2 + 1) * LANE))
-        message = jnp.concatenate([folded[(f,) + at] for f in range(3)], axis=0)
+        message = jnp.concatenate([folded[(f,) + at] for f in range(folded.shape[0])], axis=0)
         packed_ref[j * LANE : (j + 1) * LANE, :] = padded_turn(message)
 
 
 def turn_out(halo, payload, behind):
     low = iota((8, LANE), 0) < HALO
     for j in range(halo.shape[1] // LANE):
-        for f in range(3):
+        for f in range(halo.shape[0]):
             turned = halo[f, j * LANE : (j + 1) * LANE, :].T
             ends = jnp.where(low, turned[:8], turned[LANE - 8 :])
             row = behind + j // 2 * 8
             payload[f, row : row + 8, j % 2 * LANE : (j % 2 + 1) * LANE] = pltpu.roll(ends, HALO, 0)
 
 
-def wide_scratch(rows):
-    return pltpu.VMEM((3, 3, rows + 2 * MARGIN, LANE), F32)
+def wide_scratch(rows, tiles=3):
+    return pltpu.VMEM((3, tiles, rows + 2 * MARGIN, LANE), F32)
 
 
 def tile_of(ref, f, start, t, offset=0):
@@ -311,7 +300,7 @@
     ]
 
 
-def run_tangent(total, get, ready, traj, traj_halo, wide_a, wide_b, traj_ready, put, done):
+def run_tangent(total, get, ready, traj, traj_halo, wide_a, wide_b, traj_ready, put, done, joined=True):
     clear_margins(wide_a)
     clear_margins(wide_b)
     for (low, high), copies in zip(segments(total), ready):
@@ -319,9 +308,11 @@
         over_rows(low, high, lambda s: store_rows(wide_a, s, get(s)))
     for (low, high), copies in zip(segments(total), traj_ready):
         wait(copies)
-        over_rows(low, high, lambda s: store_rows(wide_b, s, tangent_rows(wide_a, traj, traj_halo, 0, s, total)))
+        over_rows(
+            low, high, lambda s: store_rows(wide_b, s, tangent_rows(wide_a, traj, traj_halo, 0, s, total, joined))
+        )
     for low, high in segments(total):
-        over_rows(low, high, lambda s: put(s, tangent_rows(wide_b, traj, traj_halo, 1, s, total)))
+        over_rows(low, high, lambda s: put(s, tangent_rows(wide_b, traj, traj_halo, 1, s, total, joined)))
         done(low, high)
 
 
@@ -353,7 +344,7 @@
     return pltpu.roll(lanes, spread_shift(plane), 1)
 
 
-ANY = pl.BlockSpec(memory_space=pl.ANY)
+ANY = pl.BlockSpec(memory_space=pltpu.HBM)
 
 
 def whole(count):
@@ -386,77 +377,118 @@
     )(*args)
 
 
-def tangent_first(increment, traj, from_left, from_right):
+def tangent_band(first, last, variance, traj):
+    _, total, columns = first.shape
+
+    def kernel(first_in, last_in, variance_in, traj_in, ahead, increment, first, last, variance, traj, wide_a, wide_b, out, sems):
+        copies = Copies(sems)
+        ready = fetch(copies, total, (first_in, first), (last_in, last), (variance_in, variance))
+        traj_ready = fetch(copies, total, (traj_in, traj))
+
+        def get(s):
+            tiles = [
+                [tile_of(first, f, s, t) - tile_of(variance, f, s, t) * tile_of(last, f, s, t) for t in range(2)]
+                for f in range(3)
+            ]
+            for f in range(3):
+                for t in range(2):
+                    set_tile(first, f, s, t, tiles[f][t])
+            return tiles
+
+        def put(s, new):
+            for f in range(3):
+                for t in range(2):
+                    set_tile(out, f, s, t, -new[f][t])
+
+        leaving = []
+
+        def done(low, high):
+            leaving.extend(copies.rows([(out, 0, total)], low, high, ahead.at[:, low:high, :]))
+            leaving.extend(copies.rows([(first, 0, total)], low, high, increment.at[:, low:high, :]))
+
+        run_tangent(total, get, ready, traj, None, wide_a, wide_b, traj_ready, put, done)
+        wait(leaving)
+
+    outs = [f32(*first.shape)] * 2
+    scratch = [vmem(*first.shape)] * 3 + [vmem(*traj.shape, dtype=traj.dtype)] + [wide_scratch(total, 2)] * 2
+    scratch += [vmem(*first.shape), pltpu.SemaphoreType.DMA((6 * len(segments(total)),))]
+    return call("tangent_band", kernel, [ANY] * 4, outs, scratch, 18, first, last, variance, traj, outs_any=True)
+
+
+def tangent_seams(increment, traj, from_left, from_right):
     _, total, columns = increment.shape
 
-    def kernel(inc_in, traj_in, from_left, from_right, ahead, traj_halo, var_halo, last_edges, inc, traj, wide_a, wide_b, halo, out, sems):
+    def kernel(inc_in, traj_in, from_left, from_right, edges, traj_halo, var_halo, last_edges, spread_halo, inc, traj, wide_a, wide_b, seams, inc_halo, out, sems):
         copies = Copies(sems)
-        ready = fetch(copies, total, (inc_in, inc))
+        inc_ready = fetch(copies, total, (inc_in, inc))
         traj_ready = fetch(copies, total, (traj_in, traj))
+        left_part = iota((LANE, LANE), 1) < LANE // 2
         for j in range(total // LANE):
             cut = slice(j * LANE, (j + 1) * LANE)
-            joined = joined_edges(from_left[:, cut], from_right[:, cut], PLANES)
+            joined = joined_edges(from_left[:MAIN, cut], from_right[:MAIN, cut], PLANES)
             last_edges[:, cut] = joined[8 * LAST : 8 * LAST + 24]
             packed = joined.T
+            spread = padded_turn(joined_edges(from_left[MAIN:, cut], from_right[MAIN:, cut], 4))
             for plane in range(6):
                 traj_halo[plane, cut, :] = halo_of(packed, TRAJ + plane).astype(traj_halo.dtype)
             for f in range(3):
                 var_halo[f, cut, :] = halo_of(packed, VAR + f)
-                halo[f, cut, :] = halo_of(packed, INC + f)
+                inc_halo[f, cut, :] = halo_of(packed, INC + f)
+                spread_halo[f, cut, :] = halo_of(spread, f)
+        for copies_of in inc_ready + traj_ready:
+            wait(copies_of)
+        for j in range(total // LANE):
+            cut = slice(j * LANE, (j + 1) * LANE)
+            for plane in range(6):
+                halo = traj_halo[plane, cut, :].astype(F32)
+                own = [traj[plane, cut, t * LANE : (t + 1) * LANE].astype(F32) for t in range(2)]
+                seams[plane, 0, cut, :] = jnp.where(left_part, own[0], halo).astype(seams.dtype)
+                seams[plane, 1, cut, :] = jnp.where(left_part, halo, own[1]).astype(seams.dtype)
 
         def get(s):
-            return [[tile_of(inc, f, s, t) for t in range(2)] + [halo[f, rows_at(s), :]] for f in range(3)]
+            left = iota((GROUP, LANE), 1) < LANE // 2
+            tiles = []
+            for f in range(3):
+                halo = inc_halo[f, rows_at(s), :]
+                tiles.append([jnp.where(left, tile_of(inc, f, s, 0), halo), jnp.where(left, halo, tile_of(inc, f, s, 1))])
+            return tiles
 
         def put(s, new):
             for f in range(3):
                 for t in range(2):
-                    set_tile(out, f, s, t, -new[f][t])
-                halo[f, rows_at(s), :] = -new[f][2]
-
-        leaving = []
-
-        def done(low, high):
-            leaving.extend(copies.rows([(out, 0, total)], low, high, ahead.at[:, low:high, :]))
-
-        run_tangent(total, get, ready, traj, traj_halo, wide_a, wide_b, traj_ready, put, done)
-        turn_out(halo, out, total)
-        end = total + extra(total)
-        leaving.extend(copies.rows([(out, 0, end)], total, end, ahead.at[:, total:end, :]))
-        wait(leaving)
-
-    outs = [f32(3, total + extra(total), columns), jax.ShapeDtypeStruct((6, total, LANE), traj.dtype)]
-    outs += [f32(3, total, LANE), f32(24, total)]
-    scratch = [vmem(*increment.shape), vmem(*traj.shape, dtype=traj.dtype)] + [wide_scratch(total)] * 2
-    scratch += [vmem(3, total, LANE), vmem(3, total + extra(total), columns)]
-    scratch += [pltpu.SemaphoreType.DMA((3 * len(segments(total)) + 1,))]
-    return call(
-        "tangent_first", kernel, [ANY, ANY] + whole(2), outs, scratch, 10, increment, traj, from_left, from_right, first_any=True
-    )
-
-
-def adjoint_first(later, later_edges, traj, traj_halo, spread, z_left, z_right):
+                    out[2 * f + t, rows_at(s), :] = -new[f][t]
+
+        nothing = [[] for _ in segments(total)]
+        run_tangent(total, get, nothing, None, seams, wide_a, wide_b, nothing, put, lambda low, high: None, False)
+        turn_out(out, edges, 0)
+
+    outs = [f32(6, extra(total), columns), jax.ShapeDtypeStruct((6, total, LANE), traj.dtype)]
+    outs += [f32(3, total, LANE), f32(24, total), f32(3, total, LANE)]
+    scratch = [vmem(*increment.shape), vmem(*traj.shape, dtype=traj.dtype)] + [wide_scratch(total, 2)] * 2
+    scratch += [vmem(6, 2, total, LANE, dtype=traj.dtype), vmem(3, total, LANE), vmem(6, total, LANE)]
+    scratch += [pltpu.SemaphoreType.DMA((2 * len(segments(total)),))]
+    return call("tangent_seams", kernel, [ANY, ANY] + whole(2), outs, scratch, 10, increment, traj, from_left, from_right)
+
+
+def adjoint_first(later, later_edges, traj, traj_halo, spread, spread_halo):
     _, total, columns = later.shape
 
-    def kernel(later_in, traj_in, traj_halo_in, spread_in, later_edges, z_left, z_right, pulled, later, traj, traj_halo, spread,
-               wide_a, wide_b, flux_a, flux_b, own, z_own, halo, out, sems):
+    def kernel(later_in, traj_in, traj_halo_in, spread_in, spread_halo_in, later_edges, pulled, later, traj, traj_halo, spread,
+               wide_a, wide_b, flux_a, flux_b, own, halo, out, sems):
         copies = Copies(sems)
         ready = fetch(copies, total, (later_in, later), (traj_in, traj), (traj_halo_in, traj_halo))
-        begin_put = fetch(copies, total, (spread_in, spread))
+        begin_put = fetch(copies, total, (spread_in, spread), (spread_halo_in, halo))
         turn_in(later_edges, own)
-        for j in range(total // LANE):
-            cut = slice(j * LANE, (j + 1) * LANE)
-            z_own[cut, :] = padded_turn(joined_edges(z_left[:, cut], z_right[:, cut], 4))
 
         def get(s):
             lanes = own[rows_at(s), :]
             return [[tile_of(later, f, s, t) for t in range(2)] + [halo_of(lanes, f)] for f in range(3)]
 
         def put(s, new):
-            lanes = z_own[rows_at(s), :]
             for f in range(3):
                 for t in range(2):
                     set_tile(out, f, s, t, tile_of(spread, f, s, t) - new[f][t])
-                halo[f, rows_at(s), :] = halo_of(lanes, f) - new[f][2]
+                halo[f, rows_at(s), :] = halo[f, rows_at(s), :] - new[f][2]
 
         leaving = []
 
@@ -471,23 +503,23 @@
 
     outs = [f32(3, total + extra(total), columns)]
     scratch = [vmem(3, total, columns), vmem(6, total, columns, dtype=traj.dtype), vmem(6, total, LANE, dtype=traj.dtype)]
-    scratch += [vmem(3, total, columns)] + [wide_scratch(total)] * 4 + [vmem(total, LANE)] * 2
+    scratch += [vmem(3, total, columns)] + [wide_scratch(total)] * 4 + [vmem(total, LANE)]
     scratch += [vmem(3, total, LANE), vmem(3, total + extra(total), columns)]
-    scratch += [pltpu.SemaphoreType.DMA((5 * len(segments(total)) + 1,))]
+    scratch += [pltpu.SemaphoreType.DMA((6 * len(segments(total)) + 1,))]
     return call(
-        "adjoint_first", kernel, [ANY] * 4 + whole(3), outs, scratch, 10,
-        later, traj, traj_halo, spread, later_edges, z_left, z_right, first_any=True,
+        "adjoint_first", kernel, [ANY] * 5 + whole(1), outs, scratch, 10,
+        later, traj, traj_halo, spread, spread_halo, later_edges, first_any=True,
     )[0]
 
 
-def tangent_second(earlier, pulled, variance, traj, traj_halo, var_halo):
+def tangent_second(earlier, earlier_edges, pulled, variance, traj, traj_halo, var_halo):
     _, total, columns = variance.shape
     end = total + extra(total)
 
-    def kernel(earlier_in, pulled_in, variance_in, traj_in, traj_halo_in, var_halo_in, ahead, increment, earl, pulled, variance,
+    def kernel(earlier_in, edges_in, pulled_in, variance_in, traj_in, traj_halo_in, var_halo_in, ahead, increment, patched, earl, pulled, variance,
                traj, traj_halo, var_halo, wide_a, wide_b, e_own, p_own, e_fold, p_fold, inc, out, sems):
         copies = Copies(sems)
-        edge_copies = copies.rows([(earlier_in, 0, end)], total, end, e_fold)
+        edge_copies = copies.rows([(edges_in, 0, extra(total))], 0, extra(total), e_fold)
         edge_copies += copies.rows([(pulled_in, 0, end)], total, end, p_fold)
         ready = fetch(copies, total, (earlier_in, earl), (pulled_in, pulled), (variance_in, variance), (var_halo_in, var_halo))
         traj_ready = fetch(copies, total, (traj_in, traj), (traj_halo_in, traj_halo))
@@ -497,12 +529,20 @@
 
         def get(s):
             e_lanes, p_lanes = e_own[rows_at(s), :], p_own[rows_at(s), :]
+            lane = iota((GROUP, LANE), 1)
             tiles = []
             for f in range(3):
-                own = [tile_of(earl, f, s, t) - tile_of(variance, f, s, t) * tile_of(pulled, f, s, t) for t in range(2)]
+                left, right = halo_of(e_lanes, 2 * f), halo_of(e_lanes, 2 * f + 1)
+                fixed = [
+                    jnp.where(lane < 2, left, tile_of(earl, f, s, 0)),
+                    jnp.where(lane >= LANE - 2, right, tile_of(earl, f, s, 1)),
+                ]
+                own = [fixed[t] - tile_of(variance, f, s, t) * tile_of(pulled, f, s, t) for t in range(2)]
                 for t in range(2):
+                    set_tile(earl, f, s, t, fixed[t])
                     set_tile(inc, f, s, t, own[t])
-                tiles.append(own + [halo_of(e_lanes, f) - var_halo[f, rows_at(s), :] * halo_of(p_lanes, f)])
+                beside = jnp.where(lane < LANE // 2, right, left)
+                tiles.append(own + [beside - var_halo[f, rows_at(s), :] * halo_of(p_lanes, f)])
             return tiles
 
         def put(s, new):
@@ -515,18 +555,19 @@
         def done(low, high):
             leaving.extend(copies.rows([(out, 0, total)], low, high, ahead.at[:, low:high, :]))
             leaving.extend(copies.rows([(inc, 0, total)], low, high, increment.at[:, low:high, :]))
+            leaving.extend(copies.rows([(earl, 0, total)], low, high, patched.at[:, low:high, :]))
 
         run_tangent(total, get, ready, traj, traj_halo, wide_a, wide_b, traj_ready, put, done)
         wait(leaving)
 
-    outs = [f32(3, total, columns)] * 2
+    outs = [f32(3, total, columns)] * 3
     scratch = [vmem(3, total, columns)] * 3 + [vmem(6, total, columns, dtype=traj.dtype), vmem(6, total, LANE, dtype=traj.dtype)]
     scratch += [vmem(3, total, LANE)] + [wide_scratch(total)] * 2 + [vmem(total, LANE)] * 2
-    scratch += [vmem(3, extra(total), columns)] * 2 + [vmem(3, total, columns)] * 2
-    scratch += [pltpu.SemaphoreType.DMA((8 * len(segments(total)) + 2,))]
+    scratch += [vmem(6, extra(total), columns), vmem(3, extra(total), columns)] + [vmem(3, total, columns)] * 2
+    scratch += [pltpu.SemaphoreType.DMA((9 * len(segments(total)) + 2,))]
     return call(
-        "tangent_second", kernel, [ANY] * 6, outs, scratch, 16,
-        earlier, pulled, variance, traj, traj_halo, var_halo, outs_any=True,
+        "tangent_second", kernel, [ANY] * 7, outs, scratch, 16,
+        earlier, earlier_edges, pulled, variance, traj, traj_halo, var_halo, outs_any=True,
     )
 
 
@@ -721,7 +762,7 @@
         out_shape=out,
         scratch_shapes=[vmem(3, high - low, columns) for _ in arrays]
         + [pltpu.SemaphoreType.DMA((len(cuts) * (sum(counts)),))],
-        compiler_params=PARAMS,
+        compiler_params=pltpu.CompilerParams(vmem_limit_bytes=20 * 1024 * 1024),
         cost_estimate=cost(9, 1),
         name="last_products" if finish else "products",
     )(*[part[0] for parts in arrays for part in parts], *scalars)
@@ -751,25 +792,11 @@
     return (y0 / beta - c1 * alpha, c1)
 
 
-def result(received, arrays, cuts, middle, m1, obs_part):
-    total, columns = cuts[-1][1], arrays[0][0][0].shape[2]
-    counts = [len(parts) for parts in arrays]
-    small = pieces(cuts)
-
-    def kernel(*refs):
-        refs = list(refs)
-        inputs = []
-        for parts in arrays:
-            inputs.append([(refs.pop(0), at, count) for _, at, count in parts])
-        received, middle, m1, obs_part, multiplier, increment, dual = refs[:7]
-        held, (multi, incr, coefs, sems) = refs[7:11], refs[11:]
+def result(received, last, d1, inc0, inc1, middle, m1, obs_part):
+    _, total, columns = last.shape
+
+    def kernel(last, d1, inc0, inc1, received, middle, m1, obs_part, multiplier, increment, dual, multi, incr, sems):
         copies = Copies(sems)
-        started = []
-        for begin, end in small:
-            group = []
-            for parts, scratch in zip(inputs, held):
-                group += copies.rows(parts, begin, end, scratch.at[:, begin:end, :])
-            started.append(group)
         sums = jnp.sum(received[...], axis=0)
         lane = iota((8, LANE), 1)
         scalars = [
@@ -777,41 +804,33 @@
             for k in range(6)
         ]
         c0, c1 = weights(*scalars)
-        coefs[0] = c0
-        coefs[1] = c1
         dual[...] = (c0[0:1] * middle[...] + c1[0:1] * m1[...]) / obs_part[...]
-        last, d1, inc0, inc1 = held
+        c0, c1 = (jnp.concatenate([c] * (GROUP // 8), axis=0) for c in (c0, c1))
         leaving = []
-        for (begin, end), group in zip(small, started):
-            wait(group)
-
-            def step(i, carry, begin=begin):
-                start = pl.ds(pl.multiple_of(begin + i * GROUP, GROUP), GROUP)
-                c0, c1 = (jnp.concatenate([coefs[k]] * 2, axis=0) for k in range(2))
+        for low, high in segments(total):
+
+            def body(s):
                 for f in range(3):
                     for t in range(2):
-                        at = (f, start, slice(t * LANE, (t + 1) * LANE))
-                        multi[at] = c0 * last[at] + c1 * d1[at]
-                        incr[at] = c0 * inc0[at] + c1 * inc1[at]
-                return carry
-
-            lax.fori_loop(0, (end - begin) // GROUP, step, 0)
-            leaving += copies.rows([(multi.at[:, begin:end, :], begin, end - begin)], begin, end, multiplier.at[:, begin:end, :])
-            leaving += copies.rows([(incr.at[:, begin:end, :], begin, end - begin)], begin, end, increment.at[:, begin:end, :])
+                        set_tile(multi, f, s, t, c0 * tile_of(last, f, s, t) + c1 * tile_of(d1, f, s, t))
+                        set_tile(incr, f, s, t, c0 * tile_of(inc0, f, s, t) + c1 * tile_of(inc1, f, s, t))
+
+            over_rows(low, high, body)
+            leaving += copies.rows([(multi, 0, total)], low, high, multiplier.at[:, low:high, :])
+            leaving += copies.rows([(incr, 0, total)], low, high, increment.at[:, low:high, :])
         wait(leaving)
 
     shape = (3, total, columns)
     return pl.pallas_call(
         kernel,
-        in_specs=[ANY] * sum(counts) + whole(4),
+        in_specs=whole(8),
         out_specs=[ANY, ANY] + whole(1),
         out_shape=[f32(*shape)] * 2 + [f32(*middle.shape)],
-        scratch_shapes=[vmem(*shape)] * 6
-        + [vmem(2, 8, LANE), pltpu.SemaphoreType.DMA((len(small) * (sum(counts) + 2),))],
-        compiler_params=PARAMS,
+        scratch_shapes=[vmem(*shape)] * 2 + [pltpu.SemaphoreType.DMA((2 * len(segments(total)),))],
+        compiler_params=pltpu.CompilerParams(vmem_limit_bytes=40 * 1024 * 1024),
         cost_estimate=cost(18, 1),
         name="result",
-    )(*[part[0] for parts in arrays for part in parts], received, middle, m1, obs_part)
+    )(last, d1, inc0, inc1, received, middle, m1, obs_part)
 
 
 def moved(block, axis, distance, wrap):
@@ -839,21 +858,21 @@
     middle, obs_part = innovations[0].reshape(-1, LANE), obs_var[0].reshape(-1, LANE)
 
     later = moved(last, "tm", -1, False)
-    to_right, to_left, inc0 = edges_call(first, last, variance, traj)
+    ahead, inc0 = tangent_band(first, last, variance, traj)
+    a1 = moved(ahead, "tm", 1, False)
+    z0 = scatter(where, (middle / obs_part).reshape(-1), total)
+    to_right, to_left = edges_call(inc0, last, variance, traj, z0)
     from_left = moved(to_right, "lon", 1, True)
     from_right = moved(to_left, "lon", -1, True)
-    ahead, traj_halo, var_halo, last_edges = tangent_first(inc0, traj, from_left, from_right)
+    ahead_edges, traj_halo, var_halo, last_edges, z0_halo = tangent_seams(inc0, traj, from_left, from_right)
     later_edges = moved(last_edges, "tm", -1, False)
-    a1 = moved(ahead, "tm", 1, False)
-    z0 = scatter(where, (middle / obs_part).reshape(-1), total)
-    z_right, z_left = spread_edges_call(z0)
-    z_left, z_right = moved(z_right, "lon", 1, True), moved(z_left, "lon", -1, True)
+    a1_edges = moved(ahead_edges, "tm", 1, False)
     m1 = observe([part(inc0, 0)], total, where)
     m1, later_edges = after(m1, later_edges)
-    d1 = adjoint_first(later, later_edges, traj, traj_halo, z0, z_left, z_right)
+    d1 = adjoint_first(later, later_edges, traj, traj_halo, z0, z0_halo)
 
     d1_later = moved(d1, "tm", -1, False)
-    ahead2, inc1 = tangent_second(a1, d1, variance, traj, traj_halo, var_halo)
+    ahead2, inc1, a1 = tangent_second(a1, a1_edges, d1, variance, traj, traj_halo, var_halo)
     a2 = moved(ahead2, "tm", 1, False)
     z1 = scatter(where, (m1 / obs_part).reshape(-1), total)
     m2 = observe([part(inc1, 0)], total, where)
@@ -871,14 +890,7 @@
         (devices, early, [], d_sums, (middle, m1, m2)),
     )
     received = lax.all_to_all(sent, ("tm", "lon"), 0, 0)
-    multiplier, increment, dual = result(
-        received,
-        ([part(last, 0)], [d1], [part(inc0, 0)], [part(inc1, 0)]),
-        [(0, total)],
-        middle,
-        m1,
-        obs_part,
-    )
+    multiplier, increment, dual = result(received, last, d1[0], inc0, inc1, middle, m1, obs_part)
     return (multiplier[None], dual.reshape(1, -1), increment[None])
 
 

time: 224 us -> 204 us (0.911)
  waiting for transfers between devices: 72.6 us -> 43.4 us
  local copies, waits for them, and re-layouts: 4.79 us -> 10.6 us
  starting transfers between devices: 18.2 us -> 23.2 us
  Pallas kernels: 110 us -> 107 us
    ppermute x9 -> x8, waiting for transfers between devices: 72.6 us -> 43.4 us  [moved(): return lax.ppermute(block, axis, route)]
    pallas_call x4 -> x5, Pallas kernels: 49.3 us -> 59.5 us  [call(): pl.pallas_call(kernel, in_specs=ins, out_specs=specs, out_shape=outs, scr...]
    pallas_call x2 -> x1, Pallas kernels: 12.8 us -> 3.73 us  [result(): pl.pallas_call(kernel, in_specs=whole(8), out_specs=[ANY, ANY] + whole(1)...]
    unnamed x26 -> x44, local copies, waits for them, and re-layouts: 4.79 us -> 10.6 us
    ppermute x9 -> x8, starting transfers between devices: 18.2 us -> 23.2 us  [moved(): return lax.ppermute(block, axis, route)]
    pallas_call x2, Pallas kernels: 11.5 us -> 7.08 us  [row_products(): pl.pallas_call(kernel, in_specs=[ANY] * sum(counts) + whole(len(scalars))...]
  transfers between devices with their start and end apart: 9 -> 8, of which waited for: 6 -> 5; matrix products, arithmetic and copies ran while one was open for 1% -> 1% of each run, Pallas kernels for 39% -> 49%
where the time goes in v3:
time: 204 us; the launch traced here: 203 us
  Pallas kernels  107 us (52%)
  waiting for transfers between devices  43.4 us (21%)
  starting transfers between devices  23.2 us (11%)
  blocking collectives  16.3 us (8%)
  local copies, waits for them, and re-layouts  10.6 us (5%)
    pallas_call x5, Pallas kernels, call(): pl.pallas_call(kernel, in_specs=ins, out_specs=specs, out_shape=outs, scr...  59.5 us
    ppermute x8, waiting for transfers between devices, moved(): return lax.ppermute(block, axis, route)  43.4 us
    ppermute x8, starting transfers between devices, moved(): return lax.ppermute(block, axis, route)  23.2 us
    all_to_all x1, blocking collectives, shards(): received = lax.all_to_all(sent, ('tm', 'lon'), 0, 0)  16.3 us
    pallas_call x2, Pallas kernels, observe(): pl.pallas_call(kernel, in_specs=[ANY] * len(parts) + [pl.BlockSpec(memory...  14.8 us
    pallas_call x2, Pallas kernels, scatter(): pl.pallas_call(kernel, in_specs=[pl.BlockSpec(memory_space=pltpu.SMEM)] *...  14.1 us
    unnamed x44, local copies, waits for them, and re-layouts  10.6 us
    pallas_call x1, Pallas kernels, edges_call(): pl.pallas_call(edges_kernel, grid=(rows // BLOCK,), in_specs=[block, bloc...  7.63 us
  transfers between devices with their start and end apart: 8, of which 5 were waited for; matrix products, arithmetic and copies ran while one was open for 1% of the time, Pallas kernels for 49%

profile of v3, /device:TPU:0, one launch (start us, length us, event | category | flops | bytes accessed | tf_op | source)
XLA Modules:
  0.0 203.2 jit_solution(10165414093914679207)
XLA Ops:
  1.9 9.9 %tangent_band.1 = (f32[3,1024,256]{2,1,0:T(8,128)}, f32[3,1024,256]{2,1,0:T(8,128)}) custom-call(f32[3,1024,256]{2,1,0:T(8,128)} %bitcast.22, f32[3,1024,256]{2,1,0:T(8,128)} %bitcast.17, f32[3,1024,256]{2,1,0:T(8,128)} %bitcast.35, bf16[6,1024,256]{2,1,0:T(8,128)(2,1)} %bitcast.29), custom_call_target="tpu_custom_call" | custom-call | flops 1024 | bytes 18874368 | tf_op jit(solution)/shard_map/tangent_band/pallas_call | solution.py:368
  11.9 5.8 %collective-permute-start.4 = (f32[3,1024,256]{2,1,0:T(8,128)}, f32[3,1024,256]{2,1,0:T(8,128)S(1)}, u32[]{:S(2)}, u32[]{:S(2)}) collective-permute-start(f32[3,1024,256]{2,1,0:T(8,128)} %get-tuple-element.27), channel_id=1, source_target_pairs={{0,8},{8,16},{16,24},{1,9},{9,17},{17,25},{2,10},{10,18},{18,26},{... | collective-permute-start | bytes 9437192 | tf_op jit(solution)/shard_map/ppermute | solution.py:842
  18.3 7.0 %scatter.2 = f32[3072,256]{1,0:T(8,128)} custom-call(s32[1024]{0:T(1024)} %bitcast.41, f32[1024]{0:T(1024)} %bitcast.46), custom_call_target="tpu_custom_call" | custom-call | flops 1024 | bytes 3145728 | tf_op jit(solution)/shard_map/scatter/pallas_call | solution.py:666
  25.3 7.6 %edges.1 = (f32[80,1024]{1,0:T(8,128)}, f32[80,1024]{1,0:T(8,128)}) custom-call(f32[3,1024,256]{2,1,0:T(8,128)} %get-tuple-element.20.increment.inc_in.refs_0_.inc0, f32[3,1024,256]{2,1,0:T(8,128)} %bitcast.18, f32[3,1024,256]{2,1,0:T(8,128)} %bitcast.36, bf16[6,1024,256]{2,1,0:T(8,128)(2,1)} %bitcast.30, f32[3,1024,256]{2,1,0:T(8,128)} %bitcast.38), custom_call_target="tpu_custom_call" | custom-call | flops 1024 | bytes 16777216 | tf_op jit(solution)/shard_map/edges/pallas_call | solution.py:86
  32.9 2.6 %collective-permute-start.2 = (f32[80,1024]{1,0:T(8,128)}, f32[80,1024]{1,0:T(8,128)S(1)}, u32[]{:S(2)}, u32[]{:S(2)}) collective-permute-start(f32[80,1024]{1,0:T(8,128)} %get-tuple-element.22), channel_id=1, source_target_pairs={{0,7},{1,0},{2,1},{3,2},{4,3},{5,4},{6,5},{7,6},{8,15},{9,8},{10,9... | collective-permute-start | bytes 983048 | tf_op jit(solution)/shard_map/ppermute | solution.py:842
  35.5 6.1 %collective-permute-done.1.from_left = f32[80,1024]{1,0:T(8,128)S(1)} collective-permute-done((f32[80,1024]{1,0:T(8,128)}, f32[80,1024]{1,0:T(8,128)S(1)}, u32[]{:S(2)}, u32[]{:S(2)}) %collective-permute-start.1) | collective-permute-done | bytes 327712 | tf_op jit(solution)/shard_map/ppermute | solution.py:842
  43.4 13.5 %tangent_seams.1 = (f32[6,32,256]{2,1,0:T(8,128)}, bf16[6,1024,128]{2,1,0:T(8,128)(2,1)}, f32[3,1024,128]{2,1,0:T(8,128)}, f32[24,1024]{1,0:T(8,128)}, f32[3,1024,128]{2,1,0:T(8,128)}) custom-call(f32[3,1024,256]{2,1,0:T(8,128)} %get-tuple-element.20.increment.inc_in.refs_0_.inc0, bf16[6,1024,256]{2,1,0:T(8,128)(2,1)} %bitcast.31, f32[80,1024]{1,0:T(8,128)} %copy-done.17, ...), custom_call_target="tpu_custom_call" | custom-call | flops 1024 | bytes 10485760 | tf_op jit(solution)/shard_map/tangent_seams/pallas_call | solution.py:368
  58.3 4.7 %collective-permute-start.5 = (f32[6,32,256]{2,1,0:T(8,128)}, f32[6,32,256]{2,1,0:T(8,128)S(1)}, u32[]{:S(2)}, u32[]{:S(2)}) collective-permute-start(f32[6,32,256]{2,1,0:T(8,128)} %get-tuple-element.28), channel_id=1, source_target_pairs={{0,8},{8,16},{16,24},{1,9},{9,17},{17,25},{2,10},{10,18},{18,26},{... | collective-permute-start | bytes 589832 | tf_op jit(solution)/shard_map/ppermute | solution.py:842
  63.6 7.4 %observe.2.refs_6_.m1 = f32[8,128]{1,0:T(8,128)} custom-call(f32[3,1024,256]{2,1,0:T(8,128)} %get-tuple-element.20.increment.inc_in.refs_0_.inc0, s32[1024]{0:T(1024)} %bitcast.42, f32[8,128]{1,0:T(8,128)} %fusion.1.refs_2_), custom_call_target="tpu_custom_call" | custom-call | flops 1024 | bytes 3145728 | tf_op jit(solution)/shard_map/observe/pallas_call | solution.py:639
  71.0 5.0 %collective-permute-done.3.later_edges = f32[24,1024]{1,0:T(8,128)S(1)} collective-permute-done((f32[24,1024]{1,0:T(8,128)}, f32[24,1024]{1,0:T(8,128)S(1)}, u32[]{:S(2)}, u32[]{:S(2)}) %collective-permute-start.3) | collective-permute-done | bytes 98336 | tf_op jit(solution)/shard_map/ppermute | solution.py:842
  77.7 12.1 %adjoint_first.1.pulled_in.refs_3_.d1 = f32[3,1056,256]{2,1,0:T(8,128)} custom-call(f32[3,1024,256]{2,1,0:T(8,128)} %copy-done.16, bf16[6,1024,256]{2,1,0:T(8,128)(2,1)} %bitcast.32, bf16[6,1024,128]{2,1,0:T(8,128)(2,1)} %get-tuple-element.23.traj_halo_in, f32[3,1024,256]{2,1,0:T(8,128)} %bitcast.39, f32[3,1024,128]{2,1,0:T(8,128)} %get-tuple-element.24.spread_halo_in, ...), custom_call_target="tpu_custom_call" | custom-call | flops 1024 | bytes 10485760 | tf_op jit(solution)/shard_map/adjoint_first/pallas_call | solution.py:368
  92.8 12.9 %tangent_second.1 = (f32[3,1024,256]{2,1,0:T(8,128)}, f32[3,1024,256]{2,1,0:T(8,128)}, f32[3,1024,256]{2,1,0:T(8,128)}) custom-call(f32[3,1024,256]{2,1,0:T(8,128)} %copy-done.15, f32[6,32,256]{2,1,0:T(8,128)} %copy-done.19, f32[3,1056,256]{2,1,0:T(8,128)} %adjoint_first.1.pulled_in.refs_3_.d1, f32[3,1024,256]{2,1,0:T(8,128)} %bitcast.37, ...), custom_call_target="tpu_custom_call" | custom-call | flops 1024 | bytes 16777216 | tf_op jit(solution)/shard_map/tangent_second/pallas_call | solution.py:368
  105.7 6.2 %collective-permute-start.6 = (f32[3,1024,256]{2,1,0:T(8,128)}, f32[3,1024,256]{2,1,0:T(8,128)}, u32[]{:S(2)}, u32[]{:S(2)}) collective-permute-start(f32[3,1024,256]{2,1,0:T(8,128)} %get-tuple-element.32), channel_id=1, source_target_pairs={{0,8},{8,16},{16,24},{1,9},{9,17},{17,25},{2,10},{10,18},{18,26},{... | collective-permute-start | bytes 9437192 | tf_op jit(solution)/shard_map/ppermute | solution.py:842
  112.5 7.1 %scatter.3 = f32[3072,256]{1,0:T(8,128)} custom-call(s32[1024]{0:T(1024)} %bitcast.43, f32[1024]{0:T(1024)} %divide_bitcast_fusion.values_smem), custom_call_target="tpu_custom_call" | custom-call | flops 1024 | bytes 3145728 | tf_op jit(solution)/shard_map/scatter/pallas_call | solution.py:666
  119.6 7.4 %observe.3.refs_7_ = f32[8,128]{1,0:T(8,128)} custom-call(f32[3,1024,256]{2,1,0:T(8,128)} %get-tuple-element.30.refs_0_.inc1, s32[1024]{0:T(1024)} %bitcast.44, f32[8,128]{1,0:T(8,128)} %fusion.1.refs_2_), custom_call_target="tpu_custom_call" | custom-call | flops 1024 | bytes 3145728 | tf_op jit(solution)/shard_map/observe/pallas_call | solution.py:639
  128.9 1.9 copy-done.8
  130.8 3.9 %products.1.refs_3_ = f32[6,16,256]{2,1,0:T(8,128)S(1)} custom-call(f32[3,1024,256]{2,1,0:T(8,128)S(1)} %bitcast.23, f32[3,1024,256]{2,1,0:T(8,128)S(1)} %bitcast.20, f32[3,1024,256]{2,1,0:T(8,128)S(1)} %copy-done.8, f32[3,1056,256]{2,1,0:T(8,128)S(1)} %copy-done), custom_call_target="tpu_custom_call" | custom-call | flops 1024 | bytes 9437184 | tf_op jit(solution)/shard_map/products/pallas_call | solution.py:758
  134.7 28.7 %collective-permute-done.7.later_in = f32[3,1056,256]{2,1,0:T(8,128)} collective-permute-done((f32[3,1056,256]{2,1,0:T(8,128)}, f32[3,1056,256]{2,1,0:T(8,128)}, u32[]{:S(2)}, u32[]{:S(2)}) %collective-permute-start.7) | collective-permute-done | bytes 3244064 | tf_op jit(solution)/shard_map/ppermute | solution.py:842
  163.4 11.0 %adjoint_second.1.refs_4_ = f32[3,16,128]{2,1,0:T(8,128)} custom-call(f32[3,1056,256]{2,1,0:T(8,128)} %collective-permute-done.7.later_in, bf16[6,1024,256]{2,1,0:T(8,128)(2,1)} %bitcast.34, bf16[6,1024,128]{2,1,0:T(8,128)(2,1)} %get-tuple-element.23.traj_halo_in, f32[3,1024,256]{2,1,0:T(8,128)} %bitcast.40, f32[3,1024,256]{2,1,0:T(8,128)} %bitcast.19, ...), custom_call_target="tpu_custom_call" | custom-call | flops 1024 | bytes 16777216 | tf_op jit(solution)/shard_map/adjoint_second/pallas_call | solution.py:368
  174.4 2.7 %collective-permute-done.6.refs_2_ = f32[3,1024,256]{2,1,0:T(8,128)} collective-permute-done((f32[3,1024,256]{2,1,0:T(8,128)}, f32[3,1024,256]{2,1,0:T(8,128)}, u32[]{:S(2)}, u32[]{:S(2)}) %collective-permute-start.6) | collective-permute-done | bytes 3145760 | tf_op jit(solution)/shard_map/ppermute | solution.py:842
  177.1 1.9 copy-done.9
  179.7 3.2 %last_products.1 = f32[32,8,128]{2,1,0:T(8,128)S(1)} custom-call(f32[3,1024,256]{2,1,0:T(8,128)S(1)} %bitcast.24, f32[3,1024,256]{2,1,0:T(8,128)S(1)} %copy-done.9, f32[3,1024,256]{2,1,0:T(8,128)} %collective-permute-done.6.refs_2_, f32[6,16,256]{2,1,0:T(8,128)S(1)} %products.1.refs_3_, f32[3,16,128]{2,1,0:T(8,128)S(1)} %copy-done.10, ...), custom_call_target="tpu_custom_call" | custom-call | flops 1024 | bytes 9437184 | tf_op jit(solution)/shard_map/last_products/pallas_call | solution.py:758
  183.0 16.3 %all_to_all.5.received = f32[32,8,128]{2,1,0:T(8,128)S(1)} all-to-all(f32[32,8,128]{2,1,0:T(8,128)S(1)} %last_products.1), channel_id=1, replica_groups=mesh['tm'=4,'lon'=8] {'tm','lon'}, dimensions={0} | all-to-all | bytes 262144 | tf_op jit(solution)/shard_map/all_to_all | solution.py:892
  199.3 3.7 %result.1 = (f32[3,1024,256]{2,1,0:T(8,128)}, f32[3,1024,256]{2,1,0:T(8,128)}, f32[8,128]{1,0:T(8,128)}) custom-call(f32[3,1024,256]{2,1,0:T(8,128)S(1)} %bitcast.21, f32[3,1056,256]{2,1,0:T(8,128)S(1)} %copy-done.1, f32[3,1024,256]{2,1,0:T(8,128)S(1)} %copy-done.4, f32[3,1024,256]{2,1,0:T(8,128)S(1)} %copy-done.7, f32[32,8,128]{2,1,0:T(8,128)S(1)} %all_to_all.5.received, ...), custom_call_target="tpu_custom_call" | custom-call | flops 1024 | bytes 18874368 | tf_op jit(solution)/shard_map/result/pallas_call | solution.py:824
  (53 shorter events, 13.5 us)
Async XLA Ops:
  0.6 75.3 %collective-permute-start = (f32[3,1024,256]{2,1,0:T(8,128)}, f32[3,1024,256]{2,1,0:T(8,128)S(1)}, u32[]{:S(2)}, u32[]{:S(2)}) collective-permute-start(f32[3,1024,256]{2,1,0:T(8,128)} %bitcast.16), channel_id=1, source_target_pairs={{8,0},{16,8},{24,16},{9,1},{17,9},{25,17},{10,2},{18,10},{26,18},{... | collective-permute-start | bytes 9437192 | tf_op jit(solution)/shard_map/ppermute | solution.py:842
  1.9 15.7 %copy-start.12 = (f32[1,1024]{1,0:T(1,128)S(1)}, f32[1,1024]{1,0:T(1,128)}, u32[]{:S(2)}) copy-start(f32[1,1024]{1,0:T(1,128)} %param.8) | copy-start | bytes 12292
  1.9 15.7 %copy-start.13 = (f32[1,1024]{1,0:T(1,128)S(1)}, f32[1,1024]{1,0:T(1,128)}, u32[]{:S(2)}) copy-start(f32[1,1024]{1,0:T(1,128)} %param.11) | copy-start | bytes 12292
  11.9 79.2 %collective-permute-start.4 = (f32[3,1024,256]{2,1,0:T(8,128)}, f32[3,1024,256]{2,1,0:T(8,128)S(1)}, u32[]{:S(2)}, u32[]{:S(2)}) collective-permute-start(f32[3,1024,256]{2,1,0:T(8,128)} %get-tuple-element.27), channel_id=1, source_target_pairs={{0,8},{8,16},{16,24},{1,9},{9,17},{17,25},{2,10},{10,18},{18,26},{... | collective-permute-start | bytes 9437192 | tf_op jit(solution)/shard_map/ppermute | solution.py:842
  32.9 8.8 %collective-permute-start.1 = (f32[80,1024]{1,0:T(8,128)}, f32[80,1024]{1,0:T(8,128)S(1)}, u32[]{:S(2)}, u32[]{:S(2)}) collective-permute-start(f32[80,1024]{1,0:T(8,128)} %get-tuple-element.21), channel_id=1, source_target_pairs={{0,1},{1,2},{2,3},{3,4},{4,5},{5,6},{6,7},{7,0},{8,9},{9,10},{10,1... | collective-permute-start | bytes 983048 | tf_op jit(solution)/shard_map/ppermute | solution.py:842
  32.9 30.1 %copy-start.20 = (s32[1,1024]{1,0:T(1,128)S(1)}, s32[1,1024]{1,0:T(1,128)}, u32[]{:S(2)}) copy-start(s32[1,1024]{1,0:T(1,128)} %param.12) | copy-start | bytes 12292
  32.9 9.8 %collective-permute-start.2 = (f32[80,1024]{1,0:T(8,128)}, f32[80,1024]{1,0:T(8,128)S(1)}, u32[]{:S(2)}, u32[]{:S(2)}) collective-permute-start(f32[80,1024]{1,0:T(8,128)} %get-tuple-element.22), channel_id=1, source_target_pairs={{0,7},{1,0},{2,1},{3,2},{4,3},{5,4},{6,5},{7,6},{8,15},{9,8},{10,9... | collective-permute-start | bytes 983048 | tf_op jit(solution)/shard_map/ppermute | solution.py:842
  57.0 19.0 %collective-permute-start.3 = (f32[24,1024]{1,0:T(8,128)}, f32[24,1024]{1,0:T(8,128)S(1)}, u32[]{:S(2)}, u32[]{:S(2)}) collective-permute-start(f32[24,1024]{1,0:T(8,128)} %get-tuple-element.25), channel_id=1, source_target_pairs={{8,0},{16,8},{24,16},{9,1},{17,9},{25,17},{10,2},{18,10},{26,18},{... | collective-permute-start | bytes 294920 | tf_op jit(solution)/shard_map/ppermute | solution.py:842
  58.3 32.8 %collective-permute-start.5 = (f32[6,32,256]{2,1,0:T(8,128)}, f32[6,32,256]{2,1,0:T(8,128)S(1)}, u32[]{:S(2)}, u32[]{:S(2)}) collective-permute-start(f32[6,32,256]{2,1,0:T(8,128)} %get-tuple-element.28), channel_id=1, source_target_pairs={{0,8},{8,16},{16,24},{1,9},{9,17},{17,25},{2,10},{10,18},{18,26},{... | collective-permute-start | bytes 589832 | tf_op jit(solution)/shard_map/ppermute | solution.py:842
  89.8 73.6 %collective-permute-start.7 = (f32[3,1056,256]{2,1,0:T(8,128)}, f32[3,1056,256]{2,1,0:T(8,128)}, u32[]{:S(2)}, u32[]{:S(2)}) collective-permute-start(f32[3,1056,256]{2,1,0:T(8,128)} %adjoint_first.1.pulled_in.refs_3_.d1), channel_id=1, source_target_pairs={{8,0},{16,8},{24,16},{9,1},{17,9},{25,17},{10,2},{18,10},{26,18},{... | collective-permute-start | bytes 9732104 | tf_op jit(solution)/shard_map/ppermute | solution.py:842
  91.1 1.7 copy-start.15
  92.8 19.1 %copy-start.11 = (f32[8,128]{1,0:T(8,128)S(1)}, f32[8,128]{1,0:T(8,128)}, u32[]{:S(2)}) copy-start(f32[8,128]{1,0:T(8,128)} %observe.2.refs_6_.m1) | copy-start | bytes 12292
  92.8 34.2 %copy-start.2 = (f32[1,3,1024,256]{3,2,1,0:T(8,128)S(1)}, f32[1,3,1024,256]{3,2,1,0:T(8,128)}, u32[]{:S(2)}) copy-start(f32[1,3,1024,256]{3,2,1,0:T(8,128)} %param.13) | copy-start | bytes 9437188
  105.7 71.4 %collective-permute-start.6 = (f32[3,1024,256]{2,1,0:T(8,128)}, f32[3,1024,256]{2,1,0:T(8,128)}, u32[]{:S(2)}, u32[]{:S(2)}) collective-permute-start(f32[3,1024,256]{2,1,0:T(8,128)} %get-tuple-element.32), channel_id=1, source_target_pairs={{0,8},{8,16},{16,24},{1,9},{9,17},{17,25},{2,10},{10,18},{18,26},{... | collective-permute-start | bytes 9437192 | tf_op jit(solution)/shard_map/ppermute | solution.py:842
  112.5 14.5 %copy-start = (f32[3,1056,256]{2,1,0:T(8,128)S(1)}, f32[3,1056,256]{2,1,0:T(8,128)}, u32[]{:S(2)}) copy-start(f32[3,1056,256]{2,1,0:T(8,128)} %adjoint_first.1.pulled_in.refs_3_.d1) | copy-start | bytes 9732100
  127.0 1.9 copy-start.5
  128.9 1.9 copy-start.8
  163.4 13.7 %copy-start.6 = (f32[1,3,1024,256]{3,2,1,0:T(8,128)S(1)}, f32[1,3,1024,256]{3,2,1,0:T(8,128)}, u32[]{:S(2)}) copy-start(f32[1,3,1024,256]{3,2,1,0:T(8,128)} %param.7) | copy-start | bytes 9437188
  163.4 13.7 %copy-start.14 = (f32[8,128]{1,0:T(8,128)S(1)}, f32[8,128]{1,0:T(8,128)}, u32[]{:S(2)}) copy-start(f32[8,128]{1,0:T(8,128)} %observe.3.refs_7_) | copy-start | bytes 12292
  163.4 35.9 %copy-start.7 = (f32[3,1024,256]{2,1,0:T(8,128)S(1)}, f32[3,1024,256]{2,1,0:T(8,128)}, u32[]{:S(2)}) copy-start(f32[3,1024,256]{2,1,0:T(8,128)} %get-tuple-element.30.refs_0_.inc1) | copy-start | bytes 9437188
  177.1 1.9 copy-start.9
  179.7 19.6 %copy-start.1 = (f32[3,1056,256]{2,1,0:T(8,128)S(1)}, f32[3,1056,256]{2,1,0:T(8,128)}, u32[]{:S(2)}) copy-start(f32[3,1056,256]{2,1,0:T(8,128)} %adjoint_first.1.pulled_in.refs_3_.d1) | copy-start | bytes 9732100
  179.7 19.6 %copy-start.3 = (f32[1,3,1024,256]{3,2,1,0:T(8,128)S(1)}, f32[1,3,1024,256]{3,2,1,0:T(8,128)}, u32[]{:S(2)}) copy-start(f32[1,3,1024,256]{3,2,1,0:T(8,128)} %param.13) | copy-start | bytes 9437188
  179.7 19.6 %copy-start.4 = (f32[3,1024,256]{2,1,0:T(8,128)S(1)}, f32[3,1024,256]{2,1,0:T(8,128)}, u32[]{:S(2)}) copy-start(f32[3,1024,256]{2,1,0:T(8,128)} %get-tuple-element.20.increment.inc_in.refs_0_.inc0) | copy-start | bytes 9437188
  (6 other events, 5.5 us)

commit v4 on v3

--- a/solution.py
+++ b/solution.py
@@ -12,6 +12,7 @@
 LANE = 128
 BLOCK = 256
 GROUP = 16
+SHARE = 9
 MARGIN = 8
 HALO = 4
 TRAJ, INC, VAR, LAST, PLANES = 0, 6, 9, 12, 16
@@ -156,10 +157,10 @@
             ref[f, t, rows - MARGIN : rows, :] = zero
 
 
-def tangent_rows(source, traj, traj_halo, step, start, total, joined=True):
+def tangent_rows(source, traj, traj_halo, step, start, base, total, joined=True):
     here, above, below = (load_rows(source, start, k) for k in (0, 1, -1))
     trajectory = traj_tiles(traj, traj_halo, step, start)
-    turn = rotation_at(start, total)
+    turn = rotation_at(start + base, total)
     ends = lane_ends()
     dx = [x_differences(here[f], *ends, joined) for f in range(3)]
     new = [[], [], []]
@@ -185,11 +186,11 @@
     return out
 
 
-def adjoint_rows(source, flux, traj, traj_halo, step, start, total):
+def adjoint_rows(source, flux, traj, traj_halo, step, start, base, total):
     here = load_rows(source, start, 0)
     above, below = (load_rows(flux, start, k) for k in (1, -1))
     trajectory = traj_tiles(traj, traj_halo, step, start)
-    turn = rotation_at(start, total)
+    turn = rotation_at(start + base, total)
     ends = lane_ends()
     east = [[], [], []]
     for t in range(3):
@@ -293,30 +294,51 @@
     return [(at, min(at + BLOCK, total)) for at in range(0, total, BLOCK)]
 
 
-def fetch(copies, total, *pairs):
+def fetch(copies, begin, end, *pairs):
     return [
-        [copy for source, target in pairs for copy in copies.rows([(source, 0, total)], low, high, target.at[..., low:high, :])]
-        for low, high in segments(total)
+        [
+            copy
+            for parts, target in pairs
+            for copy in copies.rows(parts, begin + low, begin + high, target.at[..., low:high, :])
+        ]
+        for low, high in segments(end - begin)
     ]
 
 
-def run_tangent(total, get, ready, traj, traj_halo, wide_a, wide_b, traj_ready, put, done, joined=True):
+def leave(copies, source, begin, low, high, parts):
+    started = []
+    for target, at, count in parts:
+        first, last = max(low, at), min(high, at + count)
+        if first < last:
+            started += copies.rows([(source, begin, source.shape[1])], first, last, target.at[:, first - at : last - at, :])
+    return started
+
+
+def run_tangent(span, total, get, ready, traj, traj_halo, wide_a, wide_b, traj_ready, put, done, joined=True):
+    base, end, out_begin, out_end = span
+    held = segments(end - base)
     clear_margins(wide_a)
     clear_margins(wide_b)
-    for (low, high), copies in zip(segments(total), ready):
+    for (low, high), copies in zip(held, ready):
         wait(copies)
         over_rows(low, high, lambda s: store_rows(wide_a, s, get(s)))
-    for (low, high), copies in zip(segments(total), traj_ready):
+    for (low, high), copies in zip(held, traj_ready):
         wait(copies)
         over_rows(
-            low, high, lambda s: store_rows(wide_b, s, tangent_rows(wide_a, traj, traj_halo, 0, s, total, joined))
+            low, high, lambda s: store_rows(wide_b, s, tangent_rows(wide_a, traj, traj_halo, 0, s, base, total, joined))
         )
-    for low, high in segments(total):
-        over_rows(low, high, lambda s: put(s, tangent_rows(wide_b, traj, traj_halo, 1, s, total, joined)))
-        done(low, high)
-
-
-def run_adjoint(total, get, ready, traj, traj_halo, wide_a, wide_b, flux_a, flux_b, put, begin_put, done):
+    for low, high in segments(out_end - out_begin):
+        skip = out_begin - base
+        over_rows(
+            low + skip,
+            high + skip,
+            lambda s: put(s, tangent_rows(wide_b, traj, traj_halo, 1, s, base, total, joined)),
+        )
+        done(out_begin + low, out_begin + high)
+
+
+def run_adjoint(span, total, get, ready, traj, traj_halo, wide_a, wide_b, flux_a, flux_b, put, begin_put, done):
+    base, end, out_begin, out_end = span
     clear_margins(flux_a)
     clear_margins(flux_b)
 
@@ -326,18 +348,21 @@
         store_rows(flux_a, s, north_rows(field, traj_tiles(traj, traj_halo, 1, s)))
 
     def middle(s):
-        field = adjoint_rows(wide_a, flux_a, traj, traj_halo, 1, s, total)
+        field = adjoint_rows(wide_a, flux_a, traj, traj_halo, 1, s, base, total)
         store_rows(wide_b, s, field)
         store_rows(flux_b, s, north_rows(field, traj_tiles(traj, traj_halo, 0, s)))
 
-    for (low, high), copies in zip(segments(total), ready):
+    for (low, high), copies in zip(segments(end - base), ready):
         wait(copies)
         over_rows(low, high, begin)
-    over_rows(0, total, middle)
-    for (low, high), copies in zip(segments(total), begin_put):
+    over_rows(0, end - base, middle)
+    for (low, high), copies in zip(segments(out_end - out_begin), begin_put):
         wait(copies)
-        over_rows(low, high, lambda s: put(s, adjoint_rows(wide_b, flux_b, traj, traj_halo, 0, s, total)))
-        done(low, high)
+        skip = out_begin - base
+        over_rows(
+            low + skip, high + skip, lambda s: put(s, adjoint_rows(wide_b, flux_b, traj, traj_halo, 0, s, base, total))
+        )
+        done(out_begin + low, out_begin + high)
 
 
 def halo_of(lanes, plane):
@@ -377,13 +402,16 @@
     )(*args)
 
 
-def tangent_band(first, last, variance, traj):
+def tangent_band(first, last, variance, traj, cuts):
     _, total, columns = first.shape
 
-    def kernel(first_in, last_in, variance_in, traj_in, ahead, increment, first, last, variance, traj, wide_a, wide_b, out, sems):
+    def kernel(first_in, last_in, variance_in, traj_in, *refs):
+        aheads, refs = refs[: len(cuts)], refs[len(cuts) :]
+        increment, first, last, variance, traj, wide_a, wide_b, out, sems = refs
+        aheads = [(ref, low, high - low) for ref, (low, high) in zip(aheads, cuts)]
         copies = Copies(sems)
-        ready = fetch(copies, total, (first_in, first), (last_in, last), (variance_in, variance))
-        traj_ready = fetch(copies, total, (traj_in, traj))
+        ready = fetch(copies, 0, total, *[([(r, 0, total)], to) for r, to in ((first_in, first), (last_in, last), (variance_in, variance))])
+        traj_ready = fetch(copies, 0, total, ([(traj_in, 0, total)], traj))
 
         def get(s):
             tiles = [
@@ -403,15 +431,15 @@
         leaving = []
 
         def done(low, high):
-            leaving.extend(copies.rows([(out, 0, total)], low, high, ahead.at[:, low:high, :]))
-            leaving.extend(copies.rows([(first, 0, total)], low, high, increment.at[:, low:high, :]))
-
-        run_tangent(total, get, ready, traj, None, wide_a, wide_b, traj_ready, put, done)
+            leaving.extend(leave(copies, out, 0, low, high, aheads))
+            leaving.extend(leave(copies, first, 0, low, high, [(increment, 0, total)]))
+
+        run_tangent((0, total, 0, total), total, get, ready, traj, None, wide_a, wide_b, traj_ready, put, done)
         wait(leaving)
 
-    outs = [f32(*first.shape)] * 2
+    outs = [f32(3, high - low, columns) for low, high in cuts] + [f32(*first.shape)]
     scratch = [vmem(*first.shape)] * 3 + [vmem(*traj.shape, dtype=traj.dtype)] + [wide_scratch(total, 2)] * 2
-    scratch += [vmem(*first.shape), pltpu.SemaphoreType.DMA((6 * len(segments(total)),))]
+    scratch += [vmem(*first.shape), pltpu.SemaphoreType.DMA((7 * len(segments(total)),))]
     return call("tangent_band", kernel, [ANY] * 4, outs, scratch, 18, first, last, variance, traj, outs_any=True)
 
 
@@ -420,8 +448,8 @@
 
     def kernel(inc_in, traj_in, from_left, from_right, edges, traj_halo, var_halo, last_edges, spread_halo, inc, traj, wide_a, wide_b, seams, inc_halo, out, sems):
         copies = Copies(sems)
-        inc_ready = fetch(copies, total, (inc_in, inc))
-        traj_ready = fetch(copies, total, (traj_in, traj))
+        inc_ready = fetch(copies, 0, total, ([(inc_in, 0, total)], inc))
+        traj_ready = fetch(copies, 0, total, ([(traj_in, 0, total)], traj))
         left_part = iota((LANE, LANE), 1) < LANE // 2
         for j in range(total // LANE):
             cut = slice(j * LANE, (j + 1) * LANE)
@@ -459,7 +487,7 @@
                     out[2 * f + t, rows_at(s), :] = -new[f][t]
 
         nothing = [[] for _ in segments(total)]
-        run_tangent(total, get, nothing, None, seams, wide_a, wide_b, nothing, put, lambda low, high: None, False)
+        run_tangent((0, total, 0, total), total, get, nothing, None, seams, wide_a, wide_b, nothing, put, lambda low, high: None, False)
         turn_out(out, edges, 0)
 
     outs = [f32(6, extra(total), columns), jax.ShapeDtypeStruct((6, total, LANE), traj.dtype)]
@@ -470,65 +498,98 @@
     return call("tangent_seams", kernel, [ANY, ANY] + whole(2), outs, scratch, 10, increment, traj, from_left, from_right)
 
 
-def adjoint_first(later, later_edges, traj, traj_halo, spread, spread_halo):
-    _, total, columns = later.shape
-
-    def kernel(later_in, traj_in, traj_halo_in, spread_in, spread_halo_in, later_edges, pulled, later, traj, traj_halo, spread,
-               wide_a, wide_b, flux_a, flux_b, own, halo, out, sems):
+def whole_of(total, *pairs):
+    return [([(ref, 0, total)], target) for ref, target in pairs]
+
+
+def adjoint_first(span, later, later_edges, traj, traj_halo, spread, spread_halo):
+    base, end, out_begin, out_end = span
+    held, rows = end - base, out_end - out_begin
+    total, columns = spread.shape[1:]
+    count = len(later)
+
+    def kernel(*refs):
+        later_in, refs = placed(refs[:count], later), refs[count:]
+        traj_in, traj_halo_in, spread_in, spread_halo_in, later_edges, pulled = refs[:6]
+        field, traj, traj_halo, spread, wide_a, wide_b, flux_a, flux_b, own, halo, out, sems = refs[6:]
         copies = Copies(sems)
-        ready = fetch(copies, total, (later_in, later), (traj_in, traj), (traj_halo_in, traj_halo))
-        begin_put = fetch(copies, total, (spread_in, spread), (spread_halo_in, halo))
+        ready = fetch(copies, base, end, (later_in, field), *whole_of(total, (traj_in, traj), (traj_halo_in, traj_halo)))
+        begin_put = fetch(copies, out_begin, out_end, *whole_of(total, (spread_in, spread), (spread_halo_in, halo)))
         turn_in(later_edges, own)
+        if rows < halo.shape[1]:
+            halo[:, rows:, :] = jnp.zeros((3, halo.shape[1] - rows, LANE), F32)
+        skip = base - out_begin
 
         def get(s):
-            lanes = own[rows_at(s), :]
-            return [[tile_of(later, f, s, t) for t in range(2)] + [halo_of(lanes, f)] for f in range(3)]
+            lanes = own[rows_at(s, base), :]
+            return [[tile_of(field, f, s, t) for t in range(2)] + [halo_of(lanes, f)] for f in range(3)]
 
         def put(s, new):
             for f in range(3):
                 for t in range(2):
-                    set_tile(out, f, s, t, tile_of(spread, f, s, t) - new[f][t])
-                halo[f, rows_at(s), :] = halo[f, rows_at(s), :] - new[f][2]
+                    set_tile(out, f, s, t, tile_of(spread, f, s, t, skip) - new[f][t], skip)
+                halo[f, rows_at(s, skip), :] = halo[f, rows_at(s, skip), :] - new[f][2]
 
         leaving = []
 
         def done(low, high):
-            leaving.extend(copies.rows([(out, 0, total)], low, high, pulled.at[:, low:high, :]))
-
-        run_adjoint(total, get, ready, traj, traj_halo, wide_a, wide_b, flux_a, flux_b, put, begin_put, done)
-        turn_out(halo, out, total)
-        end = total + extra(total)
-        leaving.extend(copies.rows([(out, 0, end)], total, end, pulled.at[:, total:end, :]))
+            leaving.extend(leave(copies, out, out_begin, low, high, [(pulled, out_begin, rows)]))
+
+        run_adjoint(span, total, get, ready, traj, traj_halo, wide_a, wide_b, flux_a, flux_b, put, begin_put, done)
+        turn_out(halo, out, rows)
+        after_rows = rows + extra(rows)
+        leaving.extend(copies.rows([(out, 0, after_rows)], rows, after_rows, pulled.at[:, rows:after_rows, :]))
         wait(leaving)
 
-    outs = [f32(3, total + extra(total), columns)]
-    scratch = [vmem(3, total, columns), vmem(6, total, columns, dtype=traj.dtype), vmem(6, total, LANE, dtype=traj.dtype)]
-    scratch += [vmem(3, total, columns)] + [wide_scratch(total)] * 4 + [vmem(total, LANE)]
-    scratch += [vmem(3, total, LANE), vmem(3, total + extra(total), columns)]
-    scratch += [pltpu.SemaphoreType.DMA((6 * len(segments(total)) + 1,))]
+    outs = [f32(3, rows + extra(rows), columns)]
+    scratch = [vmem(3, held, columns), vmem(6, held, columns, dtype=traj.dtype), vmem(6, held, LANE, dtype=traj.dtype)]
+    scratch += [vmem(3, rows, columns)] + [wide_scratch(held)] * 4 + [vmem(total, LANE)]
+    scratch += [vmem(3, padded(rows), LANE), vmem(3, rows + extra(rows), columns)]
+    scratch += [pltpu.SemaphoreType.DMA(((6 + count) * len(segments(held)) + 1,))]
     return call(
-        "adjoint_first", kernel, [ANY] * 5 + whole(1), outs, scratch, 10,
-        later, traj, traj_halo, spread, spread_halo, later_edges, first_any=True,
+        "adjoint_first", kernel, [ANY] * (count + 4) + whole(1), outs, scratch, 10,
+        *[p[0] for p in later], traj, traj_halo, spread, spread_halo, later_edges, first_any=True,
     )[0]
 
 
-def tangent_second(earlier, earlier_edges, pulled, variance, traj, traj_halo, var_halo):
+def unfold_parts(copies, parts, folds):
+    started = []
+    for (ref, _, count), fold in zip(parts, folds):
+        started += copies.rows([(ref, 0, count + extra(count))], count, count + extra(count), fold)
+    return started
+
+
+def unfold_all(parts, folds, packed_ref):
+    for (_, at, count), fold in zip(parts, folds):
+        unfold_in(fold, packed_ref.at[at : at + padded(count), :])
+
+
+def tangent_second(span, earlier, earlier_edges, pulled, variance, traj, traj_halo, var_halo, new_begin):
+    base, end, out_begin, out_end = span
+    held, rows = end - base, out_end - out_begin
     _, total, columns = variance.shape
-    end = total + extra(total)
-
-    def kernel(earlier_in, edges_in, pulled_in, variance_in, traj_in, traj_halo_in, var_halo_in, ahead, increment, patched, earl, pulled, variance,
-               traj, traj_halo, var_halo, wide_a, wide_b, e_own, p_own, e_fold, p_fold, inc, out, sems):
+    n_earlier, n_pulled = len(earlier), len(pulled)
+
+    def kernel(*refs):
+        earlier_in, refs = placed(refs[:n_earlier], earlier), refs[n_earlier:]
+        pulled_in, refs = placed(refs[:n_pulled], pulled), refs[n_pulled:]
+        edges_in, variance_in, traj_in, traj_halo_in, var_halo_in, ahead, increment, patched = refs[:8]
+        earl, pull, variance, traj, traj_halo, var_halo, wide_a, wide_b, e_own, p_own, e_fold = refs[8:19]
+        p_folds, (inc, out, sems) = refs[19 : 19 + n_pulled], refs[19 + n_pulled :]
         copies = Copies(sems)
         edge_copies = copies.rows([(edges_in, 0, extra(total))], 0, extra(total), e_fold)
-        edge_copies += copies.rows([(pulled_in, 0, end)], total, end, p_fold)
-        ready = fetch(copies, total, (earlier_in, earl), (pulled_in, pulled), (variance_in, variance), (var_halo_in, var_halo))
-        traj_ready = fetch(copies, total, (traj_in, traj), (traj_halo_in, traj_halo))
+        edge_copies += unfold_parts(copies, pulled_in, p_folds)
+        ready = fetch(
+            copies, base, end, (earlier_in, earl), (pulled_in, pull), *whole_of(total, (variance_in, variance), (var_halo_in, var_halo))
+        )
+        traj_ready = fetch(copies, base, end, *whole_of(total, (traj_in, traj), (traj_halo_in, traj_halo)))
         wait(edge_copies)
         unfold_in(e_fold, e_own)
-        unfold_in(p_fold, p_own)
+        unfold_all(pulled_in, p_folds, p_own)
+        skip = base - out_begin
 
         def get(s):
-            e_lanes, p_lanes = e_own[rows_at(s), :], p_own[rows_at(s), :]
+            e_lanes, p_lanes = e_own[rows_at(s, base), :], p_own[rows_at(s, base), :]
             lane = iota((GROUP, LANE), 1)
             tiles = []
             for f in range(3):
@@ -537,7 +598,7 @@
                     jnp.where(lane < 2, left, tile_of(earl, f, s, 0)),
                     jnp.where(lane >= LANE - 2, right, tile_of(earl, f, s, 1)),
                 ]
-                own = [fixed[t] - tile_of(variance, f, s, t) * tile_of(pulled, f, s, t) for t in range(2)]
+                own = [fixed[t] - tile_of(variance, f, s, t) * tile_of(pull, f, s, t) for t in range(2)]
                 for t in range(2):
                     set_tile(earl, f, s, t, fixed[t])
                     set_tile(inc, f, s, t, own[t])
@@ -548,64 +609,77 @@
         def put(s, new):
             for f in range(3):
                 for t in range(2):
-                    set_tile(out, f, s, t, -new[f][t])
+                    set_tile(out, f, s, t, -new[f][t], skip)
 
         leaving = []
 
         def done(low, high):
-            leaving.extend(copies.rows([(out, 0, total)], low, high, ahead.at[:, low:high, :]))
-            leaving.extend(copies.rows([(inc, 0, total)], low, high, increment.at[:, low:high, :]))
-            leaving.extend(copies.rows([(earl, 0, total)], low, high, patched.at[:, low:high, :]))
-
-        run_tangent(total, get, ready, traj, traj_halo, wide_a, wide_b, traj_ready, put, done)
+            leaving.extend(leave(copies, out, out_begin, low, high, [(ahead, out_begin, rows)]))
+            if low == out_begin:
+                leaving.extend(leave(copies, inc, base, new_begin, end, [(increment, new_begin, end - new_begin)]))
+                leaving.extend(leave(copies, earl, base, new_begin, end, [(patched, new_begin, end - new_begin)]))
+
+        run_tangent(span, total, get, ready, traj, traj_halo, wide_a, wide_b, traj_ready, put, done)
         wait(leaving)
 
-    outs = [f32(3, total, columns)] * 3
-    scratch = [vmem(3, total, columns)] * 3 + [vmem(6, total, columns, dtype=traj.dtype), vmem(6, total, LANE, dtype=traj.dtype)]
-    scratch += [vmem(3, total, LANE)] + [wide_scratch(total)] * 2 + [vmem(total, LANE)] * 2
-    scratch += [vmem(6, extra(total), columns), vmem(3, extra(total), columns)] + [vmem(3, total, columns)] * 2
-    scratch += [pltpu.SemaphoreType.DMA((9 * len(segments(total)) + 2,))]
+    outs = [f32(3, rows, columns)] + [f32(3, end - new_begin, columns)] * 2
+    scratch = [vmem(3, held, columns)] * 3 + [vmem(6, held, columns, dtype=traj.dtype), vmem(6, held, LANE, dtype=traj.dtype)]
+    scratch += [vmem(3, held, LANE)] + [wide_scratch(held)] * 2 + [vmem(total, LANE), vmem(total + 2 * LANE, LANE)]
+    scratch += [vmem(6, extra(total), columns)] + [vmem(3, extra(p[2]), columns) for p in pulled]
+    scratch += [vmem(3, held, columns), vmem(3, rows, columns)]
+    scratch += [pltpu.SemaphoreType.DMA(((6 + n_earlier + n_pulled) * len(segments(held)) + 4 + n_pulled,))]
     return call(
-        "tangent_second", kernel, [ANY] * 7, outs, scratch, 16,
-        earlier, earlier_edges, pulled, variance, traj, traj_halo, var_halo, outs_any=True,
+        "tangent_second", kernel, [ANY] * (n_earlier + n_pulled + 5), outs, scratch, 16,
+        *[p[0] for p in earlier], *[p[0] for p in pulled], earlier_edges, variance, traj, traj_halo, var_halo, outs_any=True,
     )
 
 
 def adjoint_second(later, traj, traj_halo, spread, last, pulled):
     _, total, columns = last.shape
-    end = total + extra(total)
-
-    def kernel(later_in, traj_in, traj_halo_in, spread_in, last_in, pulled_in, sums, later, traj, traj_halo, spread, last, pulled,
-               wide_a, wide_b, flux_a, flux_b, own, fold, sems):
+    n_later, n_pulled = len(later), len(pulled)
+
+    def kernel(*refs):
+        later_in, refs = placed(refs[:n_later], later), refs[n_later:]
+        pulled_in, refs = placed(refs[:n_pulled], pulled), refs[n_pulled:]
+        traj_in, traj_halo_in, spread_in, last_in, sums, field, traj, traj_halo, spread, last, pull = refs[:11]
+        wide_a, wide_b, flux_a, flux_b, own = refs[11:16]
+        folds, sems = refs[16:-1], refs[-1]
         copies = Copies(sems)
-        edge_copies = copies.rows([(later_in, 0, end)], total, end, fold)
-        ready = fetch(copies, total, (later_in, later), (traj_in, traj), (traj_halo_in, traj_halo))
-        begin_put = fetch(copies, total, (spread_in, spread), (last_in, last), (pulled_in, pulled))
+        edge_copies = unfold_parts(copies, later_in, folds)
+        ready = fetch(copies, 0, total, (later_in, field), *whole_of(total, (traj_in, traj), (traj_halo_in, traj_halo)))
+        begin_put = fetch(copies, 0, total, (pulled_in, pull), *whole_of(total, (spread_in, spread), (last_in, last)))
         wait(edge_copies)
-        unfold_in(fold, own)
+        unfold_all(later_in, folds, own)
         sums[...] = jnp.zeros_like(sums)
 
         def get(s):
             lanes = own[rows_at(s), :]
-            return [[tile_of(later, f, s, t) for t in range(2)] + [halo_of(lanes, f)] for f in range(3)]
+            return [[tile_of(field, f, s, t) for t in range(2)] + [halo_of(lanes, f)] for f in range(3)]
 
         def put(s, new):
             parts = [jnp.zeros((GROUP, LANE), F32)] * 3
             for f in range(3):
                 for t in range(2):
                     value = tile_of(spread, f, s, t) - new[f][t]
-                    for k, other in enumerate((tile_of(last, f, s, t), tile_of(pulled, f, s, t), value)):
+                    for k, other in enumerate((tile_of(last, f, s, t), tile_of(pull, f, s, t), value)):
                         parts[k] = parts[k] + other * value
             for k in range(3):
                 sums[k] = sums[k] + parts[k]
 
-        run_adjoint(total, get, ready, traj, traj_halo, wide_a, wide_b, flux_a, flux_b, put, begin_put, lambda low, high: None)
+        span = (0, total, 0, total)
+        run_adjoint(
+            span, total, get, ready, traj, traj_halo, wide_a, wide_b, flux_a, flux_b, put, begin_put, lambda low, high: None
+        )
 
     scratch = [vmem(3, total, columns), vmem(6, total, columns, dtype=traj.dtype), vmem(6, total, LANE, dtype=traj.dtype)]
-    scratch += [vmem(3, total, columns)] * 3 + [wide_scratch(total)] * 4 + [vmem(total, LANE), vmem(3, extra(total), columns)]
-    scratch += [pltpu.SemaphoreType.DMA((6 * len(segments(total)) + 1,))]
+    scratch += [vmem(3, total, columns)] * 3 + [wide_scratch(total)] * 4 + [vmem(total + 2 * LANE, LANE)]
+    scratch += [vmem(3, extra(p[2]), columns) for p in later]
+    scratch += [pltpu.SemaphoreType.DMA(((4 + n_later + n_pulled) * len(segments(total)) + n_later,))]
     outs = [f32(3, GROUP, LANE)]
-    return call("adjoint_second", kernel, [ANY] * 6, outs, scratch, 16, later, traj, traj_halo, spread, last, pulled)[0]
+    return call(
+        "adjoint_second", kernel, [ANY] * (n_later + n_pulled + 4), outs, scratch, 16,
+        *[p[0] for p in later], *[p[0] for p in pulled], traj, traj_halo, spread, last,
+    )[0]
 
 
 def observe(parts, total, where):
@@ -794,8 +868,12 @@
 
 def result(received, last, d1, inc0, inc1, middle, m1, obs_part):
     _, total, columns = last.shape
-
-    def kernel(last, d1, inc0, inc1, received, middle, m1, obs_part, multiplier, increment, dual, multi, incr, sems):
+    n_d1, n_inc1 = len(d1), len(inc1)
+
+    def kernel(last, inc0, *refs):
+        d1_in, refs = placed(refs[:n_d1], d1), refs[n_d1:]
+        inc1_in, refs = placed(refs[:n_inc1], inc1), refs[n_inc1:]
+        received, middle, m1, obs_part, multiplier, increment, dual, multi, incr, sems = refs
         copies = Copies(sems)
         sums = jnp.sum(received[...], axis=0)
         lane = iota((8, LANE), 1)
@@ -807,30 +885,31 @@
         dual[...] = (c0[0:1] * middle[...] + c1[0:1] * m1[...]) / obs_part[...]
         c0, c1 = (jnp.concatenate([c] * (GROUP // 8), axis=0) for c in (c0, c1))
         leaving = []
-        for low, high in segments(total):
-
-            def body(s):
-                for f in range(3):
-                    for t in range(2):
-                        set_tile(multi, f, s, t, c0 * tile_of(last, f, s, t) + c1 * tile_of(d1, f, s, t))
-                        set_tile(incr, f, s, t, c0 * tile_of(inc0, f, s, t) + c1 * tile_of(inc1, f, s, t))
-
-            over_rows(low, high, body)
-            leaving += copies.rows([(multi, 0, total)], low, high, multiplier.at[:, low:high, :])
-            leaving += copies.rows([(incr, 0, total)], low, high, increment.at[:, low:high, :])
+        for out, whole_in, parts, target in ((multi, last, d1_in, multiplier), (incr, inc0, inc1_in, increment)):
+            for ref, at, count in parts:
+                for low, high in segments(count):
+
+                    def body(s, out=out, whole_in=whole_in, ref=ref, at=at):
+                        for f in range(3):
+                            for t in range(2):
+                                value = c0 * tile_of(whole_in, f, s, t, at) + c1 * tile_of(ref, f, s, t)
+                                set_tile(out, f, s, t, value, at)
+
+                    over_rows(low, high, body)
+                    leaving += leave(copies, out, 0, at + low, at + high, [(target, 0, total)])
         wait(leaving)
 
     shape = (3, total, columns)
     return pl.pallas_call(
         kernel,
-        in_specs=whole(8),
+        in_specs=whole(6 + n_d1 + n_inc1),
         out_specs=[ANY, ANY] + whole(1),
         out_shape=[f32(*shape)] * 2 + [f32(*middle.shape)],
-        scratch_shapes=[vmem(*shape)] * 2 + [pltpu.SemaphoreType.DMA((2 * len(segments(total)),))],
+        scratch_shapes=[vmem(*shape)] * 2 + [pltpu.SemaphoreType.DMA((4 * len(segments(total)) + 4,))],
         compiler_params=pltpu.CompilerParams(vmem_limit_bytes=40 * 1024 * 1024),
         cost_estimate=cost(18, 1),
         name="result",
-    )(last, d1, inc0, inc1, received, middle, m1, obs_part)
+    )(last, inc0, *[p[0] for p in d1], *[p[0] for p in inc1], received, middle, m1, obs_part)
 
 
 def moved(block, axis, distance, wrap):
@@ -857,9 +936,13 @@
     where = obs_index[0]
     middle, obs_part = innovations[0].reshape(-1, LANE), obs_var[0].reshape(-1, LANE)
 
-    later = moved(last, "tm", -1, False)
-    ahead, inc0 = tangent_band(first, last, variance, traj)
-    a1 = moved(ahead, "tm", 1, False)
+    step = GROUP
+    cut = total * SHARE // 16 // GROUP * GROUP
+    one, two = cut - step, cut - 2 * step
+
+    later = [part(moved(last, "tm", -1, False), 0)]
+    ahead, inc0 = tangent_band(first, last, variance, traj, [(0, total)])
+    a1 = [part(moved(ahead, "tm", 1, False), 0)]
     z0 = scatter(where, (middle / obs_part).reshape(-1), total)
     to_right, to_left = edges_call(inc0, last, variance, traj, z0)
     from_left = moved(to_right, "lon", 1, True)
@@ -869,28 +952,37 @@
     a1_edges = moved(ahead_edges, "tm", 1, False)
     m1 = observe([part(inc0, 0)], total, where)
     m1, later_edges = after(m1, later_edges)
-    d1 = adjoint_first(later, later_edges, traj, traj_halo, z0, z0_halo)
-
-    d1_later = moved(d1, "tm", -1, False)
-    ahead2, inc1, a1 = tangent_second(a1, a1_edges, d1, variance, traj, traj_halo, var_halo)
-    a2 = moved(ahead2, "tm", 1, False)
+
+    d1, d1_later, a2, inc1, fixed = [], [], [], [], []
+    spans = [(0, cut, 0, one), (one - step, total, one, total)]
+    seconds = [(0, one, 0, two), (two - step, total, two, total)]
+    for c, (span, second) in enumerate(zip(spans, seconds)):
+        pulled = adjoint_first(span, later, later_edges, traj, traj_halo, z0, z0_halo)
+        d1.append(part(pulled, span[2], span[3] - span[2]))
+        d1_later.append(part(moved(pulled, "tm", -1, False), *d1[-1][1:]))
+        ahead, increment, patched = tangent_second(
+            second, a1, a1_edges, d1, variance, traj, traj_halo, var_halo, span[2]
+        )
+        a2.append(part(moved(ahead, "tm", 1, False), second[2]))
+        inc1.append(part(increment, span[2]))
+        fixed.append(part(patched, span[2]))
+    a1 = fixed
     z1 = scatter(where, (m1 / obs_part).reshape(-1), total)
-    m2 = observe([part(inc1, 0)], total, where)
-    a1, d1 = part(a1, 0, total), part(d1, 0, total)
+    m2 = observe(inc1, total, where)
     early = row_products(
-        ((0, 0), (1, 1), (0, 2), (1, 3), (2, 2), (3, 3)), ([part(first, 0)], [part(last, 0)], [a1], [d1]), 0, total
+        ((0, 0), (1, 1), (0, 2), (1, 3), (2, 2), (3, 3)), ([part(first, 0)], [part(last, 0)], a1, d1), 0, total
     )
-    d_sums = [adjoint_second(d1_later, traj, traj_halo, z1, last, d1[0])]
+    d_sums = [adjoint_second(d1_later, traj, traj_halo, z1, last, d1)]
     devices = lax.axis_size("tm") * lax.axis_size("lon")
     sent = row_products(
         ((0, 2), (1, 2), (2, 2)),
-        ([part(first, 0)], [a1], [part(a2, 0)]),
+        ([part(first, 0)], a1, a2),
         0,
         total,
         (devices, early, [], d_sums, (middle, m1, m2)),
     )
     received = lax.all_to_all(sent, ("tm", "lon"), 0, 0)
-    multiplier, increment, dual = result(received, last, d1[0], inc0, inc1, middle, m1, obs_part)
+    multiplier, increment, dual = result(received, last, d1, inc0, inc1, middle, m1, obs_part)
     return (multiplier[None], dual.reshape(1, -1), increment[None])
 
 

time: 204 us -> 195 us (0.956)
  waiting for transfers between devices: 43.4 us -> 23.4 us
  Pallas kernels: 107 us -> 115 us
  starting transfers between devices: 23.2 us -> 29.4 us
  blocking collectives: 16.3 us -> 14.2 us
    ppermute x8 -> x10, waiting for transfers between devices: 43.4 us -> 23.4 us  [moved(): return lax.ppermute(block, axis, route)]
    pallas_call x5 -> x7, Pallas kernels: 59.5 us -> 67.5 us  [call(): pl.pallas_call(kernel, in_specs=ins, out_specs=specs, out_shape=outs, scr...]
    ppermute x8 -> x10, starting transfers between devices: 23.2 us -> 29.4 us  [moved(): return lax.ppermute(block, axis, route)]
    all_to_all x1, blocking collectives: 16.3 us -> 14.2 us  [shards(): received = lax.all_to_all(sent, ('tm', 'lon'), 0, 0)]
    unnamed x44 -> x52, local copies, waits for them, and re-layouts: 10.6 us -> 9.55 us
  transfers between devices with their start and end apart: 8 -> 10, of which waited for: 5 -> 5; matrix products, arithmetic and copies ran while one was open for 1% -> 1% of each run, Pallas kernels for 49% -> 56%
where the time goes in v4:
time: 195 us
  Pallas kernels  115 us (59%)
  starting transfers between devices  29.4 us (15%)
  waiting for transfers between devices  23.4 us (12%)
  blocking collectives  14.2 us (7%)
  local copies, waits for them, and re-layouts  9.55 us (5%)
    pallas_call x7, Pallas kernels, call(): pl.pallas_call(kernel, in_specs=ins, out_specs=specs, out_shape=outs, scr...  67.5 us
    ppermute x10, starting transfers between devices, moved(): return lax.ppermute(block, axis, route)  29.4 us
    ppermute x10, waiting for transfers between devices, moved(): return lax.ppermute(block, axis, route)  23.4 us
    pallas_call x2, Pallas kernels, observe(): pl.pallas_call(kernel, in_specs=[ANY] * len(parts) + [pl.BlockSpec(memory...  15 us
    all_to_all x1, blocking collectives, shards(): received = lax.all_to_all(sent, ('tm', 'lon'), 0, 0)  14.2 us
    pallas_call x2, Pallas kernels, scatter(): pl.pallas_call(kernel, in_specs=[pl.BlockSpec(memory_space=pltpu.SMEM)] *...  14 us
    unnamed x52, local copies, waits for them, and re-layouts  9.55 us
    pallas_call x1, Pallas kernels, edges_call(): pl.pallas_call(edges_kernel, grid=(rows // BLOCK,), in_specs=[block, bloc...  7.65 us
  transfers between devices with their start and end apart: 10, of which 5 were waited for; matrix products, arithmetic and copies ran while one was open for 1% of the time, Pallas kernels for 56%

profile of v4, /device:TPU:0, one launch (start us, length us, event | category | flops | bytes accessed | tf_op | source)
XLA Modules:
  0.0 194.7 jit_solution(1076080918742190571)
XLA Ops:
  1.9 9.9 %tangent_band.1 = (f32[3,1024,256]{2,1,0:T(8,128)}, f32[3,1024,256]{2,1,0:T(8,128)}) custom-call(f32[3,1024,256]{2,1,0:T(8,128)} %bitcast.22, f32[3,1024,256]{2,1,0:T(8,128)} %bitcast.17, f32[3,1024,256]{2,1,0:T(8,128)} %bitcast.40, bf16[6,1024,256]{2,1,0:T(8,128)(2,1)} %bitcast.29), custom_call_target="tpu_custom_call" | custom-call | flops 1024 | bytes 18874368 | tf_op jit(solution)/shard_map/tangent_band/pallas_call | solution.py:393
  11.9 5.8 %collective-permute-start.4 = (f32[3,1024,256]{2,1,0:T(8,128)}, f32[3,1024,256]{2,1,0:T(8,128)S(1)}, u32[]{:S(2)}, u32[]{:S(2)}) collective-permute-start(f32[3,1024,256]{2,1,0:T(8,128)} %get-tuple-element.30), channel_id=1, source_target_pairs={{0,8},{8,16},{16,24},{1,9},{9,17},{17,25},{2,10},{10,18},{18,26},{... | collective-permute-start | bytes 9437192 | tf_op jit(solution)/shard_map/ppermute | solution.py:921
  18.2 6.9 %scatter.2 = f32[3072,256]{1,0:T(8,128)} custom-call(s32[1024]{0:T(1024)} %bitcast.45, f32[1024]{0:T(1024)} %bitcast.50), custom_call_target="tpu_custom_call" | custom-call | flops 1024 | bytes 3145728 | tf_op jit(solution)/shard_map/scatter/pallas_call | solution.py:740
  25.2 7.6 %edges.1 = (f32[80,1024]{1,0:T(8,128)}, f32[80,1024]{1,0:T(8,128)}) custom-call(f32[3,1024,256]{2,1,0:T(8,128)} %get-tuple-element.23.increment.inc_in.refs_0_.inc0, f32[3,1024,256]{2,1,0:T(8,128)} %bitcast.18, f32[3,1024,256]{2,1,0:T(8,128)} %bitcast.41, bf16[6,1024,256]{2,1,0:T(8,128)(2,1)} %bitcast.30, f32[3,1024,256]{2,1,0:T(8,128)} %bitcast.37), custom_call_target="tpu_custom_call" | custom-call | flops 1024 | bytes 16777216 | tf_op jit(solution)/shard_map/edges/pallas_call | solution.py:87
  32.9 2.6 %collective-permute-start.2 = (f32[80,1024]{1,0:T(8,128)}, f32[80,1024]{1,0:T(8,128)S(1)}, u32[]{:S(2)}, u32[]{:S(2)}) collective-permute-start(f32[80,1024]{1,0:T(8,128)} %get-tuple-element.25), channel_id=1, source_target_pairs={{0,7},{1,0},{2,1},{3,2},{4,3},{5,4},{6,5},{7,6},{8,15},{9,8},{10,9... | collective-permute-start | bytes 983048 | tf_op jit(solution)/shard_map/ppermute | solution.py:921
  35.5 6.1 %collective-permute-done.1.from_left = f32[80,1024]{1,0:T(8,128)S(1)} collective-permute-done((f32[80,1024]{1,0:T(8,128)}, f32[80,1024]{1,0:T(8,128)S(1)}, u32[]{:S(2)}, u32[]{:S(2)}) %collective-permute-start.1) | collective-permute-done | bytes 327712 | tf_op jit(solution)/shard_map/ppermute | solution.py:921
  43.3 13.6 %tangent_seams.1 = (f32[6,32,256]{2,1,0:T(8,128)}, bf16[6,1024,128]{2,1,0:T(8,128)(2,1)}, f32[3,1024,128]{2,1,0:T(8,128)}, f32[24,1024]{1,0:T(8,128)}, f32[3,1024,128]{2,1,0:T(8,128)}) custom-call(f32[3,1024,256]{2,1,0:T(8,128)} %get-tuple-element.23.increment.inc_in.refs_0_.inc0, bf16[6,1024,256]{2,1,0:T(8,128)(2,1)} %bitcast.31, f32[80,1024]{1,0:T(8,128)} %copy-done.23, ...), custom_call_target="tpu_custom_call" | custom-call | flops 1024 | bytes 10485760 | tf_op jit(solution)/shard_map/tangent_seams/pallas_call | solution.py:393
  58.2 4.7 %collective-permute-start.5 = (f32[6,32,256]{2,1,0:T(8,128)}, f32[6,32,256]{2,1,0:T(8,128)S(1)}, u32[]{:S(2)}, u32[]{:S(2)}) collective-permute-start(f32[6,32,256]{2,1,0:T(8,128)} %get-tuple-element.31), channel_id=1, source_target_pairs={{0,8},{8,16},{16,24},{1,9},{9,17},{17,25},{2,10},{10,18},{18,26},{... | collective-permute-start | bytes 589832 | tf_op jit(solution)/shard_map/ppermute | solution.py:921
  63.6 7.4 %observe.2.refs_8_.refs_6_ = f32[8,128]{1,0:T(8,128)} custom-call(f32[3,1024,256]{2,1,0:T(8,128)} %get-tuple-element.23.increment.inc_in.refs_0_.inc0, s32[1024]{0:T(1024)} %bitcast.46, f32[8,128]{1,0:T(8,128)} %fusion.1.refs_2_.refs_3_), custom_call_target="tpu_custom_call" | custom-call | flops 1024 | bytes 3145728 | tf_op jit(solution)/shard_map/observe/pallas_call | solution.py:713
  71.0 5.0 %collective-permute-done.3.refs_5_ = f32[24,1024]{1,0:T(8,128)S(1)} collective-permute-done((f32[24,1024]{1,0:T(8,128)}, f32[24,1024]{1,0:T(8,128)S(1)}, u32[]{:S(2)}, u32[]{:S(2)}) %collective-permute-start.3) | collective-permute-done | bytes 98336 | tf_op jit(solution)/shard_map/ppermute | solution.py:921
  77.7 8.2 %adjoint_first.2.refs_1_.refs_4_.refs_2_.refs_0_ = f32[3,584,256]{2,1,0:T(8,128)} custom-call(f32[3,1024,256]{2,1,0:T(8,128)} %copy-done.19, bf16[6,1024,256]{2,1,0:T(8,128)(2,1)} %bitcast.32, bf16[6,1024,128]{2,1,0:T(8,128)(2,1)} %get-tuple-element.26.refs_2_.refs_5_.refs_6_, f32[3,1024,256]{2,1,0:T(8,128)} %bitcast.38, ...), custom_call_target="tpu_custom_call" | custom-call | flops 1024 | bytes 10485760 | tf_op jit(solution)/shard_map/adjoint_first/pallas_call | solution.py:393
  91.0 8.4 %tangent_second.2 = (f32[3,544,256]{2,1,0:T(8,128)}, f32[3,560,256]{2,1,0:T(8,128)}, f32[3,560,256]{2,1,0:T(8,128)}) custom-call(f32[3,1024,256]{2,1,0:T(8,128)} %copy-done.20, f32[3,584,256]{2,1,0:T(8,128)} %adjoint_first.2.refs_1_.refs_4_.refs_2_.refs_0_, f32[6,32,256]{2,1,0:T(8,128)} %copy-done.21, f32[3,1024,256]{2,1,0:T(8,128)} %bitcast.42, ...), custom_call_target="tpu_custom_call" | custom-call | flops 1024 | bytes 16777216 | tf_op jit(solution)/shard_map/tangent_second/pallas_call | solution.py:393
  99.5 5.5 %collective-permute-start.6 = (f32[3,544,256]{2,1,0:T(8,128)}, f32[3,544,256]{2,1,0:T(8,128)}, u32[]{:S(2)}, u32[]{:S(2)}) collective-permute-start(f32[3,544,256]{2,1,0:T(8,128)} %get-tuple-element.37), channel_id=1, source_target_pairs={{0,8},{8,16},{16,24},{1,9},{9,17},{17,25},{2,10},{10,18},{18,26},{... | collective-permute-start | bytes 5013512 | tf_op jit(solution)/shard_map/ppermute | solution.py:921
  104.9 8.4 %adjoint_first.3.refs_2_.refs_5_.refs_3_.refs_1_ = f32[3,480,256]{2,1,0:T(8,128)} custom-call(f32[3,1024,256]{2,1,0:T(8,128)} %copy-done.19, bf16[6,1024,256]{2,1,0:T(8,128)(2,1)} %bitcast.34, bf16[6,1024,128]{2,1,0:T(8,128)(2,1)} %get-tuple-element.26.refs_2_.refs_5_.refs_6_, f32[3,1024,256]{2,1,0:T(8,128)} %bitcast.39, ...), custom_call_target="tpu_custom_call" | custom-call | flops 1024 | bytes 10485760 | tf_op jit(solution)/shard_map/adjoint_first/pallas_call | solution.py:393
  114.6 8.0 %tangent_second.3 = (f32[3,480,256]{2,1,0:T(8,128)}, f32[3,464,256]{2,1,0:T(8,128)}, f32[3,464,256]{2,1,0:T(8,128)}) custom-call(f32[3,1024,256]{2,1,0:T(8,128)} %copy-done.20, f32[3,584,256]{2,1,0:T(8,128)} %adjoint_first.2.refs_1_.refs_4_.refs_2_.refs_0_, f32[3,480,256]{2,1,0:T(8,128)} %adjoint_first.3.refs_2_.refs_5_.refs_3_.refs_1_, ...), custom_call_target="tpu_custom_call" | custom-call | flops 1024 | bytes 16777216 | tf_op jit(solution)/shard_map/tangent_second/pallas_call | solution.py:393
  122.6 5.7 %collective-permute-start.7 = (f32[3,480,256]{2,1,0:T(8,128)}, f32[3,480,256]{2,1,0:T(8,128)}, u32[]{:S(2)}, u32[]{:S(2)}) collective-permute-start(f32[3,480,256]{2,1,0:T(8,128)} %get-tuple-element.38), channel_id=1, source_target_pairs={{0,8},{8,16},{16,24},{1,9},{9,17},{17,25},{2,10},{10,18},{18,26},{... | collective-permute-start | bytes 4423688 | tf_op jit(solution)/shard_map/ppermute | solution.py:921
  128.9 7.1 %scatter.3 = f32[3072,256]{1,0:T(8,128)} custom-call(s32[1024]{0:T(1024)} %bitcast.47, f32[1024]{0:T(1024)} %divide_bitcast_fusion.values_smem), custom_call_target="tpu_custom_call" | custom-call | flops 1024 | bytes 3145728 | tf_op jit(solution)/shard_map/scatter/pallas_call | solution.py:740
  136.0 7.6 %observe.3.refs_9_ = f32[8,128]{1,0:T(8,128)} custom-call(f32[3,560,256]{2,1,0:T(8,128)} %get-tuple-element.33.refs_0_.refs_2_, f32[3,464,256]{2,1,0:T(8,128)} %get-tuple-element.34.refs_1_.refs_3_, s32[1024]{0:T(1024)} %bitcast.48, f32[8,128]{1,0:T(8,128)} %fusion.1.refs_2_.refs_3_), custom_call_target="tpu_custom_call" | custom-call | flops 1024 | bytes 3145728 | tf_op jit(solution)/shard_map/observe/pallas_call | solution.py:713
  146.9 3.9 %products.1.refs_5_ = f32[6,16,256]{2,1,0:T(8,128)S(1)} custom-call(f32[3,1024,256]{2,1,0:T(8,128)S(1)} %bitcast.23, f32[3,1024,256]{2,1,0:T(8,128)S(1)} %bitcast.20, f32[3,560,256]{2,1,0:T(8,128)S(1)} %copy-done.10, f32[3,464,256]{2,1,0:T(8,128)S(1)} %copy-done.12, f32[3,584,256]{2,1,0:T(8,128)S(1)} %copy-done.2, f32[3,480,256]{2,1,0:T(8,128)S(1)} %copy-done.5), custom_call_target="tpu_custom_call" | custom-call | flops 1024 | bytes 9437184 | tf_op jit(solution)/shard_map/products/pallas_call | solution.py:832
  150.9 9.1 %collective-permute-done.9.refs_1_ = f32[3,480,256]{2,1,0:T(8,128)} collective-permute-done((f32[3,480,256]{2,1,0:T(8,128)}, f32[3,480,256]{2,1,0:T(8,128)}, u32[]{:S(2)}, u32[]{:S(2)}) %collective-permute-start.9) | collective-permute-done | bytes 1474592 | tf_op jit(solution)/shard_map/ppermute | solution.py:921
  160.0 11.1 %adjoint_second.1.refs_6_ = f32[3,16,128]{2,1,0:T(8,128)} custom-call(f32[3,584,256]{2,1,0:T(8,128)} %collective-permute-done.8.refs_0_, f32[3,480,256]{2,1,0:T(8,128)} %collective-permute-done.9.refs_1_, f32[3,584,256]{2,1,0:T(8,128)} %adjoint_first.2.refs_1_.refs_4_.refs_2_.refs_0_, f32[3,480,256]{2,1,0:T(8,128)} %adjoint_first.3.refs_2_.refs_5_.refs_3_.refs_1_, ...), custom_call_target="tpu_custom_call" | custom-call | flops 1024 | bytes 16777216 | tf_op jit(solution)/shard_map/adjoint_second/pallas_call | solution.py:393
  173.3 3.3 %last_products.1 = f32[32,8,128]{2,1,0:T(8,128)S(1)} custom-call(f32[3,1024,256]{2,1,0:T(8,128)S(1)} %bitcast.24, f32[3,560,256]{2,1,0:T(8,128)S(1)} %copy-done.10, f32[3,464,256]{2,1,0:T(8,128)S(1)} %copy-done.13, f32[3,544,256]{2,1,0:T(8,128)} %collective-permute-done.6.refs_3_, f32[3,480,256]{2,1,0:T(8,128)} %collective-permute-done.7.refs_4_, ...), custom_call_target="tpu_custom_call" | custom-call | flops 1024 | bytes 9437184 | tf_op jit(solution)/shard_map/last_products/pallas_call | solution.py:832
  176.6 14.2 %all_to_all.5.refs_4_ = f32[32,8,128]{2,1,0:T(8,128)S(1)} all-to-all(f32[32,8,128]{2,1,0:T(8,128)S(1)} %last_products.1), channel_id=1, replica_groups=mesh['tm'=4,'lon'=8] {'tm','lon'}, dimensions={0} | all-to-all | bytes 262144 | tf_op jit(solution)/shard_map/all_to_all | solution.py:984
  190.8 3.7 %result.1 = (f32[3,1024,256]{2,1,0:T(8,128)}, f32[3,1024,256]{2,1,0:T(8,128)}, f32[8,128]{1,0:T(8,128)}) custom-call(f32[3,1024,256]{2,1,0:T(8,128)S(1)} %bitcast.21, f32[3,1024,256]{2,1,0:T(8,128)S(1)} %copy-done.4, f32[3,584,256]{2,1,0:T(8,128)S(1)} %copy-done.3, f32[3,480,256]{2,1,0:T(8,128)S(1)} %copy-done.6, f32[3,560,256]{2,1,0:T(8,128)S(1)} %copy-done.9, ...), custom_call_target="tpu_custom_call" | custom-call | flops 1024 | bytes 18874368 | tf_op jit(solution)/shard_map/result/pallas_call | solution.py:903
  (67 shorter events, 19.7 us)
Async XLA Ops:
  0.6 75.3 %collective-permute-start = (f32[3,1024,256]{2,1,0:T(8,128)}, f32[3,1024,256]{2,1,0:T(8,128)S(1)}, u32[]{:S(2)}, u32[]{:S(2)}) collective-permute-start(f32[3,1024,256]{2,1,0:T(8,128)} %bitcast.16), channel_id=1, source_target_pairs={{8,0},{16,8},{24,16},{9,1},{17,9},{25,17},{10,2},{18,10},{26,18},{... | collective-permute-start | bytes 9437192 | tf_op jit(solution)/shard_map/ppermute | solution.py:921
  1.9 15.7 %copy-start.16 = (f32[1,1024]{1,0:T(1,128)S(1)}, f32[1,1024]{1,0:T(1,128)}, u32[]{:S(2)}) copy-start(f32[1,1024]{1,0:T(1,128)} %param.8) | copy-start | bytes 12292
  1.9 15.7 %copy-start.17 = (f32[1,1024]{1,0:T(1,128)S(1)}, f32[1,1024]{1,0:T(1,128)}, u32[]{:S(2)}) copy-start(f32[1,1024]{1,0:T(1,128)} %param.11) | copy-start | bytes 12292
  11.9 77.4 %collective-permute-start.4 = (f32[3,1024,256]{2,1,0:T(8,128)}, f32[3,1024,256]{2,1,0:T(8,128)S(1)}, u32[]{:S(2)}, u32[]{:S(2)}) collective-permute-start(f32[3,1024,256]{2,1,0:T(8,128)} %get-tuple-element.30), channel_id=1, source_target_pairs={{0,8},{8,16},{16,24},{1,9},{9,17},{17,25},{2,10},{10,18},{18,26},{... | collective-permute-start | bytes 9437192 | tf_op jit(solution)/shard_map/ppermute | solution.py:921
  32.8 8.8 %collective-permute-start.1 = (f32[80,1024]{1,0:T(8,128)}, f32[80,1024]{1,0:T(8,128)S(1)}, u32[]{:S(2)}, u32[]{:S(2)}) collective-permute-start(f32[80,1024]{1,0:T(8,128)} %get-tuple-element.24), channel_id=1, source_target_pairs={{0,1},{1,2},{2,3},{3,4},{4,5},{5,6},{6,7},{7,0},{8,9},{9,10},{10,1... | collective-permute-start | bytes 983048 | tf_op jit(solution)/shard_map/ppermute | solution.py:921
  32.8 30.1 %copy-start.25 = (s32[1,1024]{1,0:T(1,128)S(1)}, s32[1,1024]{1,0:T(1,128)}, u32[]{:S(2)}) copy-start(s32[1,1024]{1,0:T(1,128)} %param.12) | copy-start | bytes 12292
  32.9 9.8 %collective-permute-start.2 = (f32[80,1024]{1,0:T(8,128)}, f32[80,1024]{1,0:T(8,128)S(1)}, u32[]{:S(2)}, u32[]{:S(2)}) collective-permute-start(f32[80,1024]{1,0:T(8,128)} %get-tuple-element.25), channel_id=1, source_target_pairs={{0,7},{1,0},{2,1},{3,2},{4,3},{5,4},{6,5},{7,6},{8,15},{9,8},{10,9... | collective-permute-start | bytes 983048 | tf_op jit(solution)/shard_map/ppermute | solution.py:921
  56.9 19.1 %collective-permute-start.3 = (f32[24,1024]{1,0:T(8,128)}, f32[24,1024]{1,0:T(8,128)S(1)}, u32[]{:S(2)}, u32[]{:S(2)}) collective-permute-start(f32[24,1024]{1,0:T(8,128)} %get-tuple-element.28), channel_id=1, source_target_pairs={{8,0},{16,8},{24,16},{9,1},{17,9},{25,17},{10,2},{18,10},{26,18},{... | collective-permute-start | bytes 294920 | tf_op jit(solution)/shard_map/ppermute | solution.py:921
  58.2 31.1 %collective-permute-start.5 = (f32[6,32,256]{2,1,0:T(8,128)}, f32[6,32,256]{2,1,0:T(8,128)S(1)}, u32[]{:S(2)}, u32[]{:S(2)}) collective-permute-start(f32[6,32,256]{2,1,0:T(8,128)} %get-tuple-element.31), channel_id=1, source_target_pairs={{0,8},{8,16},{16,24},{1,9},{9,17},{17,25},{2,10},{10,18},{18,26},{... | collective-permute-start | bytes 589832 | tf_op jit(solution)/shard_map/ppermute | solution.py:921
  85.9 74.1 %collective-permute-start.8 = (f32[3,584,256]{2,1,0:T(8,128)}, f32[3,584,256]{2,1,0:T(8,128)}, u32[]{:S(2)}, u32[]{:S(2)}) collective-permute-start(f32[3,584,256]{2,1,0:T(8,128)} %adjoint_first.2.refs_1_.refs_4_.refs_2_.refs_0_), channel_id=1, source_target_pairs={{8,0},{16,8},{24,16},{9,1},{17,9},{25,17},{10,2},{18,10},{26,18},{... | collective-permute-start | bytes 5382152 | tf_op jit(solution)/shard_map/ppermute | solution.py:921
  99.5 71.7 %collective-permute-start.6 = (f32[3,544,256]{2,1,0:T(8,128)}, f32[3,544,256]{2,1,0:T(8,128)}, u32[]{:S(2)}, u32[]{:S(2)}) collective-permute-start(f32[3,544,256]{2,1,0:T(8,128)} %get-tuple-element.37), channel_id=1, source_target_pairs={{0,8},{8,16},{16,24},{1,9},{9,17},{17,25},{2,10},{10,18},{18,26},{... | collective-permute-start | bytes 5013512 | tf_op jit(solution)/shard_map/ppermute | solution.py:921
  113.3 15.0 %copy-start.15 = (f32[8,128]{1,0:T(8,128)S(1)}, f32[8,128]{1,0:T(8,128)}, u32[]{:S(2)}) copy-start(f32[8,128]{1,0:T(8,128)} %observe.2.refs_8_.refs_6_) | copy-start | bytes 12292
  113.3 46.7 %collective-permute-start.9 = (f32[3,480,256]{2,1,0:T(8,128)}, f32[3,480,256]{2,1,0:T(8,128)}, u32[]{:S(2)}, u32[]{:S(2)}) collective-permute-start(f32[3,480,256]{2,1,0:T(8,128)} %adjoint_first.3.refs_2_.refs_5_.refs_3_.refs_1_), channel_id=1, source_target_pairs={{8,0},{16,8},{24,16},{9,1},{17,9},{25,17},{10,2},{18,10},{26,18},{... | collective-permute-start | bytes 4423688 | tf_op jit(solution)/shard_map/ppermute | solution.py:921
  114.6 29.0 %copy-start.5 = (f32[3,480,256]{2,1,0:T(8,128)S(1)}, f32[3,480,256]{2,1,0:T(8,128)}, u32[]{:S(2)}) copy-start(f32[3,480,256]{2,1,0:T(8,128)} %adjoint_first.3.refs_2_.refs_5_.refs_3_.refs_1_) | copy-start | bytes 4423684
  114.6 29.0 %copy-start.10 = (f32[3,560,256]{2,1,0:T(8,128)S(1)}, f32[3,560,256]{2,1,0:T(8,128)}, u32[]{:S(2)}) copy-start(f32[3,560,256]{2,1,0:T(8,128)} %get-tuple-element.35.refs_2_.refs_1_) | copy-start | bytes 5160964
  122.6 48.5 %collective-permute-start.7 = (f32[3,480,256]{2,1,0:T(8,128)}, f32[3,480,256]{2,1,0:T(8,128)}, u32[]{:S(2)}, u32[]{:S(2)}) collective-permute-start(f32[3,480,256]{2,1,0:T(8,128)} %get-tuple-element.38), channel_id=1, source_target_pairs={{0,8},{8,16},{16,24},{1,9},{9,17},{17,25},{2,10},{10,18},{18,26},{... | collective-permute-start | bytes 4423688 | tf_op jit(solution)/shard_map/ppermute | solution.py:921
  128.9 14.8 %copy-start.2 = (f32[3,584,256]{2,1,0:T(8,128)S(1)}, f32[3,584,256]{2,1,0:T(8,128)}, u32[]{:S(2)}) copy-start(f32[3,584,256]{2,1,0:T(8,128)} %adjoint_first.2.refs_1_.refs_4_.refs_2_.refs_0_) | copy-start | bytes 5382148
  160.0 11.2 %copy-start.18 = (f32[8,128]{1,0:T(8,128)S(1)}, f32[8,128]{1,0:T(8,128)}, u32[]{:S(2)}) copy-start(f32[8,128]{1,0:T(8,128)} %observe.3.refs_9_) | copy-start | bytes 12292
  160.0 30.8 %copy-start.9 = (f32[3,560,256]{2,1,0:T(8,128)S(1)}, f32[3,560,256]{2,1,0:T(8,128)}, u32[]{:S(2)}) copy-start(f32[3,560,256]{2,1,0:T(8,128)} %get-tuple-element.33.refs_0_.refs_2_) | copy-start | bytes 5160964
  160.0 30.8 %copy-start.11 = (f32[3,464,256]{2,1,0:T(8,128)S(1)}, f32[3,464,256]{2,1,0:T(8,128)}, u32[]{:S(2)}) copy-start(f32[3,464,256]{2,1,0:T(8,128)} %get-tuple-element.34.refs_1_.refs_3_) | copy-start | bytes 4276228
  173.3 17.5 %copy-start.1 = (f32[1,3,1024,256]{3,2,1,0:T(8,128)S(1)}, f32[1,3,1024,256]{3,2,1,0:T(8,128)}, u32[]{:S(2)}) copy-start(f32[1,3,1024,256]{3,2,1,0:T(8,128)} %param.13) | copy-start | bytes 9437188
  173.3 17.5 %copy-start.3 = (f32[3,584,256]{2,1,0:T(8,128)S(1)}, f32[3,584,256]{2,1,0:T(8,128)}, u32[]{:S(2)}) copy-start(f32[3,584,256]{2,1,0:T(8,128)} %adjoint_first.2.refs_1_.refs_4_.refs_2_.refs_0_) | copy-start | bytes 5382148
  173.3 17.5 %copy-start.4 = (f32[3,1024,256]{2,1,0:T(8,128)S(1)}, f32[3,1024,256]{2,1,0:T(8,128)}, u32[]{:S(2)}) copy-start(f32[3,1024,256]{2,1,0:T(8,128)} %get-tuple-element.23.increment.inc_in.refs_0_.inc0) | copy-start | bytes 9437188
  173.3 17.5 %copy-start.6 = (f32[3,480,256]{2,1,0:T(8,128)S(1)}, f32[3,480,256]{2,1,0:T(8,128)}, u32[]{:S(2)}) copy-start(f32[3,480,256]{2,1,0:T(8,128)} %adjoint_first.3.refs_2_.refs_5_.refs_3_.refs_1_) | copy-start | bytes 4423684
  (12 other events, 30.6 us)

commit v5 on v4

--- a/solution.py
+++ b/solution.py
@@ -11,6 +11,7 @@
 
 LANE = 128
 BLOCK = 256
+SEGMENT = 128
 GROUP = 16
 SHARE = 9
 MARGIN = 8
@@ -291,7 +292,7 @@
 
 
 def segments(total):
-    return [(at, min(at + BLOCK, total)) for at in range(0, total, BLOCK)]
+    return [(at, min(at + SEGMENT, total)) for at in range(0, total, SEGMENT)]
 
 
 def fetch(copies, begin, end, *pairs):
@@ -634,7 +635,9 @@
     )
 
 
-def adjoint_second(later, traj, traj_halo, spread, last, pulled):
+def adjoint_second(span, later, traj, traj_halo, spread, last, pulled):
+    base, end, out_begin, out_end = span
+    held, rows = end - base, out_end - out_begin
     _, total, columns = last.shape
     n_later, n_pulled = len(later), len(pulled)
 
@@ -646,35 +649,35 @@
         folds, sems = refs[16:-1], refs[-1]
         copies = Copies(sems)
         edge_copies = unfold_parts(copies, later_in, folds)
-        ready = fetch(copies, 0, total, (later_in, field), *whole_of(total, (traj_in, traj), (traj_halo_in, traj_halo)))
-        begin_put = fetch(copies, 0, total, (pulled_in, pull), *whole_of(total, (spread_in, spread), (last_in, last)))
+        ready = fetch(copies, base, end, (later_in, field), *whole_of(total, (traj_in, traj), (traj_halo_in, traj_halo)))
+        begin_put = fetch(copies, out_begin, out_end, (pulled_in, pull), *whole_of(total, (spread_in, spread), (last_in, last)))
         wait(edge_copies)
         unfold_all(later_in, folds, own)
         sums[...] = jnp.zeros_like(sums)
+        skip = base - out_begin
 
         def get(s):
-            lanes = own[rows_at(s), :]
+            lanes = own[rows_at(s, base), :]
             return [[tile_of(field, f, s, t) for t in range(2)] + [halo_of(lanes, f)] for f in range(3)]
 
         def put(s, new):
             parts = [jnp.zeros((GROUP, LANE), F32)] * 3
             for f in range(3):
                 for t in range(2):
-                    value = tile_of(spread, f, s, t) - new[f][t]
-                    for k, other in enumerate((tile_of(last, f, s, t), tile_of(pull, f, s, t), value)):
+                    value = tile_of(spread, f, s, t, skip) - new[f][t]
+                    for k, other in enumerate((tile_of(last, f, s, t, skip), tile_of(pull, f, s, t, skip), value)):
                         parts[k] = parts[k] + other * value
             for k in range(3):
                 sums[k] = sums[k] + parts[k]
 
-        span = (0, total, 0, total)
         run_adjoint(
             span, total, get, ready, traj, traj_halo, wide_a, wide_b, flux_a, flux_b, put, begin_put, lambda low, high: None
         )
 
-    scratch = [vmem(3, total, columns), vmem(6, total, columns, dtype=traj.dtype), vmem(6, total, LANE, dtype=traj.dtype)]
-    scratch += [vmem(3, total, columns)] * 3 + [wide_scratch(total)] * 4 + [vmem(total + 2 * LANE, LANE)]
+    scratch = [vmem(3, held, columns), vmem(6, held, columns, dtype=traj.dtype), vmem(6, held, LANE, dtype=traj.dtype)]
+    scratch += [vmem(3, rows, columns)] * 3 + [wide_scratch(held)] * 4 + [vmem(total + 2 * LANE, LANE)]
     scratch += [vmem(3, extra(p[2]), columns) for p in later]
-    scratch += [pltpu.SemaphoreType.DMA(((4 + n_later + n_pulled) * len(segments(total)) + n_later,))]
+    scratch += [pltpu.SemaphoreType.DMA(((4 + n_later + n_pulled) * len(segments(held)) + n_later,))]
     outs = [f32(3, GROUP, LANE)]
     return call(
         "adjoint_second", kernel, [ANY] * (n_later + n_pulled + 4), outs, scratch, 16,
@@ -972,7 +975,9 @@
     early = row_products(
         ((0, 0), (1, 1), (0, 2), (1, 3), (2, 2), (3, 3)), ([part(first, 0)], [part(last, 0)], a1, d1), 0, total
     )
-    d_sums = [adjoint_second(d1_later, traj, traj_halo, z1, last, d1)]
+    d_sums = [
+        adjoint_second(second, d1_later[: c + 1], traj, traj_halo, z1, last, d1) for c, second in enumerate(seconds)
+    ]
     devices = lax.axis_size("tm") * lax.axis_size("lon")
     sent = row_products(
         ((0, 2), (1, 2), (2, 2)),

time: 195 us -> 194 us (level)
    pallas_call x7 -> x8, Pallas kernels: 67.5 us -> 67.3 us  [call(): pl.pallas_call(kernel, in_specs=ins, out_specs=specs, out_shape=outs, scr...]
    unnamed x52 -> x54, local copies, waits for them, and re-layouts: 9.55 us -> 9.55 us
  transfers between devices with their start and end apart: 10 -> 10, of which waited for: 5 -> 6; matrix products, arithmetic and copies ran while one was open for 1% -> 1% of each run, Pallas kernels for 56% -> 56%
where the time goes in v5:
time: 194 us
  Pallas kernels  115 us (59%)
  starting transfers between devices  29.5 us (15%)
  waiting for transfers between devices  21.8 us (11%)
  blocking collectives  14.8 us (8%)
  local copies, waits for them, and re-layouts  9.55 us (5%)
    pallas_call x8, Pallas kernels, call(): pl.pallas_call(kernel, in_specs=ins, out_specs=specs, out_shape=outs, scr...  67.3 us
    ppermute x10, starting transfers between devices, moved(): return lax.ppermute(block, axis, route)  29.5 us
    ppermute x10, waiting for transfers between devices, moved(): return lax.ppermute(block, axis, route)  21.8 us
    pallas_call x2, Pallas kernels, observe(): pl.pallas_call(kernel, in_specs=[ANY] * len(parts) + [pl.BlockSpec(memory...  15 us
    all_to_all x1, blocking collectives, shards(): received = lax.all_to_all(sent, ('tm', 'lon'), 0, 0)  14.8 us
    pallas_call x2, Pallas kernels, scatter(): pl.pallas_call(kernel, in_specs=[pl.BlockSpec(memory_space=pltpu.SMEM)] *...  14.1 us
    unnamed x54, local copies, waits for them, and re-layouts  9.55 us
    pallas_call x1, Pallas kernels, edges_call(): pl.pallas_call(edges_kernel, grid=(rows // BLOCK,), in_specs=[block, bloc...  7.65 us
  transfers between devices with their start and end apart: 10, of which 6 were waited for; matrix products, arithmetic and copies ran while one was open for 1% of the time, Pallas kernels for 56%

profile of v5, /device:TPU:0, one launch (start us, length us, event | category | flops | bytes accessed | tf_op | source)
XLA Modules:
  0.0 193.6 jit_solution(1288729572152208228)
XLA Ops:
  1.9 9.4 %tangent_band.1 = (f32[3,1024,256]{2,1,0:T(8,128)}, f32[3,1024,256]{2,1,0:T(8,128)}) custom-call(f32[3,1024,256]{2,1,0:T(8,128)} %bitcast.23, f32[3,1024,256]{2,1,0:T(8,128)} %bitcast.17, f32[3,1024,256]{2,1,0:T(8,128)} %bitcast.42, bf16[6,1024,256]{2,1,0:T(8,128)(2,1)} %bitcast.30), custom_call_target="tpu_custom_call" | custom-call | flops 1024 | bytes 18874368 | tf_op jit(solution)/shard_map/tangent_band/pallas_call | solution.py:394
  11.3 5.8 %collective-permute-start.4 = (f32[3,1024,256]{2,1,0:T(8,128)}, f32[3,1024,256]{2,1,0:T(8,128)S(1)}, u32[]{:S(2)}, u32[]{:S(2)}) collective-permute-start(f32[3,1024,256]{2,1,0:T(8,128)} %get-tuple-element.30), channel_id=1, source_target_pairs={{0,8},{8,16},{16,24},{1,9},{9,17},{17,25},{2,10},{10,18},{18,26},{... | collective-permute-start | bytes 9437192 | tf_op jit(solution)/shard_map/ppermute | solution.py:924
  17.7 7.0 %scatter.2 = f32[3072,256]{1,0:T(8,128)} custom-call(s32[1024]{0:T(1024)} %bitcast.48, f32[1024]{0:T(1024)} %bitcast.53), custom_call_target="tpu_custom_call" | custom-call | flops 1024 | bytes 3145728 | tf_op jit(solution)/shard_map/scatter/pallas_call | solution.py:743
  24.7 7.6 %edges.1 = (f32[80,1024]{1,0:T(8,128)}, f32[80,1024]{1,0:T(8,128)}) custom-call(f32[3,1024,256]{2,1,0:T(8,128)} %get-tuple-element.23.increment.inc_in.refs_0_.inc0, f32[3,1024,256]{2,1,0:T(8,128)} %bitcast.18, f32[3,1024,256]{2,1,0:T(8,128)} %bitcast.43, bf16[6,1024,256]{2,1,0:T(8,128)(2,1)} %bitcast.31, f32[3,1024,256]{2,1,0:T(8,128)} %bitcast.39), custom_call_target="tpu_custom_call" | custom-call | flops 1024 | bytes 16777216 | tf_op jit(solution)/shard_map/edges/pallas_call | solution.py:88
  35.0 6.1 %collective-permute-done.1.from_left = f32[80,1024]{1,0:T(8,128)S(1)} collective-permute-done((f32[80,1024]{1,0:T(8,128)}, f32[80,1024]{1,0:T(8,128)S(1)}, u32[]{:S(2)}, u32[]{:S(2)}) %collective-permute-start.1) | collective-permute-done | bytes 327712 | tf_op jit(solution)/shard_map/ppermute | solution.py:924
  42.8 10.9 %tangent_seams.1 = (f32[6,32,256]{2,1,0:T(8,128)}, bf16[6,1024,128]{2,1,0:T(8,128)(2,1)}, f32[3,1024,128]{2,1,0:T(8,128)}, f32[24,1024]{1,0:T(8,128)}, f32[3,1024,128]{2,1,0:T(8,128)}) custom-call(f32[3,1024,256]{2,1,0:T(8,128)} %get-tuple-element.23.increment.inc_in.refs_0_.inc0, bf16[6,1024,256]{2,1,0:T(8,128)(2,1)} %bitcast.32, f32[80,1024]{1,0:T(8,128)} %copy-done.24, ...), custom_call_target="tpu_custom_call" | custom-call | flops 1024 | bytes 10485760 | tf_op jit(solution)/shard_map/tangent_seams/pallas_call | solution.py:394
  55.0 4.6 %collective-permute-start.5 = (f32[6,32,256]{2,1,0:T(8,128)}, f32[6,32,256]{2,1,0:T(8,128)S(1)}, u32[]{:S(2)}, u32[]{:S(2)}) collective-permute-start(f32[6,32,256]{2,1,0:T(8,128)} %get-tuple-element.31), channel_id=1, source_target_pairs={{0,8},{8,16},{16,24},{1,9},{9,17},{17,25},{2,10},{10,18},{18,26},{... | collective-permute-start | bytes 589832 | tf_op jit(solution)/shard_map/ppermute | solution.py:924
  60.2 7.4 %observe.2.refs_9_.refs_6_ = f32[8,128]{1,0:T(8,128)} custom-call(f32[3,1024,256]{2,1,0:T(8,128)} %get-tuple-element.23.increment.inc_in.refs_0_.inc0, s32[1024]{0:T(1024)} %bitcast.49, f32[8,128]{1,0:T(8,128)} %fusion.1.refs_2_.refs_3_), custom_call_target="tpu_custom_call" | custom-call | flops 1024 | bytes 3145728 | tf_op jit(solution)/shard_map/observe/pallas_call | solution.py:716
  67.6 8.4 %collective-permute-done.3.refs_5_ = f32[24,1024]{1,0:T(8,128)S(1)} collective-permute-done((f32[24,1024]{1,0:T(8,128)}, f32[24,1024]{1,0:T(8,128)S(1)}, u32[]{:S(2)}, u32[]{:S(2)}) %collective-permute-start.3) | collective-permute-done | bytes 98336 | tf_op jit(solution)/shard_map/ppermute | solution.py:924
  77.7 8.1 %adjoint_first.2.refs_1_.refs_4_.refs_2_.refs_0_ = f32[3,584,256]{2,1,0:T(8,128)} custom-call(f32[3,1024,256]{2,1,0:T(8,128)} %copy-done.20, bf16[6,1024,256]{2,1,0:T(8,128)(2,1)} %bitcast.33, bf16[6,1024,128]{2,1,0:T(8,128)(2,1)} %get-tuple-element.26.refs_2_.refs_5_.refs_6_.refs_4_, f32[3,1024,256]{2,1,0:T(8,128)} %bitcast.40, ...), custom_call_target="tpu_custom_call" | custom-call | flops 1024 | bytes 10485760 | tf_op jit(solution)/shard_map/adjoint_first/pallas_call | solution.py:394
  90.5 7.8 %tangent_second.2 = (f32[3,544,256]{2,1,0:T(8,128)}, f32[3,560,256]{2,1,0:T(8,128)}, f32[3,560,256]{2,1,0:T(8,128)}) custom-call(f32[3,1024,256]{2,1,0:T(8,128)} %copy-done.21, f32[3,584,256]{2,1,0:T(8,128)} %adjoint_first.2.refs_1_.refs_4_.refs_2_.refs_0_, f32[6,32,256]{2,1,0:T(8,128)} %copy-done.22, f32[3,1024,256]{2,1,0:T(8,128)} %bitcast.44, ...), custom_call_target="tpu_custom_call" | custom-call | flops 1024 | bytes 16777216 | tf_op jit(solution)/shard_map/tangent_second/pallas_call | solution.py:394
  98.3 5.5 %collective-permute-start.6 = (f32[3,544,256]{2,1,0:T(8,128)}, f32[3,544,256]{2,1,0:T(8,128)}, u32[]{:S(2)}, u32[]{:S(2)}) collective-permute-start(f32[3,544,256]{2,1,0:T(8,128)} %get-tuple-element.37), channel_id=1, source_target_pairs={{0,8},{8,16},{16,24},{1,9},{9,17},{17,25},{2,10},{10,18},{18,26},{... | collective-permute-start | bytes 5013512 | tf_op jit(solution)/shard_map/ppermute | solution.py:924
  103.8 7.1 %adjoint_first.3.refs_2_.refs_5_.refs_3_.refs_1_ = f32[3,480,256]{2,1,0:T(8,128)} custom-call(f32[3,1024,256]{2,1,0:T(8,128)} %copy-done.20, bf16[6,1024,256]{2,1,0:T(8,128)(2,1)} %bitcast.35, bf16[6,1024,128]{2,1,0:T(8,128)(2,1)} %get-tuple-element.26.refs_2_.refs_5_.refs_6_.refs_4_, f32[3,1024,256]{2,1,0:T(8,128)} %bitcast.41, ...), custom_call_target="tpu_custom_call" | custom-call | flops 1024 | bytes 10485760 | tf_op jit(solution)/shard_map/adjoint_first/pallas_call | solution.py:394
  112.2 8.2 %tangent_second.3 = (f32[3,480,256]{2,1,0:T(8,128)}, f32[3,464,256]{2,1,0:T(8,128)}, f32[3,464,256]{2,1,0:T(8,128)}) custom-call(f32[3,1024,256]{2,1,0:T(8,128)} %copy-done.21, f32[3,584,256]{2,1,0:T(8,128)} %adjoint_first.2.refs_1_.refs_4_.refs_2_.refs_0_, f32[3,480,256]{2,1,0:T(8,128)} %adjoint_first.3.refs_2_.refs_5_.refs_3_.refs_1_, ...), custom_call_target="tpu_custom_call" | custom-call | flops 1024 | bytes 16777216 | tf_op jit(solution)/shard_map/tangent_second/pallas_call | solution.py:394
  120.4 5.7 %collective-permute-start.7 = (f32[3,480,256]{2,1,0:T(8,128)}, f32[3,480,256]{2,1,0:T(8,128)}, u32[]{:S(2)}, u32[]{:S(2)}) collective-permute-start(f32[3,480,256]{2,1,0:T(8,128)} %get-tuple-element.38), channel_id=1, source_target_pairs={{0,8},{8,16},{16,24},{1,9},{9,17},{17,25},{2,10},{10,18},{18,26},{... | collective-permute-start | bytes 4423688 | tf_op jit(solution)/shard_map/ppermute | solution.py:924
  126.7 7.1 %scatter.3 = f32[3072,256]{1,0:T(8,128)} custom-call(s32[1024]{0:T(1024)} %bitcast.50, f32[1024]{0:T(1024)} %divide_bitcast_fusion.values_smem), custom_call_target="tpu_custom_call" | custom-call | flops 1024 | bytes 3145728 | tf_op jit(solution)/shard_map/scatter/pallas_call | solution.py:743
  133.8 7.6 %observe.3.refs_10_ = f32[8,128]{1,0:T(8,128)} custom-call(f32[3,560,256]{2,1,0:T(8,128)} %get-tuple-element.33.refs_0_.refs_2_, f32[3,464,256]{2,1,0:T(8,128)} %get-tuple-element.34.refs_1_.refs_3_, s32[1024]{0:T(1024)} %bitcast.51, f32[8,128]{1,0:T(8,128)} %fusion.1.refs_2_.refs_3_), custom_call_target="tpu_custom_call" | custom-call | flops 1024 | bytes 3145728 | tf_op jit(solution)/shard_map/observe/pallas_call | solution.py:716
  144.7 3.9 %products.1.refs_5_ = f32[6,16,256]{2,1,0:T(8,128)S(1)} custom-call(f32[3,1024,256]{2,1,0:T(8,128)S(1)} %bitcast.24, f32[3,1024,256]{2,1,0:T(8,128)S(1)} %bitcast.21, f32[3,560,256]{2,1,0:T(8,128)S(1)} %copy-done.9, f32[3,464,256]{2,1,0:T(8,128)S(1)} %copy-done.12, f32[3,584,256]{2,1,0:T(8,128)S(1)} %copy-done.2, f32[3,480,256]{2,1,0:T(8,128)S(1)} %copy-done.4), custom_call_target="tpu_custom_call" | custom-call | flops 1024 | bytes 9437184 | tf_op jit(solution)/shard_map/products/pallas_call | solution.py:835
  148.7 7.0 %adjoint_second.2.refs_6_ = f32[3,16,128]{2,1,0:T(8,128)} custom-call(f32[3,584,256]{2,1,0:T(8,128)} %collective-permute-done.8.refs_0_, f32[3,584,256]{2,1,0:T(8,128)} %adjoint_first.2.refs_1_.refs_4_.refs_2_.refs_0_, f32[3,480,256]{2,1,0:T(8,128)} %adjoint_first.3.refs_2_.refs_5_.refs_3_.refs_1_, bf16[6,1024,256]{2,1,0:T(8,128)(2,1)} %bitcast.37, ...), custom_call_target="tpu_custom_call" | custom-call | flops 1024 | bytes 16777216 | tf_op jit(solution)/shard_map/adjoint_second/pallas_call | solution.py:394
  155.7 4.2 %collective-permute-done.9.refs_1_ = f32[3,480,256]{2,1,0:T(8,128)} collective-permute-done((f32[3,480,256]{2,1,0:T(8,128)}, f32[3,480,256]{2,1,0:T(8,128)}, u32[]{:S(2)}, u32[]{:S(2)}) %collective-permute-start.9) | collective-permute-done | bytes 1474592 | tf_op jit(solution)/shard_map/ppermute | solution.py:924
  159.9 8.8 %adjoint_second.3.refs_7_ = f32[3,16,128]{2,1,0:T(8,128)} custom-call(f32[3,584,256]{2,1,0:T(8,128)} %collective-permute-done.8.refs_0_, f32[3,480,256]{2,1,0:T(8,128)} %collective-permute-done.9.refs_1_, f32[3,584,256]{2,1,0:T(8,128)} %adjoint_first.2.refs_1_.refs_4_.refs_2_.refs_0_, f32[3,480,256]{2,1,0:T(8,128)} %adjoint_first.3.refs_2_.refs_5_.refs_3_.refs_1_, ...), custom_call_target="tpu_custom_call" | custom-call | flops 1024 | bytes 16777216 | tf_op jit(solution)/shard_map/adjoint_second/pallas_call | solution.py:394
  171.5 3.3 %last_products.1 = f32[32,8,128]{2,1,0:T(8,128)S(1)} custom-call(f32[3,1024,256]{2,1,0:T(8,128)S(1)} %bitcast.25, f32[3,560,256]{2,1,0:T(8,128)S(1)} %copy-done.9, f32[3,464,256]{2,1,0:T(8,128)S(1)} %copy-done.13, f32[3,544,256]{2,1,0:T(8,128)} %collective-permute-done.6.refs_3_, f32[3,480,256]{2,1,0:T(8,128)} %collective-permute-done.7.refs_4_, ...), custom_call_target="tpu_custom_call" | custom-call | flops 1024 | bytes 9437184 | tf_op jit(solution)/shard_map/last_products/pallas_call | solution.py:835
  174.8 14.8 %all_to_all.5.refs_4_ = f32[32,8,128]{2,1,0:T(8,128)S(1)} all-to-all(f32[32,8,128]{2,1,0:T(8,128)S(1)} %last_products.1), channel_id=1, replica_groups=mesh['tm'=4,'lon'=8] {'tm','lon'}, dimensions={0} | all-to-all | bytes 262144 | tf_op jit(solution)/shard_map/all_to_all | solution.py:989
  189.7 3.7 %result.1 = (f32[3,1024,256]{2,1,0:T(8,128)}, f32[3,1024,256]{2,1,0:T(8,128)}, f32[8,128]{1,0:T(8,128)}) custom-call(f32[3,1024,256]{2,1,0:T(8,128)S(1)} %bitcast.22, f32[3,1024,256]{2,1,0:T(8,128)S(1)} %copy-done.6, f32[3,584,256]{2,1,0:T(8,128)S(1)} %copy-done.3, f32[3,480,256]{2,1,0:T(8,128)S(1)} %copy-done.5, f32[3,560,256]{2,1,0:T(8,128)S(1)} %copy-done.10, ...), custom_call_target="tpu_custom_call" | custom-call | flops 1024 | bytes 18874368 | tf_op jit(solution)/shard_map/result/pallas_call | solution.py:906
  (70 shorter events, 22.5 us)
Async XLA Ops:
  0.6 75.3 %collective-permute-start = (f32[3,1024,256]{2,1,0:T(8,128)}, f32[3,1024,256]{2,1,0:T(8,128)S(1)}, u32[]{:S(2)}, u32[]{:S(2)}) collective-permute-start(f32[3,1024,256]{2,1,0:T(8,128)} %bitcast.16), channel_id=1, source_target_pairs={{8,0},{16,8},{24,16},{9,1},{17,9},{25,17},{10,2},{18,10},{26,18},{... | collective-permute-start | bytes 9437192 | tf_op jit(solution)/shard_map/ppermute | solution.py:924
  1.9 15.1 %copy-start.17 = (f32[1,1024]{1,0:T(1,128)S(1)}, f32[1,1024]{1,0:T(1,128)}, u32[]{:S(2)}) copy-start(f32[1,1024]{1,0:T(1,128)} %param.8) | copy-start | bytes 12292
  1.9 15.1 %copy-start.18 = (f32[1,1024]{1,0:T(1,128)S(1)}, f32[1,1024]{1,0:T(1,128)}, u32[]{:S(2)}) copy-start(f32[1,1024]{1,0:T(1,128)} %param.11) | copy-start | bytes 12292
  11.3 77.4 %collective-permute-start.4 = (f32[3,1024,256]{2,1,0:T(8,128)}, f32[3,1024,256]{2,1,0:T(8,128)S(1)}, u32[]{:S(2)}, u32[]{:S(2)}) collective-permute-start(f32[3,1024,256]{2,1,0:T(8,128)} %get-tuple-element.30), channel_id=1, source_target_pairs={{0,8},{8,16},{16,24},{1,9},{9,17},{17,25},{2,10},{10,18},{18,26},{... | collective-permute-start | bytes 9437192 | tf_op jit(solution)/shard_map/ppermute | solution.py:924
  32.3 8.8 %collective-permute-start.1 = (f32[80,1024]{1,0:T(8,128)}, f32[80,1024]{1,0:T(8,128)S(1)}, u32[]{:S(2)}, u32[]{:S(2)}) collective-permute-start(f32[80,1024]{1,0:T(8,128)} %get-tuple-element.24), channel_id=1, source_target_pairs={{0,1},{1,2},{2,3},{3,4},{4,5},{5,6},{6,7},{7,0},{8,9},{9,10},{10,1... | collective-permute-start | bytes 983048 | tf_op jit(solution)/shard_map/ppermute | solution.py:924
  32.3 27.3 %copy-start.26 = (s32[1,1024]{1,0:T(1,128)S(1)}, s32[1,1024]{1,0:T(1,128)}, u32[]{:S(2)}) copy-start(s32[1,1024]{1,0:T(1,128)} %param.12) | copy-start | bytes 12292
  32.3 9.8 %collective-permute-start.2 = (f32[80,1024]{1,0:T(8,128)}, f32[80,1024]{1,0:T(8,128)S(1)}, u32[]{:S(2)}, u32[]{:S(2)}) collective-permute-start(f32[80,1024]{1,0:T(8,128)} %get-tuple-element.25), channel_id=1, source_target_pairs={{0,7},{1,0},{2,1},{3,2},{4,3},{5,4},{6,5},{7,6},{8,15},{9,8},{10,9... | collective-permute-start | bytes 983048 | tf_op jit(solution)/shard_map/ppermute | solution.py:924
  53.7 22.3 %collective-permute-start.3 = (f32[24,1024]{1,0:T(8,128)}, f32[24,1024]{1,0:T(8,128)S(1)}, u32[]{:S(2)}, u32[]{:S(2)}) collective-permute-start(f32[24,1024]{1,0:T(8,128)} %get-tuple-element.28), channel_id=1, source_target_pairs={{8,0},{16,8},{24,16},{9,1},{17,9},{25,17},{10,2},{18,10},{26,18},{... | collective-permute-start | bytes 294920 | tf_op jit(solution)/shard_map/ppermute | solution.py:924
  55.0 33.7 %collective-permute-start.5 = (f32[6,32,256]{2,1,0:T(8,128)}, f32[6,32,256]{2,1,0:T(8,128)S(1)}, u32[]{:S(2)}, u32[]{:S(2)}) collective-permute-start(f32[6,32,256]{2,1,0:T(8,128)} %get-tuple-element.31), channel_id=1, source_target_pairs={{0,8},{8,16},{16,24},{1,9},{9,17},{17,25},{2,10},{10,18},{18,26},{... | collective-permute-start | bytes 589832 | tf_op jit(solution)/shard_map/ppermute | solution.py:924
  85.8 62.9 %collective-permute-start.8 = (f32[3,584,256]{2,1,0:T(8,128)}, f32[3,584,256]{2,1,0:T(8,128)}, u32[]{:S(2)}, u32[]{:S(2)}) collective-permute-start(f32[3,584,256]{2,1,0:T(8,128)} %adjoint_first.2.refs_1_.refs_4_.refs_2_.refs_0_), channel_id=1, source_target_pairs={{8,0},{16,8},{24,16},{9,1},{17,9},{25,17},{10,2},{18,10},{26,18},{... | collective-permute-start | bytes 5382152 | tf_op jit(solution)/shard_map/ppermute | solution.py:924
  98.3 71.1 %collective-permute-start.6 = (f32[3,544,256]{2,1,0:T(8,128)}, f32[3,544,256]{2,1,0:T(8,128)}, u32[]{:S(2)}, u32[]{:S(2)}) collective-permute-start(f32[3,544,256]{2,1,0:T(8,128)} %get-tuple-element.37), channel_id=1, source_target_pairs={{0,8},{8,16},{16,24},{1,9},{9,17},{17,25},{2,10},{10,18},{18,26},{... | collective-permute-start | bytes 5013512 | tf_op jit(solution)/shard_map/ppermute | solution.py:924
  110.8 15.2 %copy-start.16 = (f32[8,128]{1,0:T(8,128)S(1)}, f32[8,128]{1,0:T(8,128)}, u32[]{:S(2)}) copy-start(f32[8,128]{1,0:T(8,128)} %observe.2.refs_9_.refs_6_) | copy-start | bytes 12292
  110.9 49.0 %collective-permute-start.9 = (f32[3,480,256]{2,1,0:T(8,128)}, f32[3,480,256]{2,1,0:T(8,128)}, u32[]{:S(2)}, u32[]{:S(2)}) collective-permute-start(f32[3,480,256]{2,1,0:T(8,128)} %adjoint_first.3.refs_2_.refs_5_.refs_3_.refs_1_), channel_id=1, source_target_pairs={{8,0},{16,8},{24,16},{9,1},{17,9},{25,17},{10,2},{18,10},{26,18},{... | collective-permute-start | bytes 4423688 | tf_op jit(solution)/shard_map/ppermute | solution.py:924
  112.2 29.3 %copy-start.4 = (f32[3,480,256]{2,1,0:T(8,128)S(1)}, f32[3,480,256]{2,1,0:T(8,128)}, u32[]{:S(2)}) copy-start(f32[3,480,256]{2,1,0:T(8,128)} %adjoint_first.3.refs_2_.refs_5_.refs_3_.refs_1_) | copy-start | bytes 4423684
  112.2 29.3 %copy-start.9 = (f32[3,560,256]{2,1,0:T(8,128)S(1)}, f32[3,560,256]{2,1,0:T(8,128)}, u32[]{:S(2)}) copy-start(f32[3,560,256]{2,1,0:T(8,128)} %get-tuple-element.35.refs_2_.refs_1_) | copy-start | bytes 5160964
  120.4 49.0 %collective-permute-start.7 = (f32[3,480,256]{2,1,0:T(8,128)}, f32[3,480,256]{2,1,0:T(8,128)}, u32[]{:S(2)}, u32[]{:S(2)}) collective-permute-start(f32[3,480,256]{2,1,0:T(8,128)} %get-tuple-element.38), channel_id=1, source_target_pairs={{0,8},{8,16},{16,24},{1,9},{9,17},{17,25},{2,10},{10,18},{18,26},{... | collective-permute-start | bytes 4423688 | tf_op jit(solution)/shard_map/ppermute | solution.py:924
  126.7 14.8 %copy-start.2 = (f32[3,584,256]{2,1,0:T(8,128)S(1)}, f32[3,584,256]{2,1,0:T(8,128)}, u32[]{:S(2)}) copy-start(f32[3,584,256]{2,1,0:T(8,128)} %adjoint_first.2.refs_1_.refs_4_.refs_2_.refs_0_) | copy-start | bytes 5382148
  155.7 13.7 %copy-start.14 = (f32[3,16,128]{2,1,0:T(8,128)S(1)}, f32[3,16,128]{2,1,0:T(8,128)}, u32[]{:S(2)}) copy-start(f32[3,16,128]{2,1,0:T(8,128)} %adjoint_second.2.refs_6_) | copy-start | bytes 73732
  159.9 29.7 %copy-start.10 = (f32[3,560,256]{2,1,0:T(8,128)S(1)}, f32[3,560,256]{2,1,0:T(8,128)}, u32[]{:S(2)}) copy-start(f32[3,560,256]{2,1,0:T(8,128)} %get-tuple-element.33.refs_0_.refs_2_) | copy-start | bytes 5160964
  159.9 29.7 %copy-start.11 = (f32[3,464,256]{2,1,0:T(8,128)S(1)}, f32[3,464,256]{2,1,0:T(8,128)}, u32[]{:S(2)}) copy-start(f32[3,464,256]{2,1,0:T(8,128)} %get-tuple-element.34.refs_1_.refs_3_) | copy-start | bytes 4276228
  171.5 18.2 %copy-start.1 = (f32[1,3,1024,256]{3,2,1,0:T(8,128)S(1)}, f32[1,3,1024,256]{3,2,1,0:T(8,128)}, u32[]{:S(2)}) copy-start(f32[1,3,1024,256]{3,2,1,0:T(8,128)} %param.13) | copy-start | bytes 9437188
  171.5 18.2 %copy-start.3 = (f32[3,584,256]{2,1,0:T(8,128)S(1)}, f32[3,584,256]{2,1,0:T(8,128)}, u32[]{:S(2)}) copy-start(f32[3,584,256]{2,1,0:T(8,128)} %adjoint_first.2.refs_1_.refs_4_.refs_2_.refs_0_) | copy-start | bytes 5382148
  171.5 18.2 %copy-start.5 = (f32[3,480,256]{2,1,0:T(8,128)S(1)}, f32[3,480,256]{2,1,0:T(8,128)}, u32[]{:S(2)}) copy-start(f32[3,480,256]{2,1,0:T(8,128)} %adjoint_first.3.refs_2_.refs_5_.refs_3_.refs_1_) | copy-start | bytes 4423684
  171.5 18.2 %copy-start.6 = (f32[3,1024,256]{2,1,0:T(8,128)S(1)}, f32[3,1024,256]{2,1,0:T(8,128)}, u32[]{:S(2)}) copy-start(f32[3,1024,256]{2,1,0:T(8,128)} %get-tuple-element.23.increment.inc_in.refs_0_.inc0) | copy-start | bytes 9437188
  (13 other events, 42.7 us)
